TPU v7x, 128 devices: a whole 4x4x4 slice. The times are simulated.
128 devices in a mesh: wide: 16 (over y, z), narrow: 8 (over x, core).
Axes of the slice: x: 4, y: 4, z: 4, core: 2. Of those that a mesh axis runs over, the one named last changes fastest.
Arguments:
- hidden: bfloat16 [128, 16384], P('narrow', 'wide'), may hold values from -6 to 6
- gain: bfloat16 [16384], P('wide'), may hold values from 0.5 to 1.5
- sign_in: int32 [16384], P('wide'), may hold values from 0 to 1
- qkv_weight: bfloat16 [16384, 18432], P('wide', 'narrow'), may hold values from -0.046875 to 0.046875
- out_weight: bfloat16 [16384, 16384], P('narrow', 'wide'), may hold values from -0.046875 to 0.046875
- sign_attn: int32 [16384], P('narrow'), may hold values from 0 to 1
- key_cache: bfloat16 [128, 8, 4096, 128], P('wide', 'narrow'), may hold values from -512 to 512, as said below
- value_cache: bfloat16 [128, 8, 4096, 128], P('wide', 'narrow'), may hold values from -6 to 6
- lengths: int32 [128], P('wide'), may hold values from 1024 to 4096
Outputs:
- layer_out: bfloat16 [128, 16384], P('narrow', 'wide')
Inputs may be any that keep to these rules, and one draw needn't show every extreme that they name: `key_cache`: cached keys mostly of magnitude about 2, with some slots far larger in the hidden draw.
All inputs are finite; a program needn't handle non-finite values. Where the computation divides by a largest or mean magnitude, that divisor is 1e-20 or more.
Results may differ from a plain program's by a relative error of at most 0.018.
Values may be sent and summed in bfloat16 or wider, within the bound.
No kernel may reach another device: no remote copies, remote signals or barrier semaphores. Data moves between devices by JAX's collectives and lax.ppermute only.
A program may use at most 128 MiB of HBM per device.

v0:
```python
import math

import jax
import jax.numpy as jnp
from jax import lax
from jax.sharding import Mesh
from jax.sharding import PartitionSpec as P

D = 16384
HD = 128
QG = 16
WIDE = ("wide_0", "wide_1")


ROPE_BASE = 500000.0


def one_axis_at_a_time(value, axes):
    for axis in axes:
        value = lax.psum(value, axis)
    return value


def side_by_side(arrays, axis, dim, along):
    columns = [a.reshape(*a.shape[:along], -1) for a in arrays]
    both = jnp.concatenate(columns, axis=along)
    filled, at, gathered = (lax.all_gather(both, axis, axis=dim, tiled=True), 0, [])
    for a, column in zip(arrays, columns):
        piece = filled[..., at : at + column.shape[along]]
        gathered.append(piece.reshape(*piece.shape[:along], *a.shape[along:]))
        at += column.shape[along]
    return tuple(gathered)


def split_up(value, dim, peers):
    before, after = (value.shape[:dim], value.shape[dim + 1 :])
    return jnp.moveaxis(value.reshape(*before, peers, -1, *after), dim, 0)


def summed_on_arrival(value, axis, dim):
    tiles = split_up(value, dim, lax.axis_size(axis))
    arrived = lax.all_to_all(tiles, axis, split_axis=0, concat_axis=0, tiled=True)
    return arrived.astype(jnp.float32).sum(axis=0)


def hadamard(order):
    places = jnp.arange(order, dtype=jnp.int32)
    common = places[:, None] & places[None, :]
    parity = jnp.zeros((order, order), jnp.int32)
    for bit_pos in range(order.bit_length() - 1):
        parity = parity ^ common >> bit_pos & 1
    return (1 - 2 * parity).astype(jnp.float32) / math.sqrt(order)


def rotate_blocks(values, sign_bits, width):
    signs = (2 * sign_bits - 1).astype(jnp.float32)
    blocks = (values * signs).reshape(values.shape[:-1] + (values.shape[-1] // width, width))
    turned = jnp.einsum("...bk,kj->...bj", blocks, hadamard(width))
    scales = (jnp.max(jnp.abs(turned), axis=-1) + 1e-06).astype(jnp.bfloat16)
    payload = (turned / scales.astype(jnp.float32)[..., None]).astype(jnp.bfloat16)
    return (payload, scales)


def rotary(vectors, positions):
    half_width = vectors.shape[-1] // 2
    frequency = jnp.exp(
        jnp.arange(half_width, dtype=jnp.float32) * (-2.0 * math.log(ROPE_BASE) / vectors.shape[-1])
    )
    angles = positions.astype(jnp.float32)[:, None] * frequency[None, :]
    cosine = jnp.cos(angles)[:, None, :]
    sines = jnp.sin(angles)[:, None, :]
    lower_half = vectors[..., :half_width]
    upper_half = vectors[..., half_width:]
    return jnp.concatenate(
        [lower_half * cosine - upper_half * sines, upper_half * cosine + lower_half * sines],
        axis=-1,
    )


def body(hidden, gain, sign_in, qkv_weight, out_weight, sign_attn, key_cache, value_cache, lengths):
    rows = hidden.astype(jnp.float32)
    squares = one_axis_at_a_time(jnp.sum(rows * rows, axis=1), WIDE)
    factor = lax.rsqrt(squares / D + 1e-05)
    normed = rows * factor[:, None] * gain.astype(jnp.float32)[None, :]
    payload, scales = rotate_blocks(normed, sign_in, HD)
    payload_all, scales_all = side_by_side((payload, scales), "narrow", 0, 2)
    weight_blocks = qkv_weight.reshape(payload.shape[1], HD, qkv_weight.shape[1])
    own_lists = key_cache.shape[0]
    products = jnp.einsum(
        "rbk,bkc->rbc", payload_all, weight_blocks, preferred_element_type=jnp.float32
    )
    projected = summed_on_arrival(
        jnp.einsum("rbc,rb->rc", products, scales_all.astype(jnp.float32)).astype(jnp.bfloat16),
        WIDE,
        0,
    )
    groups = key_cache.shape[1]
    grouped = projected.reshape(own_lists, groups, QG + 2, HD)
    queries = rotary(grouped[:, :, :QG, :].reshape(own_lists, groups * QG, HD), lengths)
    queries = queries.astype(jnp.bfloat16).reshape(own_lists, groups, QG, HD)
    keys_new = rotary(grouped[:, :, QG, :], lengths).astype(jnp.bfloat16)
    values_new = grouped[:, :, QG + 1, :].astype(jnp.bfloat16)
    inverse_root = 1.0 / math.sqrt(HD)
    live = jnp.arange(key_cache.shape[2], dtype=jnp.int32)[None, :] < lengths[:, None]
    live_mask = live[:, None, None, :]
    scores = (
        jnp.einsum("lgqk,lgsk->lgqs", queries, key_cache, preferred_element_type=jnp.float32)
        * inverse_root
    )
    fresh = (
        jnp.einsum("lgqk,lgk->lgq", queries, keys_new, preferred_element_type=jnp.float32)
        * inverse_root
    )
    scores = jnp.where(live_mask, scores, -1e30)
    peak = jnp.maximum(jnp.max(scores, axis=-1), fresh)
    weights = jnp.where(live_mask, jnp.exp(scores - peak[..., None]), 0.0)
    weight_new = jnp.exp(fresh - peak)
    denom_sum = jnp.sum(weights, axis=-1) + weight_new
    probs = (weights / denom_sum[..., None]).astype(jnp.bfloat16)
    prob_new = (weight_new / denom_sum).astype(jnp.bfloat16)
    attended = jnp.einsum("lgqs,lgsk->lgqk", probs, value_cache, preferred_element_type=jnp.float32)
    attended = (
        attended
        + prob_new.astype(jnp.float32)[..., None] * values_new.astype(jnp.float32)[:, :, None, :]
    )
    local_heads = groups * QG
    out_blocks, out_scale = rotate_blocks(
        attended.reshape(own_lists, local_heads * HD), sign_attn, HD
    )
    blocks_all, scale_all = side_by_side((out_blocks, out_scale), WIDE, 0, 2)
    head_weights = out_weight.reshape(local_heads, HD, out_weight.shape[1])
    products = jnp.einsum(
        "rhk,hkd->rhd", blocks_all, head_weights, preferred_element_type=jnp.float32
    )
    mixed = summed_on_arrival(
        jnp.einsum("rhd,rh->rd", products, scale_all.astype(jnp.float32)).astype(jnp.bfloat16),
        "narrow",
        0,
    )
    return (rows + mixed).astype(jnp.bfloat16)


def solution(mesh):
    split = Mesh(mesh.devices.reshape(4, 4, mesh.shape["narrow"]), ("wide_0", "wide_1", "narrow"))
    placed = (
        P("narrow", WIDE),
        P(WIDE),
        P(WIDE),
        P(WIDE, "narrow"),
        P("narrow", WIDE),
        P("narrow"),
        P(WIDE, "narrow", None, None),
        P(WIDE, "narrow", None, None),
        P(WIDE),
    )
    return jax.shard_map(
        body, mesh=split, in_specs=placed, out_specs=P("narrow", WIDE), check_vma=False
    )
```

profile of v0, /device:TPU:0, one launch (start us, length us, event | category | flops | bytes accessed | tf_op | source)
XLA Modules:
  0.0 117.6 jit_solution(16247789897836685528)
XLA Ops:
  0.0 0.7 add_convert_fusion.3
  0.7 0.7 convert_element_type.120
  1.4 0.9 fusion.37
  2.3 10.8 %psum.14 = f32[16]{0:T(128)S(1)} all-reduce(f32[16]{0:T(128)S(1)} %fusion.37), channel_id=1, replica_groups=mesh['wide_0'=4,'wide_1'=4,'narrow'=8] {'wide_0'}, use_global_device_ids=true, to_apply=%region_1.0 | all-reduce | flops 16 | bytes 128 | tf_op jit(solution)/shard_map/psum | solution.py:20
  13.1 11.8 %psum.15 = f32[16]{0:T(128)S(1)} all-reduce(f32[16]{0:T(128)S(1)} %psum.14), channel_id=1, replica_groups=mesh['wide_0'=4,'wide_1'=4,'narrow'=8] {'wide_1'}, use_global_device_ids=true, to_apply=%region_2.0 | all-reduce | flops 16 | bytes 128 | tf_op jit(solution)/shard_map/psum | solution.py:20
  24.8 0.8 fusion.40
  25.7 0.3 abs_reduce_fusion.1
  26.0 0.2 copy.28
  26.2 0.1 divide_convert_fusion.4
  26.3 13.5 %all_gather.6 = bf16[128,8,129]{2,1,0:T(8,128)(2,1)S(1)} all-gather(bf16[16,8,129]{2,1,0:T(8,128)(2,1)S(1)} %pad_maximum_fusion), channel_id=1, replica_groups=mesh['wide_0'=4,'wide_1'=4,'narrow'=8] {'narrow'}, dimensions={0}, use_global_device_ids=true | all-gather | bytes 297216 | tf_op jit(solution)/shard_map/all_gather | solution.py:27
  39.8 3.7 %convolution_bitcast_fusion = bf16[128,8,2304]{2,0,1:T(8,128)(2,1)S(1)} fusion(bf16[8,128,2304]{2,1,0:T(8,128)(2,1)} %bitcast.80, bf16[128,8,128]{2,1,0:T(8,128)(2,1)S(1)} %slice.45), kind=kOutput, calls=%fused_computation.8 | convolution fusion | flops 603979776 | bytes 9699328 | tf_op jit(solution)/shard_map/rbk,bkc->rbc/dot_general | solution.py:89
  43.5 0.0 copy-start.2
  43.5 0.0 copy-start.1
  43.5 3.4 %fusion = bf16[128,1,2304]{2,1,0:T(2,128)(2,1)S(1)} fusion(bf16[128,8,2304]{2,0,1:T(8,128)(2,1)S(1)} %convolution_bitcast_fusion, bf16[128,8,129]{2,1,0:T(8,128)(2,1)S(1)} %all_gather.6), kind=kOutput, calls=%fused_computation | convolution fusion | flops 4718592 | bytes 5570560 | tf_op jit(solution)/shard_map/rbc,rb->rc/dot_general | solution.py:93
  47.0 0.9 copy.68
  47.8 3.6 %all-to-all-start = ((bf16[16,8,2304]{2,1,0:T(8,128)(2,1)}), bf16[16,8,2304]{2,1,0:T(8,128)(2,1)S(1)}, u32[]{:S(2)}, u32[]{:S(2)}) async-start(bf16[16,8,2304]{2,1,0:T(8,128)(2,1)} %bitcast.77), calls=%async_computation | async-start | bytes 1179648 | tf_op jit(solution)/shard_map/all_to_all | solution.py:42
  51.4 0.0 copy-done.2
  51.4 0.1 iota_compare_fusion
  51.6 0.1 multiply_cosine_fusion.1
  51.7 0.0 copy-done.1
  51.7 12.7 %all-to-all-done = bf16[16,8,2304]{2,1,0:T(8,128)(2,1)S(1)} async-done(((bf16[16,8,2304]{2,1,0:T(8,128)(2,1)}), bf16[16,8,2304]{2,1,0:T(8,128)(2,1)S(1)}, u32[]{:S(2)}, u32[]{:S(2)}) %all-to-all-start) | async-done | bytes 589856 | tf_op jit(solution)/shard_map/all_to_all | solution.py:42
  64.4 0.1 convert_reduce_fusion
  64.5 0.1 fusion.63
  64.7 0.1 maximum_bitcast_fusion
  64.8 0.1 subtract_convert_fusion
  64.8 0.2 fusion.53
  65.0 5.8 %fusion.89 = (f32[8,16]{1,0:T(8,128)S(1)}, f32[8,16,4096]{2,1,0:T(8,128)S(1)}) fusion(bf16[8,1,4096,128]{3,2,1,0:T(8,128)(2,1)} %param.15, bf16[8,16,64]{2,1,0:T(8,128)(2,1)S(1)} %get-tuple-element.6, bf16[8,16,64]{2,1,0:T(8,128)(2,1)S(1)} %get-tuple-element.5, pred[8,4096]{1,0:T(8,128)(4,1)S(1)} %iota_compare_fusion), kind=kOutput, calls=%fused_computation.113 | convolution fusion | flops 135856000 | bytes 10551808 | tf_op jit(solution)/shard_map/lgqk,lgsk->lgqs/dot_general | solution.py:107
  70.8 0.6 fusion.14
  71.5 5.1 %abs_reduce_fusion = (f32[8,16]{1,0:T(8,128)S(1)}, f32[8,16,128]{2,1,0:T(8,128)S(1)}) fusion(bf16[8,1,4096,128]{3,2,1,0:T(8,128)(2,1)} %param.16, f32[8,16,4096]{2,1,0:T(8,128)S(1)} %get-tuple-element.20, f32[8,16]{1,0:T(8,128)S(1)} %get-tuple-element.8, f32[8,16]{1,0:T(8,128)S(1)} %multiply_maximum_fusion, pred[8,4096]{1,0:T(8,128)(4,1)S(1)} %iota_compare_fusion, ...), kind=kOutput, calls=%fused_computation.47 | convolution fusion | flops 141000576 | bytes 10598400 | tf_op jit(solution)/shard_map/...bk,kj->...bj/dot_general | solution.py:58
  76.6 0.1 copy.32
  76.7 0.1 divide_convert_fusion.3
  76.9 22.8 %all_gather.7 = bf16[128,16,129]{2,1,0:T(8,128)(2,1)S(1)} all-gather(bf16[8,16,129]{2,1,0:T(8,128)(2,1)S(1)} %pad_maximum_fusion.1), channel_id=1, replica_groups=mesh['wide_0'=4,'wide_1'=4,'narrow'=8] {'wide_0','wide_1'}, dimensions={0}, use_global_device_ids=true | all-gather | bytes 561408 | tf_op jit(solution)/shard_map/all_gather | solution.py:27
  99.7 0.1 slice.52
  99.8 3.4 %convolution_bitcast_fusion.1 = bf16[128,16,1024]{2,0,1:T(8,128)(2,1)S(1)} fusion(bf16[16,128,1024]{2,1,0:T(8,128)(2,1)} %bitcast.81, bf16[128,16,128]{2,1,0:T(8,128)(2,1)S(1)} %slice.52), kind=kOutput, calls=%fused_computation.11 | convolution fusion | flops 536870912 | bytes 8912896 | tf_op jit(solution)/shard_map/rhk,hkd->rhd/dot_general | solution.py:132
  103.2 0.0 copy-start
  103.2 2.6 %fusion.6 = bf16[128,1,1024]{2,1,0:T(2,128)(2,1)S(1)} fusion(bf16[128,16,1024]{2,0,1:T(8,128)(2,1)S(1)} %convolution_bitcast_fusion.1, bf16[128,16,129]{2,1,0:T(8,128)(2,1)S(1)} %all_gather.7), kind=kOutput, calls=%fused_computation.6 | convolution fusion | flops 4194304 | bytes 4980736 | tf_op jit(solution)/shard_map/rhd,rh->rd/dot_general | solution.py:136
  105.8 0.1 copy.69
  105.9 11.0 %all_to_all.10 = bf16[8,16,1024]{2,1,0:T(8,128)(2,1)S(1)} all-to-all(bf16[8,16,1024]{2,1,0:T(8,128)(2,1)S(1)} %bitcast.82), channel_id=1, replica_groups=mesh['wide_0'=4,'wide_1'=4,'narrow'=8] {'narrow'}, dimensions={0} | all-to-all | bytes 524288 | tf_op jit(solution)/shard_map/all_to_all | solution.py:42
  117.0 0.0 copy-done
  117.0 0.6 fusion.41
  (17 shorter events, 0.2 us)
Async XLA Ops:
  43.5 7.9 %copy-start.2 = (s32[8]{0:T(128)S(1)}, s32[8]{0:T(128)}, u32[]{:S(2)}) copy-start(s32[8]{0:T(128)} %param.17) | copy-start | bytes 100
  43.5 8.2 %copy-start.1 = (s32[2048]{0:T(1024)S(1)}, s32[2048]{0:T(1024)}, u32[]{:S(2)}) copy-start(s32[2048]{0:T(1024)} %param.14) | copy-start | bytes 24580
  47.8 16.6 %all-to-all-start = ((bf16[16,8,2304]{2,1,0:T(8,128)(2,1)}), bf16[16,8,2304]{2,1,0:T(8,128)(2,1)S(1)}, u32[]{:S(2)}, u32[]{:S(2)}) async-start(bf16[16,8,2304]{2,1,0:T(8,128)(2,1)} %bitcast.77), calls=%async_computation | async-start | bytes 1179648 | tf_op jit(solution)/shard_map/all_to_all | solution.py:42
  103.2 13.8 %copy-start = (bf16[16,1024]{1,0:T(8,128)(2,1)S(1)}, bf16[16,1024]{1,0:T(8,128)(2,1)}, u32[]{:S(2)}) copy-start(bf16[16,1024]{1,0:T(8,128)(2,1)} %param.9) | copy-start | bytes 98308
where the time goes:
time: 119 us; the launch traced here: 118 us
  blocking collectives  69.9 us (59%)
  matrix products  24.5 us (21%)
  waiting for transfers between devices  12.7 us (11%)
  other arithmetic  5.21 us (4%)
  starting transfers between devices  3.58 us (3%)
  local copies, waits for them, and re-layouts  1.44 us (1%)
    all_gather x2, blocking collectives, side_by_side(): lax.all_gather(both, axis, axis=dim, tiled=True)  36.3 us
    psum x2, blocking collectives, one_axis_at_a_time(): value = lax.psum(value, axis)  22.6 us
    all_to_all x1, waiting for transfers between devices, summed_on_arrival(): lax.all_to_all(tiles, axis, split_axis=0, concat_axis=0, tiled=True)  12.7 us
    all_to_all x1, blocking collectives, summed_on_arrival(): lax.all_to_all(tiles, axis, split_axis=0, concat_axis=0, tiled=True)  11 us
    dot_general x1, matrix products, body(): jnp.einsum('lgqk,lgsk->lgqs', queries, key_cache, preferred_element_type=...  5.79 us
    dot_general x2, matrix products, rotate_blocks(): turned = jnp.einsum('...bk,kj->...bj', blocks, hadamard(width))  5.36 us
    dot_general x1, matrix products, body(): jnp.einsum('rbk,bkc->rbc', payload_all, weight_blocks, preferred_element_...  3.71 us
    all_to_all x1, starting transfers between devices, summed_on_arrival(): lax.all_to_all(tiles, axis, split_axis=0, concat_axis=0, tiled=True)  3.58 us
  transfers between devices with their start and end apart: 1, of which 1 were waited for; matrix products, arithmetic and copies ran while one was open for 0% of the time, Pallas kernels for 0%

commit v1 on v0

v1 whole, which is shorter than its diff:
```python
import math

import jax
import jax.numpy as jnp
from jax import lax
from jax.experimental import pallas as pl
from jax.experimental.pallas import tpu as pltpu
from jax.sharding import Mesh
from jax.sharding import PartitionSpec as P

D = 16384
HD = 128
QG = 16
WIDE = ("y", "z")
ROPE_BASE = 500000.0
EXTRA = 128
MIB = 1 << 20
VMEM = pl.BlockSpec(memory_space=pltpu.VMEM)
SMEM = pl.BlockSpec(memory_space=pltpu.SMEM)
HBM = pl.BlockSpec(memory_space=pl.ANY)
F32 = jnp.float32
BF16 = jnp.bfloat16


def hadamard_signs():
    common = lax.broadcasted_iota(jnp.int32, (HD, HD), 0) & lax.broadcasted_iota(jnp.int32, (HD, HD), 1)
    common = common ^ (common >> 4)
    common = common ^ (common >> 2)
    common = common ^ (common >> 1)
    return (1 - 2 * (common & 1)).astype(F32).astype(BF16)


def two_piece_dot(values, matrix):
    high = values.astype(BF16)
    low = (values - high.astype(F32)).astype(BF16)
    return jnp.dot(high, matrix, preferred_element_type=F32) + jnp.dot(low, matrix, preferred_element_type=F32)


def rotate_in_kernel(own_ref, other_ref, gain_ref, sign_ref, out_ref):
    features = own_ref.shape[1]
    matrix = hadamard_signs()
    steer = gain_ref[...].astype(F32) * (2 * sign_ref[...] - 1).astype(F32)
    lane = lax.broadcasted_iota(jnp.int32, (16, EXTRA), 1)
    for at, ref in enumerate((own_ref, other_ref)):
        rows = ref[...].astype(F32)
        squares = jnp.sum(rows * rows, axis=1, keepdims=True)
        first = squares.astype(BF16).astype(F32)
        second = (squares - first).astype(BF16).astype(F32)
        third = squares - first - second
        pieces = jnp.where(lane == 0, first, jnp.where(lane == 1, second, jnp.where(lane == 2, third, 0.0)))
        out_ref[16 * at : 16 * at + 16, features:] = pieces.astype(BF16)
        steered = rows * steer
        for b in range(features // HD):
            turned = two_piece_dot(steered[:, b * HD : (b + 1) * HD], matrix) * (1.0 / math.sqrt(HD))
            out_ref[16 * at : 16 * at + 16, b * HD : (b + 1) * HD] = turned.astype(BF16)


def project_kernel(place_ref, x0, x1, x2, x3, weight_hbm, out_ref, weight, sems):
    parts, width = 3, weight.shape[1] // 3
    features = weight.shape[0]

    def fetch(i):
        cols = pl.ds(i * width, width)
        return pltpu.make_async_copy(weight_hbm.at[:, cols], weight.at[:, cols], sems.at[i])

    for i in range(parts):
        fetch(i).start()
    x, c = place_ref[0], place_ref[1]
    received = (x0, x1, x2, x3)
    targets = []
    for s in range(4):
        for other in range(2):
            core = c if other == 0 else 1 - c
            source = 2 * ((x - s) & 3) + core
            targets += [2 * source, 2 * source + 1]
    for s in range(4):
        extra = received[s][:, features:].astype(F32)
        for j in range(4):
            out_ref[targets[4 * s + j], :, weight.shape[1] :] = extra[8 * j : 8 * j + 8].astype(BF16)
    rows = jnp.concatenate([r[:, :features] for r in received], axis=0)
    for i in range(parts):
        fetch(i).wait()
        product = jnp.dot(rows, weight[:, i * width : (i + 1) * width], preferred_element_type=F32)
        for j in range(16):
            out_ref[targets[j], :, i * width : (i + 1) * width] = product[8 * j : 8 * j + 8].astype(BF16)


CHUNK = 1024


def attend_kernel(
    lengths_ref, arrived_ref, cos_ref, sin_ref, sign_ref, key_hbm, value_hbm, out_ref,
    keys, values, queries, scores, attended, sems,
):
    lists = lengths_ref.shape[0]
    slots = keys.shape[1]
    chunks = slots // CHUNK

    def fetch(which, pair, half, chunk):
        source, target = ((key_hbm, keys), (value_hbm, values))[which]
        span = pl.ds(chunk * CHUNK, CHUNK)
        return pltpu.make_async_copy(
            source.at[2 * pair + half, 0, span, :],
            target.at[pair, span, pl.ds(half * HD, HD)],
            sems.at[which, pair, half, chunk],
        )

    longest = [jnp.maximum(lengths_ref[2 * p], lengths_ref[2 * p + 1]) for p in range(lists // 2)]
    for pair in range(lists // 2):
        for chunk in range(chunks):

            @pl.when(chunk * CHUNK < longest[pair])
            def _():
                for which in range(2):
                    for half in range(2):
                        fetch(which, pair, half, chunk).start()

    total = arrived_ref[0].astype(F32)
    for w in range(1, arrived_ref.shape[0]):
        total = total + arrived_ref[w].astype(F32)
    columns = (QG + 2) * HD
    squares = jnp.sum(total[:, columns:], axis=1, keepdims=True)
    factor = lax.rsqrt(squares * (1.0 / D) + 1e-05)
    cosine, sine = cos_ref[...], sin_ref[...]
    for h in range(QG + 2):
        vector = total[:, h * HD : (h + 1) * HD] * factor
        if h <= QG:
            vector = vector * cosine + pltpu.roll(vector, HD // 2, 1) * sine
        queries[:, h, :] = vector.astype(BF16).astype(F32)

    scale = 1.0 / math.sqrt(HD)
    row = lax.broadcasted_iota(jnp.int32, (2 * QG, 1), 0)
    for pair in range(lists // 2):
        first, second = queries[2 * pair], queries[2 * pair + 1]
        q_both = jnp.concatenate([first[:QG], second[:QG]], axis=0)
        blank = jnp.zeros((QG, HD), F32)
        q_wide = jnp.concatenate(
            [jnp.concatenate([first[:QG], blank], axis=1), jnp.concatenate([blank, second[:QG]], axis=1)], axis=0
        ).astype(BF16)
        k_new = jnp.concatenate(
            [jnp.broadcast_to(v[QG : QG + 1], (QG, HD)) for v in (first, second)], axis=0
        )
        v_new = jnp.concatenate(
            [jnp.broadcast_to(v[QG + 1 : QG + 2], (QG, HD)) for v in (first, second)], axis=0
        )
        fresh = jnp.sum(q_both * k_new, axis=1, keepdims=True) * scale
        length = jnp.where(row < QG, lengths_ref[2 * pair], lengths_ref[2 * pair + 1])
        live_chunks = (longest[pair] + CHUNK - 1) // CHUNK

        def score(chunk, peak):
            for half in range(2):
                fetch(0, pair, half, chunk).wait()
            start = pl.multiple_of(chunk * CHUNK, CHUNK)
            block = lax.dot_general(
                q_wide, keys[pair, pl.ds(start, CHUNK), :], (((1,), (1,)), ((), ())), preferred_element_type=F32
            )
            slot = lax.broadcasted_iota(jnp.int32, (2 * QG, CHUNK), 1) + start
            block = jnp.where(slot < length, block * scale, -1e30)
            scores[:, pl.ds(start, CHUNK)] = block
            for t in range(CHUNK // HD):
                peak = jnp.maximum(peak, block[:, t * HD : (t + 1) * HD])
            return peak

        peak = lax.fori_loop(0, live_chunks, score, jnp.full((2 * QG, HD), -1e30, F32))
        peak = jnp.maximum(jnp.max(peak, axis=1, keepdims=True), fresh)

        def mix(chunk, carry):
            mass, mixed = carry
            for half in range(2):
                fetch(1, pair, half, chunk).wait()
            start = pl.multiple_of(chunk * CHUNK, CHUNK)
            weight = jnp.exp(scores[:, pl.ds(start, CHUNK)] - peak)
            for t in range(CHUNK // HD):
                mass = mass + weight[:, t * HD : (t + 1) * HD]
            mixed = mixed + jnp.dot(
                weight.astype(BF16), values[pair, pl.ds(start, CHUNK), :], preferred_element_type=F32
            )
            return mass, mixed

        mass, mixed = lax.fori_loop(
            0, live_chunks, mix, (jnp.zeros((2 * QG, HD), F32), jnp.zeros((2 * QG, 2 * HD), F32))
        )
        weight_new = jnp.exp(fresh - peak)
        denominator = jnp.sum(mass, axis=1, keepdims=True) + weight_new
        own = jnp.concatenate([mixed[:QG, :HD], mixed[QG:, HD:]], axis=0)
        own = (own + weight_new.astype(BF16).astype(F32) * v_new) / denominator
        attended[2 * QG * pair : 2 * QG * (pair + 1), :] = own

    matrix = hadamard_signs()
    steered = []
    for h in range(QG):
        sign = (2 * sign_ref[:, h * HD : (h + 1) * HD] - 1).astype(F32)
        steered.append(attended[pl.ds(h, lists, stride=QG), :] * sign)
    turned = two_piece_dot(jnp.concatenate(steered, axis=0), matrix) * (1.0 / math.sqrt(HD))
    for h in range(QG):
        piece = turned[lists * h : lists * (h + 1)].astype(BF16)
        for w in range(out_ref.shape[0]):
            out_ref[w, :, h * HD : (h + 1) * HD] = piece


def mix_kernel(place_ref, rows_ref, weight_hbm, keep_ref, send_ref, weight, sems):
    parts, width = 4, weight.shape[1] // 4

    def fetch(i):
        cols = pl.ds(i * width, width)
        return pltpu.make_async_copy(weight_hbm.at[:, cols], weight.at[:, cols], sems.at[i])

    for i in range(parts):
        fetch(i).start()
    c = place_ref[1]
    rows = jnp.concatenate([rows_ref[x, c] for x in range(4)] + [rows_ref[x, 1 - c] for x in range(4)], axis=0)
    for i in range(parts):
        fetch(i).wait()
        product = jnp.dot(rows, weight[:, i * width : (i + 1) * width], preferred_element_type=F32)
        for x in range(4):
            keep_ref[x, :, i * width : (i + 1) * width] = product[16 * x : 16 * x + 16]
            send_ref[x, :, i * width : (i + 1) * width] = product[64 + 16 * x : 80 + 16 * x].astype(BF16)


def pair_sum_kernel(place_ref, keep_ref, got_ref, own_ref, s1, s2, s3):
    x = place_ref[0]
    own_ref[...] = keep_ref[x] + got_ref[x].astype(F32)
    for s, ref in ((1, s1), (2, s2), (3, s3)):
        to = (x + s) & 3
        ref[...] = (keep_ref[to] + got_ref[to].astype(F32)).astype(BF16)


def last_kernel(hidden_ref, own_ref, r1, r2, r3, out_ref):
    mixed = own_ref[...] + r1[...].astype(F32) + r2[...].astype(F32) + r3[...].astype(F32)
    out_ref[...] = (hidden_ref[...].astype(F32) + mixed).astype(BF16)


def params(limit):
    return pltpu.CompilerParams(vmem_limit_bytes=limit * MIB)


def along_x(value):
    return [lax.ppermute(value, "x", [(i, (i + s) % 4) for i in range(4)]) for s in (1, 2, 3)]


def across_cores(value):
    return lax.ppermute(value, "core", [(0, 1), (1, 0)])


def body(hidden, gain, sign_in, qkv_weight, out_weight, sign_attn, key_cache, value_cache, lengths):
    rows, features = hidden.shape
    columns = qkv_weight.shape[1]
    own_lists, _, slots, _ = key_cache.shape
    peers = lax.axis_size(WIDE)
    place = jnp.stack([lax.axis_index("x"), lax.axis_index("core")]).astype(jnp.int32)

    rotated = pl.pallas_call(
        rotate_in_kernel,
        out_shape=jax.ShapeDtypeStruct((2 * rows, features + EXTRA), BF16),
        in_specs=[VMEM] * 4,
        out_specs=VMEM,
        name="rotate_in",
    )(hidden, across_cores(hidden), gain.reshape(1, -1), sign_in.reshape(1, -1))
    partial = pl.pallas_call(
        project_kernel,
        out_shape=jax.ShapeDtypeStruct((peers, own_lists, columns + EXTRA), BF16),
        in_specs=[SMEM] + [VMEM] * 4 + [HBM],
        out_specs=VMEM,
        scratch_shapes=[pltpu.VMEM((features, columns), BF16), pltpu.SemaphoreType.DMA((3,))],
        compiler_params=params(16),
        name="project",
    )(place, rotated, *along_x(rotated), qkv_weight)
    arrived = lax.all_to_all(partial, WIDE, split_axis=0, concat_axis=0, tiled=True)

    frequency = jnp.exp(jnp.arange(HD // 2, dtype=F32) * (-2.0 * math.log(ROPE_BASE) / HD))
    angles = lengths.astype(F32)[:, None] * frequency[None, :]
    cosine, sine = jnp.cos(angles), jnp.sin(angles)
    sent = pl.pallas_call(
        attend_kernel,
        out_shape=jax.ShapeDtypeStruct((peers, own_lists, QG * HD), BF16),
        in_specs=[SMEM] + [VMEM] * 4 + [HBM] * 2,
        out_specs=VMEM,
        scratch_shapes=[
            pltpu.VMEM((own_lists // 2, slots, 2 * HD), BF16),
            pltpu.VMEM((own_lists // 2, slots, 2 * HD), BF16),
            pltpu.VMEM((own_lists, 24, HD), F32),
            pltpu.VMEM((2 * QG, slots), F32),
            pltpu.VMEM((own_lists * QG, HD), F32),
            pltpu.SemaphoreType.DMA((2, own_lists // 2, 2, slots // CHUNK)),
        ],
        compiler_params=params(32),
        name="attend",
    )(
        lengths,
        arrived,
        jnp.concatenate([cosine, cosine], axis=1),
        jnp.concatenate([-sine, sine], axis=1),
        sign_attn.reshape(1, -1),
        key_cache,
        value_cache,
    )
    gathered = lax.all_to_all(sent, WIDE, split_axis=0, concat_axis=0, tiled=True)
    keep, send = pl.pallas_call(
        mix_kernel,
        out_shape=(
            jax.ShapeDtypeStruct((4, rows, features), F32),
            jax.ShapeDtypeStruct((4, rows, features), BF16),
        ),
        in_specs=[SMEM, VMEM, HBM],
        out_specs=(VMEM, VMEM),
        scratch_shapes=[pltpu.VMEM(out_weight.shape, BF16), pltpu.SemaphoreType.DMA((4,))],
        compiler_params=params(16),
        name="mix",
    )(place, gathered.reshape(4, 2, rows, QG * HD), out_weight)
    own, *sends = pl.pallas_call(
        pair_sum_kernel,
        out_shape=(jax.ShapeDtypeStruct((rows, features), F32),)
        + (jax.ShapeDtypeStruct((rows, features), BF16),) * 3,
        in_specs=[SMEM, VMEM, VMEM],
        out_specs=(VMEM,) * 4,
        name="pair_sum",
    )(place, keep, across_cores(send))
    got = [
        lax.ppermute(v, "x", [(i, (i + s) % 4) for i in range(4)]) for s, v in zip((1, 2, 3), sends)
    ]
    return pl.pallas_call(
        last_kernel,
        out_shape=jax.ShapeDtypeStruct((rows, features), BF16),
        in_specs=[VMEM] * 5,
        out_specs=VMEM,
        name="last",
    )(hidden, own, *got)


def solution(mesh):
    split = Mesh(mesh.devices.reshape(4, 4, 4, 2), ("y", "z", "x", "core"))
    narrow = ("x", "core")
    placed = (
        P(narrow, WIDE),
        P(WIDE),
        P(WIDE),
        P(WIDE, narrow),
        P(narrow, WIDE),
        P(narrow),
        P(WIDE, narrow, None, None),
        P(WIDE, narrow, None, None),
        P(WIDE),
    )
    return jax.shard_map(
        body, mesh=split, in_specs=placed, out_specs=P(narrow, WIDE), check_vma=False
    )
```

time: 119 us -> 90 us (0.76)
  blocking collectives: 69.9 us -> 13.4 us
  matrix products: 24.5 us -> 0 us
  Pallas kernels: 0 us -> 22.9 us
  starting transfers between devices: 3.58 us -> 18.7 us
  local copies, waits for them, and re-layouts: 1.44 us -> 15.2 us
  waiting for transfers between devices: 12.7 us -> 17.7 us
  other arithmetic: 5.21 us -> 0.93 us
    all_gather x2 -> x0, blocking collectives: 36.3 us -> none  [side_by_side(): lax.all_gather(both, axis, axis=dim, tiled=True)]
    dot_general x8 -> x0, matrix products: 24.5 us -> none  [the longest x1 5.79 us: body(): jnp.einsum('lgqk,lgsk->lgqs', queries, key_cache, preferred_element_type=...]
    pallas_call x0 -> x6, Pallas kernels: none -> 22.9 us  [the longest x1 12 us: body(): pl.pallas_call(attend_kernel, out_shape=jax.ShapeDtypeStruct((peers, own_...]
    psum x2 -> x0, blocking collectives: 22.6 us -> none  [one_axis_at_a_time(): value = lax.psum(value, axis)]
    unnamed x8 -> x28, local copies, waits for them, and re-layouts: 0.04 us -> 13.9 us
    ppermute x0 -> x8, starting transfers between devices: none -> 10.7 us  [the longest x3 5.75 us: along_x(): lax.ppermute(value, 'x', [(i, (i + s) % 4) for i in range(4)])]
    ppermute x0 -> x8, waiting for transfers between devices: none -> 6.54 us  [the longest x3 3.05 us: along_x(): lax.ppermute(value, 'x', [(i, (i + s) % 4) for i in range(4)])]
    all_to_all x1, starting transfers between devices: 3.58 us -> 8.06 us  [body(): lax.all_to_all(partial, WIDE, split_axis=0, concat_axis=0, tiled=True)]
  transfers between devices with their start and end apart: 1 -> 9, of which waited for: 1 -> 8; matrix products, arithmetic and copies ran while one was open for 0% -> 2% of each run, Pallas kernels for 0% -> 0%
where the time goes in v1:
time: 90 us; the launch traced here: 88.8 us
  Pallas kernels  22.9 us (25%)
  starting transfers between devices  18.7 us (21%)
  waiting for transfers between devices  17.7 us (20%)
  local copies, waits for them, and re-layouts  15.2 us (17%)
  blocking collectives  13.4 us (15%)
  other arithmetic  0.93 us (1%)
    unnamed x28, local copies, waits for them, and re-layouts  13.9 us
    all_to_all x1, blocking collectives, body(): lax.all_to_all(sent, WIDE, split_axis=0, concat_axis=0, tiled=True)  13.4 us
    pallas_call x1, Pallas kernels, body(): pl.pallas_call(attend_kernel, out_shape=jax.ShapeDtypeStruct((peers, own_...  12 us
    all_to_all x1, waiting for transfers between devices, body(): lax.all_to_all(partial, WIDE, split_axis=0, concat_axis=0, tiled=True)  11.1 us
    all_to_all x1, starting transfers between devices, body(): lax.all_to_all(partial, WIDE, split_axis=0, concat_axis=0, tiled=True)  8.06 us
    ppermute x3, starting transfers between devices, along_x(): lax.ppermute(value, 'x', [(i, (i + s) % 4) for i in range(4)])  5.75 us
    ppermute x3, starting transfers between devices, body(): lax.ppermute(v, 'x', [(i, (i + s) % 4) for i in range(4)])  4.91 us
    ppermute x3, waiting for transfers between devices, along_x(): lax.ppermute(value, 'x', [(i, (i + s) % 4) for i in range(4)])  3.05 us
  transfers between devices with their start and end apart: 9, of which 8 were waited for; matrix products, arithmetic and copies ran while one was open for 2% of the time, Pallas kernels for 0%

profile of v1, /device:TPU:0, one launch (start us, length us, event | category | flops | bytes accessed | tf_op | source)
XLA Modules:
  0.0 88.8 jit_solution(3602492048901692927)
XLA Ops:
  0.0 0.0 collective-permute-start
  0.0 1.3 %reshape.18.gain_ref = bf16[1,1024]{1,0:T(2,128)(2,1)} reshape(bf16[1024]{0:T(1024)(128)(2,1)} %param.10) | data formatting | bytes 4096 | tf_op jit(solution)/shard_map/reshape | solution.py:258
  1.3 0.1 collective-permute-done.other_ref
  1.4 0.6 copy-done.13
  2.0 1.8 %rotate_in.1.x0 = bf16[32,1152]{1,0:T(8,128)(2,1)} custom-call(bf16[16,1024]{1,0:T(8,128)(2,1)} %hidden_ref.1, bf16[16,1024]{1,0:T(8,128)(2,1)} %copy-done.13, bf16[1,1024]{1,0:T(2,128)(2,1)} %reshape.18.gain_ref, s32[1,1024]{1,0:T(1,128)} %bitcast.7), custom_call_target="tpu_custom_call" | custom-call | tf_op jit(solution)/shard_map/rotate_in/pallas_call | solution.py:252
  3.8 1.6 %collective-permute-start.1 = (bf16[32,1152]{1,0:T(8,128)(2,1)}, bf16[32,1152]{1,0:T(8,128)(2,1)S(1)}, u32[]{:S(2)}, u32[]{:S(2)}) collective-permute-start(bf16[32,1152]{1,0:T(8,128)(2,1)} %rotate_in.1.x0), channel_id=1, source_target_pairs={{0,2},{2,4},{4,6},{6,0},{1,3},{3,5},{5,7},{7,1},{8,10},{10,12},{12... | collective-permute-start | bytes 221192 | tf_op jit(solution)/shard_map/ppermute | solution.py:238
  5.4 2.7 %collective-permute-start.2 = (bf16[32,1152]{1,0:T(8,128)(2,1)}, bf16[32,1152]{1,0:T(8,128)(2,1)S(1)}, u32[]{:S(2)}, u32[]{:S(2)}) collective-permute-start(bf16[32,1152]{1,0:T(8,128)(2,1)} %rotate_in.1.x0), channel_id=1, source_target_pairs={{0,4},{2,6},{4,0},{6,2},{1,5},{3,7},{5,1},{7,3},{8,12},{10,14},{12... | collective-permute-start | bytes 221192 | tf_op jit(solution)/shard_map/ppermute | solution.py:238
  8.2 1.4 %collective-permute-start.3 = (bf16[32,1152]{1,0:T(8,128)(2,1)}, bf16[32,1152]{1,0:T(8,128)(2,1)S(1)}, u32[]{:S(2)}, u32[]{:S(2)}) collective-permute-start(bf16[32,1152]{1,0:T(8,128)(2,1)} %rotate_in.1.x0), channel_id=1, source_target_pairs={{0,6},{2,0},{4,2},{6,4},{1,7},{3,1},{5,3},{7,5},{8,14},{10,8},{12,... | collective-permute-start | bytes 221192 | tf_op jit(solution)/shard_map/ppermute | solution.py:238
  9.6 0.1 pad_add_fusion.place_ref
  9.7 0.0 copy-start.7
  9.7 0.1 collective-permute-done.1.x1
  9.8 2.6 %collective-permute-done.2.x2 = bf16[32,1152]{1,0:T(8,128)(2,1)S(1)} collective-permute-done((bf16[32,1152]{1,0:T(8,128)(2,1)}, bf16[32,1152]{1,0:T(8,128)(2,1)S(1)}, u32[]{:S(2)}, u32[]{:S(2)}) %collective-permute-start.2) | collective-permute-done | bytes 73760 | tf_op jit(solution)/shard_map/ppermute | solution.py:238
  12.5 0.3 collective-permute-done.3.x3
  12.7 0.0 copy-start.2
  12.7 2.3 %copy-done.2 = bf16[1024,2304]{1,0:T(8,128)(2,1)S(1)} copy-done((bf16[1024,2304]{1,0:T(8,128)(2,1)S(1)}, bf16[1024,2304]{1,0:T(8,128)(2,1)}, u32[]{:S(2)}) %copy-start.2) | copy-done | bytes 4718616
  15.1 0.0 copy-start.4
  15.1 0.9 copy-done.4
  16.0 3.0 %project.1 = bf16[16,8,2432]{2,1,0:T(8,128)(2,1)} custom-call(s32[2]{0:T(128)S(1)} %pad_add_fusion.place_ref, bf16[32,1152]{1,0:T(8,128)(2,1)S(1)} %copy-done.4, bf16[32,1152]{1,0:T(8,128)(2,1)S(1)} %collective-permute-done.1.x1, bf16[32,1152]{1,0:T(8,128)(2,1)S(1)} %collective-permute-done.2.x2, bf16[32,1152]{1,0:T(8,128)(2,1)S(1)} %collective-permute-done.3.x3, ...), custom_call_target="tpu_custom_call" | custom-call | tf_op jit(solution)/shard_map/project/pallas_call | solution.py:259
  19.0 8.1 %all-to-all-start = ((bf16[16,8,2432]{2,1,0:T(8,128)(2,1)}), bf16[16,8,2432]{2,1,0:T(8,128)(2,1)S(1)}, u32[]{:S(2)}, u32[]{:S(2)}) async-start(bf16[16,8,2432]{2,1,0:T(8,128)(2,1)} %project.1), calls=%async_computation | async-start | bytes 1245184 | tf_op jit(solution)/shard_map/all_to_all | solution.py:268
  27.0 0.7 convert_element_type.3
  27.7 0.1 fusion
  27.8 0.1 pad_maximum_fusion
  27.9 11.1 %all-to-all-done.arrived_ref = bf16[16,8,2432]{2,1,0:T(8,128)(2,1)S(1)} async-done(((bf16[16,8,2432]{2,1,0:T(8,128)(2,1)}), bf16[16,8,2432]{2,1,0:T(8,128)(2,1)S(1)}, u32[]{:S(2)}, u32[]{:S(2)}) %all-to-all-start) | async-done | bytes 622624 | tf_op jit(solution)/shard_map/all_to_all | solution.py:268
  39.0 3.4 %copy-done = bf16[8,1,4096,128]{3,2,1,0:T(8,128)(2,1)S(1)} copy-done((bf16[8,1,4096,128]{3,2,1,0:T(8,128)(2,1)S(1)}, bf16[8,1,4096,128]{3,2,1,0:T(8,128)(2,1)}, u32[]{:S(2)}) %copy-start) | copy-done | bytes 8388632
  42.4 3.4 %copy-done.1 = bf16[8,1,4096,128]{3,2,1,0:T(8,128)(2,1)S(1)} copy-done((bf16[8,1,4096,128]{3,2,1,0:T(8,128)(2,1)S(1)}, bf16[8,1,4096,128]{3,2,1,0:T(8,128)(2,1)}, u32[]{:S(2)}) %copy-start.1) | copy-done | bytes 8388632
  45.8 0.7 copy-done.6
  46.5 0.7 copy-done.8
  47.1 12.0 %attend.1 = bf16[16,8,2048]{2,1,0:T(8,128)(2,1)S(1)} custom-call(s32[8]{0:T(128)S(1)} %copy-done.8, bf16[16,8,2432]{2,1,0:T(8,128)(2,1)S(1)} %all-to-all-done.arrived_ref, f32[8,128]{1,0:T(8,128)S(1)} %get-tuple-element.20.cos_ref, f32[8,128]{1,0:T(8,128)S(1)} %get-tuple-element.21.sin_ref, s32[1,2048]{1,0:T(1,128)S(1)} %bitcast.6, ...), custom_call_target="tpu_custom_call" | custom-call | tf_op jit(solution)/shard_map/attend/pallas_call | solution.py:273
  59.2 13.4 %all_to_all.10 = bf16[16,8,2048]{2,1,0:T(8,128)(2,1)S(1)} all-to-all(bf16[16,8,2048]{2,1,0:T(8,128)(2,1)S(1)} %attend.1), channel_id=1, replica_groups=mesh['y'=4,'z'=4,'x'=4,'core'=2] {'y','z'}, dimensions={0} | all-to-all | bytes 1048576 | tf_op jit(solution)/shard_map/all_to_all | solution.py:297
  72.6 0.0 copy-done.7
  72.6 0.0 copy-done.3
  72.6 2.8 %mix.1 = (f32[4,16,1024]{2,1,0:T(8,128)S(1)}, bf16[4,16,1024]{2,1,0:T(8,128)(2,1)S(1)}) custom-call(s32[2]{0:T(128)S(1)} %pad_add_fusion.place_ref, bf16[4,2,16,2048]{3,2,1,0:T(8,128)(2,1)S(1)} %bitcast.5, bf16[2048,1024]{1,0:T(8,128)(2,1)S(1)} %copy-done.3), custom_call_target="tpu_custom_call" | custom-call | tf_op jit(solution)/shard_map/mix/pallas_call | solution.py:298
  75.5 0.0 copy-start.5
  75.5 0.7 copy-done.5
  76.2 0.0 collective-permute-start.4
  76.2 1.3 %collective-permute-done.4.got_ref = bf16[4,16,1024]{2,1,0:T(8,128)(2,1)S(1)} collective-permute-done((bf16[4,16,1024]{2,1,0:T(8,128)(2,1)S(1)}, bf16[4,16,1024]{2,1,0:T(8,128)(2,1)S(1)}, u32[]{:S(2)}, u32[]{:S(2)}) %collective-permute-start.4) | collective-permute-done | bytes 131104 | tf_op jit(solution)/shard_map/ppermute | solution.py:242
  77.5 0.6 copy-done.9
  78.2 1.7 %pair_sum.1 = (f32[16,1024]{1,0:T(8,128)}, bf16[16,1024]{1,0:T(8,128)(2,1)}, bf16[16,1024]{1,0:T(8,128)(2,1)}, bf16[16,1024]{1,0:T(8,128)(2,1)}) custom-call(s32[2]{0:T(128)} %copy-done.7, f32[4,16,1024]{2,1,0:T(8,128)} %copy-done.5, bf16[4,16,1024]{2,1,0:T(8,128)(2,1)} %copy-done.9), custom_call_target="tpu_custom_call" | custom-call | tf_op jit(solution)/shard_map/pair_sum/pallas_call | solution.py:310
  79.8 0.0 collective-permute-start.5
  79.8 2.8 %collective-permute-start.6 = (bf16[16,1024]{1,0:T(8,128)(2,1)}, bf16[16,1024]{1,0:T(8,128)(2,1)S(1)}, u32[]{:S(2)}, u32[]{:S(2)}) collective-permute-start(bf16[16,1024]{1,0:T(8,128)(2,1)} %get-tuple-element.15), channel_id=1, source_target_pairs={{0,4},{2,6},{4,0},{6,2},{1,5},{3,7},{5,1},{7,3},{8,12},{10,14},{12... | collective-permute-start | bytes 98312 | tf_op jit(solution)/shard_map/ppermute | solution.py:319
  82.6 2.1 %collective-permute-start.7 = (bf16[16,1024]{1,0:T(8,128)(2,1)}, bf16[16,1024]{1,0:T(8,128)(2,1)S(1)}, u32[]{:S(2)}, u32[]{:S(2)}) collective-permute-start(bf16[16,1024]{1,0:T(8,128)(2,1)} %get-tuple-element.16), channel_id=1, source_target_pairs={{0,6},{2,0},{4,2},{6,4},{1,7},{3,1},{5,3},{7,5},{8,14},{10,8},{12,... | collective-permute-start | bytes 98312 | tf_op jit(solution)/shard_map/ppermute | solution.py:319
  84.7 0.9 %collective-permute-done.5.r1 = bf16[16,1024]{1,0:T(8,128)(2,1)S(1)} collective-permute-done((bf16[16,1024]{1,0:T(8,128)(2,1)}, bf16[16,1024]{1,0:T(8,128)(2,1)S(1)}, u32[]{:S(2)}, u32[]{:S(2)}) %collective-permute-start.5) | collective-permute-done | bytes 32800 | tf_op jit(solution)/shard_map/ppermute | solution.py:319
  85.6 0.0 collective-permute-done.6.r2
  85.6 1.1 %collective-permute-done.7.r3 = bf16[16,1024]{1,0:T(8,128)(2,1)S(1)} collective-permute-done((bf16[16,1024]{1,0:T(8,128)(2,1)}, bf16[16,1024]{1,0:T(8,128)(2,1)S(1)}, u32[]{:S(2)}, u32[]{:S(2)}) %collective-permute-start.7) | collective-permute-done | bytes 32800 | tf_op jit(solution)/shard_map/ppermute | solution.py:319
  86.7 0.0 copy-done.10
  86.7 0.0 copy-done.11
  86.7 0.6 copy-done.12
  87.3 1.5 %last.1 = bf16[16,1024]{1,0:T(8,128)(2,1)} custom-call(bf16[16,1024]{1,0:T(8,128)(2,1)} %hidden_ref.1, f32[16,1024]{1,0:T(8,128)} %get-tuple-element.13.own_ref, bf16[16,1024]{1,0:T(8,128)(2,1)} %copy-done.10, bf16[16,1024]{1,0:T(8,128)(2,1)} %copy-done.11, bf16[16,1024]{1,0:T(8,128)(2,1)} %copy-done.12), custom_call_target="tpu_custom_call" | custom-call | tf_op jit(solution)/shard_map/last/pallas_call | solution.py:321
  (11 shorter events, 0.0 us)
Async XLA Ops:
  0.0 1.4 %collective-permute-start = (bf16[16,1024]{1,0:T(8,128)(2,1)}, bf16[16,1024]{1,0:T(8,128)(2,1)S(1)}, u32[]{:S(2)}, u32[]{:S(2)}) collective-permute-start(bf16[16,1024]{1,0:T(8,128)(2,1)} %hidden_ref.1), channel_id=1, source_target_pairs={{0,1},{1,0},{2,3},{3,2},{4,5},{5,4},{6,7},{7,6},{8,9},{9,8},{10,11... | collective-permute-start | bytes 98312 | tf_op jit(solution)/shard_map/ppermute | solution.py:242
  1.4 0.6 copy-start.13
  3.8 6.0 %collective-permute-start.1 = (bf16[32,1152]{1,0:T(8,128)(2,1)}, bf16[32,1152]{1,0:T(8,128)(2,1)S(1)}, u32[]{:S(2)}, u32[]{:S(2)}) collective-permute-start(bf16[32,1152]{1,0:T(8,128)(2,1)} %rotate_in.1.x0), channel_id=1, source_target_pairs={{0,2},{2,4},{4,6},{6,0},{1,3},{3,5},{5,7},{7,1},{8,10},{10,12},{12... | collective-permute-start | bytes 221192 | tf_op jit(solution)/shard_map/ppermute | solution.py:238
  5.4 7.0 %collective-permute-start.2 = (bf16[32,1152]{1,0:T(8,128)(2,1)}, bf16[32,1152]{1,0:T(8,128)(2,1)S(1)}, u32[]{:S(2)}, u32[]{:S(2)}) collective-permute-start(bf16[32,1152]{1,0:T(8,128)(2,1)} %rotate_in.1.x0), channel_id=1, source_target_pairs={{0,4},{2,6},{4,0},{6,2},{1,5},{3,7},{5,1},{7,3},{8,12},{10,14},{12... | collective-permute-start | bytes 221192 | tf_op jit(solution)/shard_map/ppermute | solution.py:238
  8.2 4.6 %collective-permute-start.3 = (bf16[32,1152]{1,0:T(8,128)(2,1)}, bf16[32,1152]{1,0:T(8,128)(2,1)S(1)}, u32[]{:S(2)}, u32[]{:S(2)}) collective-permute-start(bf16[32,1152]{1,0:T(8,128)(2,1)} %rotate_in.1.x0), channel_id=1, source_target_pairs={{0,6},{2,0},{4,2},{6,4},{1,7},{3,1},{5,3},{7,5},{8,14},{10,8},{12,... | collective-permute-start | bytes 221192 | tf_op jit(solution)/shard_map/ppermute | solution.py:238
  9.7 62.9 %copy-start.7 = (s32[2]{0:T(128)}, s32[2]{0:T(128)S(1)}, u32[]{:S(2)}) copy-start(s32[2]{0:T(128)S(1)} %pad_add_fusion.place_ref) | copy-start | bytes 28
  12.7 2.3 %copy-start.2 = (bf16[1024,2304]{1,0:T(8,128)(2,1)S(1)}, bf16[1024,2304]{1,0:T(8,128)(2,1)}, u32[]{:S(2)}) copy-start(bf16[1024,2304]{1,0:T(8,128)(2,1)} %weight_hbm.2) | copy-start | bytes 14155780
  15.1 0.9 copy-start.4
  19.0 20.0 %all-to-all-start = ((bf16[16,8,2432]{2,1,0:T(8,128)(2,1)}), bf16[16,8,2432]{2,1,0:T(8,128)(2,1)S(1)}, u32[]{:S(2)}, u32[]{:S(2)}) async-start(bf16[16,8,2432]{2,1,0:T(8,128)(2,1)} %project.1), calls=%async_computation | async-start | bytes 1245184 | tf_op jit(solution)/shard_map/all_to_all | solution.py:268
  39.0 3.4 %copy-start = (bf16[8,1,4096,128]{3,2,1,0:T(8,128)(2,1)S(1)}, bf16[8,1,4096,128]{3,2,1,0:T(8,128)(2,1)}, u32[]{:S(2)}) copy-start(bf16[8,1,4096,128]{3,2,1,0:T(8,128)(2,1)} %key_hbm.1) | copy-start | bytes 25165828
  42.4 3.4 %copy-start.1 = (bf16[8,1,4096,128]{3,2,1,0:T(8,128)(2,1)S(1)}, bf16[8,1,4096,128]{3,2,1,0:T(8,128)(2,1)}, u32[]{:S(2)}) copy-start(bf16[8,1,4096,128]{3,2,1,0:T(8,128)(2,1)} %value_hbm.1) | copy-start | bytes 25165828
  45.8 0.7 copy-start.6
  46.5 0.7 copy-start.8
  47.1 25.5 %copy-start.3 = (bf16[2048,1024]{1,0:T(8,128)(2,1)S(1)}, bf16[2048,1024]{1,0:T(8,128)(2,1)}, u32[]{:S(2)}) copy-start(bf16[2048,1024]{1,0:T(8,128)(2,1)} %weight_hbm.3) | copy-start | bytes 12582916
  75.5 0.7 copy-start.5
  76.2 1.3 %collective-permute-start.4 = (bf16[4,16,1024]{2,1,0:T(8,128)(2,1)S(1)}, bf16[4,16,1024]{2,1,0:T(8,128)(2,1)S(1)}, u32[]{:S(2)}, u32[]{:S(2)}) collective-permute-start(bf16[4,16,1024]{2,1,0:T(8,128)(2,1)S(1)} %get-tuple-element.12), channel_id=1, source_target_pairs={{0,1},{1,0},{2,3},{3,2},{4,5},{5,4},{6,7},{7,6},{8,9},{9,8},{10,11... | collective-permute-start | bytes 393224 | tf_op jit(solution)/shard_map/ppermute | solution.py:242
  77.5 0.6 copy-start.9
  79.8 5.8 %collective-permute-start.5 = (bf16[16,1024]{1,0:T(8,128)(2,1)}, bf16[16,1024]{1,0:T(8,128)(2,1)S(1)}, u32[]{:S(2)}, u32[]{:S(2)}) collective-permute-start(bf16[16,1024]{1,0:T(8,128)(2,1)} %get-tuple-element.14), channel_id=1, source_target_pairs={{0,2},{2,4},{4,6},{6,0},{1,3},{3,5},{5,7},{7,1},{8,10},{10,12},{12... | collective-permute-start | bytes 98312 | tf_op jit(solution)/shard_map/ppermute | solution.py:319
  79.8 5.8 %collective-permute-start.6 = (bf16[16,1024]{1,0:T(8,128)(2,1)}, bf16[16,1024]{1,0:T(8,128)(2,1)S(1)}, u32[]{:S(2)}, u32[]{:S(2)}) collective-permute-start(bf16[16,1024]{1,0:T(8,128)(2,1)} %get-tuple-element.15), channel_id=1, source_target_pairs={{0,4},{2,6},{4,0},{6,2},{1,5},{3,7},{5,1},{7,3},{8,12},{10,14},{12... | collective-permute-start | bytes 98312 | tf_op jit(solution)/shard_map/ppermute | solution.py:319
  82.6 4.1 %collective-permute-start.7 = (bf16[16,1024]{1,0:T(8,128)(2,1)}, bf16[16,1024]{1,0:T(8,128)(2,1)S(1)}, u32[]{:S(2)}, u32[]{:S(2)}) collective-permute-start(bf16[16,1024]{1,0:T(8,128)(2,1)} %get-tuple-element.16), channel_id=1, source_target_pairs={{0,6},{2,0},{4,2},{6,4},{1,7},{3,1},{5,3},{7,5},{8,14},{10,8},{12,... | collective-permute-start | bytes 98312 | tf_op jit(solution)/shard_map/ppermute | solution.py:319
  85.6 1.1 %copy-start.10 = (bf16[16,1024]{1,0:T(8,128)(2,1)}, bf16[16,1024]{1,0:T(8,128)(2,1)S(1)}, u32[]{:S(2)}) copy-start(bf16[16,1024]{1,0:T(8,128)(2,1)S(1)} %collective-permute-done.5.r1) | copy-start | bytes 98308
  85.6 1.1 %copy-start.11 = (bf16[16,1024]{1,0:T(8,128)(2,1)}, bf16[16,1024]{1,0:T(8,128)(2,1)S(1)}, u32[]{:S(2)}) copy-start(bf16[16,1024]{1,0:T(8,128)(2,1)S(1)} %collective-permute-done.6.r2) | copy-start | bytes 98308
  86.7 0.6 copy-start.12

commit v2 on v1

--- a/solution.py
+++ b/solution.py
@@ -36,10 +36,10 @@
     return jnp.dot(high, matrix, preferred_element_type=F32) + jnp.dot(low, matrix, preferred_element_type=F32)
 
 
-def rotate_in_kernel(own_ref, other_ref, gain_ref, sign_ref, out_ref):
+def rotate_in_kernel(own_ref, other_ref, steer_ref, out_ref):
     features = own_ref.shape[1]
     matrix = hadamard_signs()
-    steer = gain_ref[...].astype(F32) * (2 * sign_ref[...] - 1).astype(F32)
+    steer = steer_ref[...]
     lane = lax.broadcasted_iota(jnp.int32, (16, EXTRA), 1)
     for at, ref in enumerate((own_ref, other_ref)):
         rows = ref[...].astype(F32)
@@ -55,16 +55,9 @@
             out_ref[16 * at : 16 * at + 16, b * HD : (b + 1) * HD] = turned.astype(BF16)
 
 
-def project_kernel(place_ref, x0, x1, x2, x3, weight_hbm, out_ref, weight, sems):
+def project_kernel(place_ref, x0, x1, x2, x3, weight, out_ref):
     parts, width = 3, weight.shape[1] // 3
     features = weight.shape[0]
-
-    def fetch(i):
-        cols = pl.ds(i * width, width)
-        return pltpu.make_async_copy(weight_hbm.at[:, cols], weight.at[:, cols], sems.at[i])
-
-    for i in range(parts):
-        fetch(i).start()
     x, c = place_ref[0], place_ref[1]
     received = (x0, x1, x2, x3)
     targets = []
@@ -79,41 +72,24 @@
             out_ref[targets[4 * s + j], :, weight.shape[1] :] = extra[8 * j : 8 * j + 8].astype(BF16)
     rows = jnp.concatenate([r[:, :features] for r in received], axis=0)
     for i in range(parts):
-        fetch(i).wait()
         product = jnp.dot(rows, weight[:, i * width : (i + 1) * width], preferred_element_type=F32)
         for j in range(16):
             out_ref[targets[j], :, i * width : (i + 1) * width] = product[8 * j : 8 * j + 8].astype(BF16)
 
 
 CHUNK = 1024
+COVER = (10, 10, 10)
 
 
 def attend_kernel(
-    lengths_ref, arrived_ref, cos_ref, sin_ref, sign_ref, key_hbm, value_hbm, out_ref,
-    keys, values, queries, scores, attended, sems,
+    lengths_ref, arrived_ref, cos_ref, sin_ref, sign_ref, keys, values, out_ref, queries, scores, attended
 ):
     lists = lengths_ref.shape[0]
-    slots = keys.shape[1]
-    chunks = slots // CHUNK
-
-    def fetch(which, pair, half, chunk):
-        source, target = ((key_hbm, keys), (value_hbm, values))[which]
-        span = pl.ds(chunk * CHUNK, CHUNK)
-        return pltpu.make_async_copy(
-            source.at[2 * pair + half, 0, span, :],
-            target.at[pair, span, pl.ds(half * HD, HD)],
-            sems.at[which, pair, half, chunk],
-        )
-
     longest = [jnp.maximum(lengths_ref[2 * p], lengths_ref[2 * p + 1]) for p in range(lists // 2)]
-    for pair in range(lists // 2):
-        for chunk in range(chunks):
-
-            @pl.when(chunk * CHUNK < longest[pair])
-            def _():
-                for which in range(2):
-                    for half in range(2):
-                        fetch(which, pair, half, chunk).start()
+
+    def wide(ref, pair, start):
+        span = pl.ds(start, CHUNK)
+        return jnp.concatenate([ref[2 * pair, 0, span, :], ref[2 * pair + 1, 0, span, :]], axis=1)
 
     total = arrived_ref[0].astype(F32)
     for w in range(1, arrived_ref.shape[0]):
@@ -148,11 +124,9 @@
         live_chunks = (longest[pair] + CHUNK - 1) // CHUNK
 
         def score(chunk, peak):
-            for half in range(2):
-                fetch(0, pair, half, chunk).wait()
             start = pl.multiple_of(chunk * CHUNK, CHUNK)
             block = lax.dot_general(
-                q_wide, keys[pair, pl.ds(start, CHUNK), :], (((1,), (1,)), ((), ())), preferred_element_type=F32
+                q_wide, wide(keys, pair, start), (((1,), (1,)), ((), ())), preferred_element_type=F32
             )
             slot = lax.broadcasted_iota(jnp.int32, (2 * QG, CHUNK), 1) + start
             block = jnp.where(slot < length, block * scale, -1e30)
@@ -166,14 +140,12 @@
 
         def mix(chunk, carry):
             mass, mixed = carry
-            for half in range(2):
-                fetch(1, pair, half, chunk).wait()
             start = pl.multiple_of(chunk * CHUNK, CHUNK)
             weight = jnp.exp(scores[:, pl.ds(start, CHUNK)] - peak)
             for t in range(CHUNK // HD):
                 mass = mass + weight[:, t * HD : (t + 1) * HD]
             mixed = mixed + jnp.dot(
-                weight.astype(BF16), values[pair, pl.ds(start, CHUNK), :], preferred_element_type=F32
+                weight.astype(BF16), wide(values, pair, start), preferred_element_type=F32
             )
             return mass, mixed
 
@@ -189,8 +161,7 @@
     matrix = hadamard_signs()
     steered = []
     for h in range(QG):
-        sign = (2 * sign_ref[:, h * HD : (h + 1) * HD] - 1).astype(F32)
-        steered.append(attended[pl.ds(h, lists, stride=QG), :] * sign)
+        steered.append(attended[pl.ds(h, lists, stride=QG), :] * sign_ref[:, h * HD : (h + 1) * HD])
     turned = two_piece_dot(jnp.concatenate(steered, axis=0), matrix) * (1.0 / math.sqrt(HD))
     for h in range(QG):
         piece = turned[lists * h : lists * (h + 1)].astype(BF16)
@@ -198,19 +169,11 @@
             out_ref[w, :, h * HD : (h + 1) * HD] = piece
 
 
-def mix_kernel(place_ref, rows_ref, weight_hbm, keep_ref, send_ref, weight, sems):
+def mix_kernel(place_ref, rows_ref, weight, keep_ref, send_ref):
     parts, width = 4, weight.shape[1] // 4
-
-    def fetch(i):
-        cols = pl.ds(i * width, width)
-        return pltpu.make_async_copy(weight_hbm.at[:, cols], weight.at[:, cols], sems.at[i])
-
-    for i in range(parts):
-        fetch(i).start()
     c = place_ref[1]
     rows = jnp.concatenate([rows_ref[x, c] for x in range(4)] + [rows_ref[x, 1 - c] for x in range(4)], axis=0)
     for i in range(parts):
-        fetch(i).wait()
         product = jnp.dot(rows, weight[:, i * width : (i + 1) * width], preferred_element_type=F32)
         for x in range(4):
             keep_ref[x, :, i * width : (i + 1) * width] = product[16 * x : 16 * x + 16]
@@ -234,6 +197,10 @@
     return pltpu.CompilerParams(vmem_limit_bytes=limit * MIB)
 
 
+def cost(microseconds):
+    return pl.CostEstimate(flops=int(microseconds * 1.1e9), transcendentals=0, bytes_accessed=int(microseconds * 3e6))
+
+
 def along_x(value):
     return [lax.ppermute(value, "x", [(i, (i + s) % 4) for i in range(4)]) for s in (1, 2, 3)]
 
@@ -249,20 +216,23 @@
     peers = lax.axis_size(WIDE)
     place = jnp.stack([lax.axis_index("x"), lax.axis_index("core")]).astype(jnp.int32)
 
+    steer = gain.astype(F32) * (2 * sign_in - 1).astype(F32)
     rotated = pl.pallas_call(
         rotate_in_kernel,
         out_shape=jax.ShapeDtypeStruct((2 * rows, features + EXTRA), BF16),
-        in_specs=[VMEM] * 4,
+        in_specs=[VMEM] * 3,
         out_specs=VMEM,
+        compiler_params=params(4),
+        cost_estimate=cost(COVER[0]),
         name="rotate_in",
-    )(hidden, across_cores(hidden), gain.reshape(1, -1), sign_in.reshape(1, -1))
+    )(hidden, across_cores(hidden), steer.reshape(1, -1))
     partial = pl.pallas_call(
         project_kernel,
         out_shape=jax.ShapeDtypeStruct((peers, own_lists, columns + EXTRA), BF16),
-        in_specs=[SMEM] + [VMEM] * 4 + [HBM],
+        in_specs=[SMEM] + [VMEM] * 5,
         out_specs=VMEM,
-        scratch_shapes=[pltpu.VMEM((features, columns), BF16), pltpu.SemaphoreType.DMA((3,))],
-        compiler_params=params(16),
+        compiler_params=params(8),
+        cost_estimate=cost(COVER[1]),
         name="project",
     )(place, rotated, *along_x(rotated), qkv_weight)
     arrived = lax.all_to_all(partial, WIDE, split_axis=0, concat_axis=0, tiled=True)
@@ -273,24 +243,22 @@
     sent = pl.pallas_call(
         attend_kernel,
         out_shape=jax.ShapeDtypeStruct((peers, own_lists, QG * HD), BF16),
-        in_specs=[SMEM] + [VMEM] * 4 + [HBM] * 2,
+        in_specs=[SMEM] + [VMEM] * 6,
         out_specs=VMEM,
         scratch_shapes=[
-            pltpu.VMEM((own_lists // 2, slots, 2 * HD), BF16),
-            pltpu.VMEM((own_lists // 2, slots, 2 * HD), BF16),
             pltpu.VMEM((own_lists, 24, HD), F32),
             pltpu.VMEM((2 * QG, slots), F32),
             pltpu.VMEM((own_lists * QG, HD), F32),
-            pltpu.SemaphoreType.DMA((2, own_lists // 2, 2, slots // CHUNK)),
         ],
-        compiler_params=params(32),
+        compiler_params=params(20),
+        cost_estimate=cost(COVER[2]),
         name="attend",
     )(
-        lengths,
+        jnp.minimum(lengths, slots),
         arrived,
         jnp.concatenate([cosine, cosine], axis=1),
         jnp.concatenate([-sine, sine], axis=1),
-        sign_attn.reshape(1, -1),
+        (2 * sign_attn - 1).astype(F32).reshape(1, -1),
         key_cache,
         value_cache,
     )
@@ -301,10 +269,9 @@
             jax.ShapeDtypeStruct((4, rows, features), F32),
             jax.ShapeDtypeStruct((4, rows, features), BF16),
         ),
-        in_specs=[SMEM, VMEM, HBM],
+        in_specs=[SMEM, VMEM, VMEM],
         out_specs=(VMEM, VMEM),
-        scratch_shapes=[pltpu.VMEM(out_weight.shape, BF16), pltpu.SemaphoreType.DMA((4,))],
-        compiler_params=params(16),
+        compiler_params=params(8),
         name="mix",
     )(place, gathered.reshape(4, 2, rows, QG * HD), out_weight)
     own, *sends = pl.pallas_call(
@@ -313,6 +280,7 @@
         + (jax.ShapeDtypeStruct((rows, features), BF16),) * 3,
         in_specs=[SMEM, VMEM, VMEM],
         out_specs=(VMEM,) * 4,
+        compiler_params=params(4),
         name="pair_sum",
     )(place, keep, across_cores(send))
     got = [
@@ -323,6 +291,7 @@
         out_shape=jax.ShapeDtypeStruct((rows, features), BF16),
         in_specs=[VMEM] * 5,
         out_specs=VMEM,
+        compiler_params=params(4),
         name="last",
     )(hidden, own, *got)
 

time: 90 us -> 74.6 us (0.83)
  Pallas kernels: 22.9 us -> 12.9 us
  local copies, waits for them, and re-layouts: 15.2 us -> 7.54 us
  blocking collectives: 13.4 us -> 15 us
    unnamed x28 -> x14, local copies, waits for them, and re-layouts: 13.9 us -> 7.54 us
    pallas_call x1, Pallas kernels: 12 us -> 7.8 us  [body(): pl.pallas_call(attend_kernel, out_shape=jax.ShapeDtypeStruct((peers, own_...]
    pallas_call x1, Pallas kernels: 2.85 us -> 1.26 us  [body(): pl.pallas_call(mix_kernel, out_shape=(jax.ShapeDtypeStruct((4, rows, feat...]
    all_to_all x1, blocking collectives: 13.4 us -> 15 us  [body(): lax.all_to_all(sent, WIDE, split_axis=0, concat_axis=0, tiled=True)]
    pallas_call x1, Pallas kernels: 1.81 us -> 0.4 us  [body(): pl.pallas_call(rotate_in_kernel, out_shape=jax.ShapeDtypeStruct((2 * rows...]
    reshape x1 -> x0, local copies, waits for them, and re-layouts: 1.27 us -> none  [body(): gain.reshape(1, -1)]
    pallas_call x1, Pallas kernels: 1.66 us -> 0.57 us  [body(): pl.pallas_call(pair_sum_kernel, out_shape=(jax.ShapeDtypeStruct((rows, fe...]
  transfers between devices with their start and end apart: 9 -> 9, of which waited for: 8 -> 7; matrix products, arithmetic and copies ran while one was open for 2% -> 2% of each run, Pallas kernels for 0% -> 0%
where the time goes in v2:
time: 74.6 us; the launch traced here: 73.7 us
  starting transfers between devices  19 us (25%)
  waiting for transfers between devices  17.6 us (24%)
  blocking collectives  15 us (20%)
  Pallas kernels  12.9 us (17%)
  local copies, waits for them, and re-layouts  7.54 us (10%)
  other arithmetic  1.71 us (2%)
    all_to_all x1, blocking collectives, body(): lax.all_to_all(sent, WIDE, split_axis=0, concat_axis=0, tiled=True)  15 us
    all_to_all x1, waiting for transfers between devices, body(): lax.all_to_all(partial, WIDE, split_axis=0, concat_axis=0, tiled=True)  11.8 us
    all_to_all x1, starting transfers between devices, body(): lax.all_to_all(partial, WIDE, split_axis=0, concat_axis=0, tiled=True)  8.05 us
    pallas_call x1, Pallas kernels, body(): pl.pallas_call(attend_kernel, out_shape=jax.ShapeDtypeStruct((peers, own_...  7.8 us
    unnamed x14, local copies, waits for them, and re-layouts  7.54 us
    ppermute x3, starting transfers between devices, along_x(): lax.ppermute(value, 'x', [(i, (i + s) % 4) for i in range(4)])  5.76 us
    ppermute x3, starting transfers between devices, body(): lax.ppermute(v, 'x', [(i, (i + s) % 4) for i in range(4)])  5.11 us
    ppermute x3, waiting for transfers between devices, along_x(): lax.ppermute(value, 'x', [(i, (i + s) % 4) for i in range(4)])  2.84 us
  transfers between devices with their start and end apart: 9, of which 7 were waited for; matrix products, arithmetic and copies ran while one was open for 2% of the time, Pallas kernels for 0%

profile of v2, /device:TPU:0, one launch (start us, length us, event | category | flops | bytes accessed | tf_op | source)
XLA Modules:
  0.0 73.7 jit_solution(138804602240771357)
XLA Ops:
  0.0 0.0 collective-permute-start
  0.0 0.7 convert_multiply_fusion
  0.7 0.7 fusion.1
  1.4 0.0 collective-permute-done.other_ref
  1.4 0.0 copy-start.1
  1.4 0.8 %copy-done.1 = bf16[16,1024]{1,0:T(8,128)(2,1)S(1)} copy-done((bf16[16,1024]{1,0:T(8,128)(2,1)S(1)}, bf16[16,1024]{1,0:T(8,128)(2,1)}, u32[]{:S(2)}) %copy-start.1) | copy-done | bytes 32792
  2.2 0.0 copy-start.5
  2.2 0.4 rotate_in.1.x0
  2.6 1.6 %collective-permute-start.1 = (bf16[32,1152]{1,0:T(8,128)(2,1)S(1)}, bf16[32,1152]{1,0:T(8,128)(2,1)S(1)}, u32[]{:S(2)}, u32[]{:S(2)}) collective-permute-start(bf16[32,1152]{1,0:T(8,128)(2,1)S(1)} %rotate_in.1.x0), channel_id=1, source_target_pairs={{0,2},{2,4},{4,6},{6,0},{1,3},{3,5},{5,7},{7,1},{8,10},{10,12},{12... | collective-permute-start | bytes 221192 | tf_op jit(solution)/shard_map/ppermute | solution.py:205
  4.2 2.7 %collective-permute-start.2 = (bf16[32,1152]{1,0:T(8,128)(2,1)S(1)}, bf16[32,1152]{1,0:T(8,128)(2,1)S(1)}, u32[]{:S(2)}, u32[]{:S(2)}) collective-permute-start(bf16[32,1152]{1,0:T(8,128)(2,1)S(1)} %rotate_in.1.x0), channel_id=1, source_target_pairs={{0,4},{2,6},{4,0},{6,2},{1,5},{3,7},{5,1},{7,3},{8,12},{10,14},{12... | collective-permute-start | bytes 221192 | tf_op jit(solution)/shard_map/ppermute | solution.py:205
  6.9 1.4 %collective-permute-start.3 = (bf16[32,1152]{1,0:T(8,128)(2,1)S(1)}, bf16[32,1152]{1,0:T(8,128)(2,1)S(1)}, u32[]{:S(2)}, u32[]{:S(2)}) collective-permute-start(bf16[32,1152]{1,0:T(8,128)(2,1)S(1)} %rotate_in.1.x0), channel_id=1, source_target_pairs={{0,6},{2,0},{4,2},{6,4},{1,7},{3,1},{5,3},{7,5},{8,14},{10,8},{12,... | collective-permute-start | bytes 221192 | tf_op jit(solution)/shard_map/ppermute | solution.py:205
  8.4 0.1 pad_add_fusion.place_ref
  8.4 0.0 copy-start.6
  8.4 0.1 collective-permute-done.1.x1
  8.5 2.6 %collective-permute-done.2.x2 = bf16[32,1152]{1,0:T(8,128)(2,1)S(1)} collective-permute-done((bf16[32,1152]{1,0:T(8,128)(2,1)S(1)}, bf16[32,1152]{1,0:T(8,128)(2,1)S(1)}, u32[]{:S(2)}, u32[]{:S(2)}) %collective-permute-start.2) | collective-permute-done | bytes 73760 | tf_op jit(solution)/shard_map/ppermute | solution.py:205
  11.2 0.1 collective-permute-done.3.x3
  11.3 0.0 copy-done.5
  11.3 2.2 %project.1 = bf16[16,8,2432]{2,1,0:T(8,128)(2,1)} custom-call(s32[2]{0:T(128)S(1)} %pad_add_fusion.place_ref, bf16[32,1152]{1,0:T(8,128)(2,1)S(1)} %rotate_in.1.x0, bf16[32,1152]{1,0:T(8,128)(2,1)S(1)} %collective-permute-done.1.x1, bf16[32,1152]{1,0:T(8,128)(2,1)S(1)} %collective-permute-done.2.x2, bf16[32,1152]{1,0:T(8,128)(2,1)S(1)} %collective-permute-done.3.x3, ...), custom_call_target="tpu_custom_call" | custom-call | flops 11000000512 | bytes 30000000 | tf_op jit(solution)/shard_map/project/pallas_call | solution.py:229
  13.5 8.0 %all-to-all-start = ((bf16[16,8,2432]{2,1,0:T(8,128)(2,1)}), bf16[16,8,2432]{2,1,0:T(8,128)(2,1)S(1)}, u32[]{:S(2)}, u32[]{:S(2)}) async-start(bf16[16,8,2432]{2,1,0:T(8,128)(2,1)} %project.1), calls=%async_computation | async-start | bytes 1245184 | tf_op jit(solution)/shard_map/all_to_all | solution.py:238
  21.6 0.1 fusion
  21.7 0.1 pad_maximum_fusion
  21.7 0.0 copy-done.6
  21.8 11.8 %all-to-all-done.arrived_ref = bf16[16,8,2432]{2,1,0:T(8,128)(2,1)S(1)} async-done(((bf16[16,8,2432]{2,1,0:T(8,128)(2,1)}), bf16[16,8,2432]{2,1,0:T(8,128)(2,1)S(1)}, u32[]{:S(2)}, u32[]{:S(2)}) %all-to-all-start) | async-done | bytes 622624 | tf_op jit(solution)/shard_map/all_to_all | solution.py:238
  33.6 0.0 copy-start.3
  33.6 3.4 %copy-done.3 = bf16[8,1,4096,128]{3,2,1,0:T(8,128)(2,1)S(1)} copy-done((bf16[8,1,4096,128]{3,2,1,0:T(8,128)(2,1)S(1)}, bf16[8,1,4096,128]{3,2,1,0:T(8,128)(2,1)}, u32[]{:S(2)}) %copy-start.3) | copy-done | bytes 8388632
  36.9 0.0 copy-start.4
  36.9 3.4 %copy-done.4 = bf16[8,1,4096,128]{3,2,1,0:T(8,128)(2,1)S(1)} copy-done((bf16[8,1,4096,128]{3,2,1,0:T(8,128)(2,1)S(1)}, bf16[8,1,4096,128]{3,2,1,0:T(8,128)(2,1)}, u32[]{:S(2)}) %copy-start.4) | copy-done | bytes 8388632
  40.3 0.0 copy-start
  40.3 0.0 copy-start.2
  40.3 7.8 %attend.1 = bf16[16,8,2048]{2,1,0:T(8,128)(2,1)S(1)} custom-call(s32[8]{0:T(128)S(1)} %get-tuple-element.21.lengths_ref, bf16[16,8,2432]{2,1,0:T(8,128)(2,1)S(1)} %all-to-all-done.arrived_ref, f32[8,128]{1,0:T(8,128)S(1)} %get-tuple-element.22.cos_ref, f32[8,128]{1,0:T(8,128)S(1)} %get-tuple-element.23.sin_ref, f32[1,2048]{1,0:T(1,128)S(1)} %bitcast.6, ...), custom_call_target="tpu_custom_call" | custom-call | flops 11000000512 | bytes 30000000 | tf_op jit(solution)/shard_map/attend/pallas_call | solution.py:243
  48.1 15.0 %all_to_all.10 = bf16[16,8,2048]{2,1,0:T(8,128)(2,1)S(1)} all-to-all(bf16[16,8,2048]{2,1,0:T(8,128)(2,1)S(1)} %attend.1), channel_id=1, replica_groups=mesh['y'=4,'z'=4,'x'=4,'core'=2] {'y','z'}, dimensions={0} | all-to-all | bytes 1048576 | tf_op jit(solution)/shard_map/all_to_all | solution.py:265
  63.1 0.0 copy-done
  63.1 1.3 %mix.1 = (f32[4,16,1024]{2,1,0:T(8,128)S(1)}, bf16[4,16,1024]{2,1,0:T(8,128)(2,1)S(1)}) custom-call(s32[2]{0:T(128)S(1)} %pad_add_fusion.place_ref, bf16[4,2,16,2048]{3,2,1,0:T(8,128)(2,1)S(1)} %bitcast.5, bf16[2048,1024]{1,0:T(8,128)(2,1)S(1)} %copy-done), custom_call_target="tpu_custom_call" | custom-call | tf_op jit(solution)/shard_map/mix/pallas_call | solution.py:266
  64.4 0.1 collective-permute-start.4
  64.5 1.3 %collective-permute-done.4.got_ref = bf16[4,16,1024]{2,1,0:T(8,128)(2,1)S(1)} collective-permute-done((bf16[4,16,1024]{2,1,0:T(8,128)(2,1)S(1)}, bf16[4,16,1024]{2,1,0:T(8,128)(2,1)S(1)}, u32[]{:S(2)}, u32[]{:S(2)}) %collective-permute-start.4) | collective-permute-done | bytes 131104 | tf_op jit(solution)/shard_map/ppermute | solution.py:209
  65.8 0.6 pair_sum.1
  66.4 0.1 collective-permute-start.5
  66.5 2.7 %collective-permute-start.6 = (bf16[16,1024]{1,0:T(8,128)(2,1)S(1)}, bf16[16,1024]{1,0:T(8,128)(2,1)S(1)}, u32[]{:S(2)}, u32[]{:S(2)}) collective-permute-start(bf16[16,1024]{1,0:T(8,128)(2,1)S(1)} %get-tuple-element.15), channel_id=1, source_target_pairs={{0,4},{2,6},{4,0},{6,2},{1,5},{3,7},{5,1},{7,3},{8,12},{10,14},{12... | collective-permute-start | bytes 98312 | tf_op jit(solution)/shard_map/ppermute | solution.py:287
  69.2 2.3 %collective-permute-start.7 = (bf16[16,1024]{1,0:T(8,128)(2,1)S(1)}, bf16[16,1024]{1,0:T(8,128)(2,1)S(1)}, u32[]{:S(2)}, u32[]{:S(2)}) collective-permute-start(bf16[16,1024]{1,0:T(8,128)(2,1)S(1)} %get-tuple-element.16), channel_id=1, source_target_pairs={{0,6},{2,0},{4,2},{6,4},{1,7},{3,1},{5,3},{7,5},{8,14},{10,8},{12,... | collective-permute-start | bytes 98312 | tf_op jit(solution)/shard_map/ppermute | solution.py:287
  71.5 0.6 collective-permute-done.5.r1
  72.1 0.0 collective-permute-done.6.r2
  72.1 1.0 %collective-permute-done.7.r3 = bf16[16,1024]{1,0:T(8,128)(2,1)S(1)} collective-permute-done((bf16[16,1024]{1,0:T(8,128)(2,1)S(1)}, bf16[16,1024]{1,0:T(8,128)(2,1)S(1)}, u32[]{:S(2)}, u32[]{:S(2)}) %collective-permute-start.7) | collective-permute-done | bytes 32800 | tf_op jit(solution)/shard_map/ppermute | solution.py:287
  73.1 0.0 copy-done.2
  73.1 0.6 last.1
  (2 shorter events, 0.0 us)
Async XLA Ops:
  0.0 1.4 %collective-permute-start = (bf16[16,1024]{1,0:T(8,128)(2,1)}, bf16[16,1024]{1,0:T(8,128)(2,1)S(1)}, u32[]{:S(2)}, u32[]{:S(2)}) collective-permute-start(bf16[16,1024]{1,0:T(8,128)(2,1)} %hidden_ref.1), channel_id=1, source_target_pairs={{0,1},{1,0},{2,3},{3,2},{4,5},{5,4},{6,7},{7,6},{8,9},{9,8},{10,11... | collective-permute-start | bytes 98312 | tf_op jit(solution)/shard_map/ppermute | solution.py:209
  1.4 0.8 %copy-start.1 = (bf16[16,1024]{1,0:T(8,128)(2,1)S(1)}, bf16[16,1024]{1,0:T(8,128)(2,1)}, u32[]{:S(2)}) copy-start(bf16[16,1024]{1,0:T(8,128)(2,1)} %hidden_ref.1) | copy-start | bytes 98308
  2.2 9.1 %copy-start.5 = (bf16[1024,2304]{1,0:T(8,128)(2,1)S(1)}, bf16[1024,2304]{1,0:T(8,128)(2,1)}, u32[]{:S(2)}) copy-start(bf16[1024,2304]{1,0:T(8,128)(2,1)} %weight.2) | copy-start | bytes 14155780
  2.6 5.9 %collective-permute-start.1 = (bf16[32,1152]{1,0:T(8,128)(2,1)S(1)}, bf16[32,1152]{1,0:T(8,128)(2,1)S(1)}, u32[]{:S(2)}, u32[]{:S(2)}) collective-permute-start(bf16[32,1152]{1,0:T(8,128)(2,1)S(1)} %rotate_in.1.x0), channel_id=1, source_target_pairs={{0,2},{2,4},{4,6},{6,0},{1,3},{3,5},{5,7},{7,1},{8,10},{10,12},{12... | collective-permute-start | bytes 221192 | tf_op jit(solution)/shard_map/ppermute | solution.py:205
  4.2 7.0 %collective-permute-start.2 = (bf16[32,1152]{1,0:T(8,128)(2,1)S(1)}, bf16[32,1152]{1,0:T(8,128)(2,1)S(1)}, u32[]{:S(2)}, u32[]{:S(2)}) collective-permute-start(bf16[32,1152]{1,0:T(8,128)(2,1)S(1)} %rotate_in.1.x0), channel_id=1, source_target_pairs={{0,4},{2,6},{4,0},{6,2},{1,5},{3,7},{5,1},{7,3},{8,12},{10,14},{12... | collective-permute-start | bytes 221192 | tf_op jit(solution)/shard_map/ppermute | solution.py:205
  6.9 4.4 %collective-permute-start.3 = (bf16[32,1152]{1,0:T(8,128)(2,1)S(1)}, bf16[32,1152]{1,0:T(8,128)(2,1)S(1)}, u32[]{:S(2)}, u32[]{:S(2)}) collective-permute-start(bf16[32,1152]{1,0:T(8,128)(2,1)S(1)} %rotate_in.1.x0), channel_id=1, source_target_pairs={{0,6},{2,0},{4,2},{6,4},{1,7},{3,1},{5,3},{7,5},{8,14},{10,8},{12,... | collective-permute-start | bytes 221192 | tf_op jit(solution)/shard_map/ppermute | solution.py:205
  8.4 13.3 %copy-start.6 = (s32[2048]{0:T(1024)S(1)}, s32[2048]{0:T(1024)}, u32[]{:S(2)}) copy-start(s32[2048]{0:T(1024)} %param.14) | copy-start | bytes 24580
  13.5 20.1 %all-to-all-start = ((bf16[16,8,2432]{2,1,0:T(8,128)(2,1)}), bf16[16,8,2432]{2,1,0:T(8,128)(2,1)S(1)}, u32[]{:S(2)}, u32[]{:S(2)}) async-start(bf16[16,8,2432]{2,1,0:T(8,128)(2,1)} %project.1), calls=%async_computation | async-start | bytes 1245184 | tf_op jit(solution)/shard_map/all_to_all | solution.py:238
  33.6 3.4 %copy-start.3 = (bf16[8,1,4096,128]{3,2,1,0:T(8,128)(2,1)S(1)}, bf16[8,1,4096,128]{3,2,1,0:T(8,128)(2,1)}, u32[]{:S(2)}) copy-start(bf16[8,1,4096,128]{3,2,1,0:T(8,128)(2,1)} %keys.1) | copy-start | bytes 25165828
  36.9 3.4 %copy-start.4 = (bf16[8,1,4096,128]{3,2,1,0:T(8,128)(2,1)S(1)}, bf16[8,1,4096,128]{3,2,1,0:T(8,128)(2,1)}, u32[]{:S(2)}) copy-start(bf16[8,1,4096,128]{3,2,1,0:T(8,128)(2,1)} %values.1) | copy-start | bytes 25165828
  40.3 22.8 %copy-start = (bf16[2048,1024]{1,0:T(8,128)(2,1)S(1)}, bf16[2048,1024]{1,0:T(8,128)(2,1)}, u32[]{:S(2)}) copy-start(bf16[2048,1024]{1,0:T(8,128)(2,1)} %weight.3) | copy-start | bytes 12582916
  40.3 32.8 %copy-start.2 = (bf16[16,1024]{1,0:T(8,128)(2,1)S(1)}, bf16[16,1024]{1,0:T(8,128)(2,1)}, u32[]{:S(2)}) copy-start(bf16[16,1024]{1,0:T(8,128)(2,1)} %hidden_ref.1) | copy-start | bytes 98308
  64.4 1.4 %collective-permute-start.4 = (bf16[4,16,1024]{2,1,0:T(8,128)(2,1)S(1)}, bf16[4,16,1024]{2,1,0:T(8,128)(2,1)S(1)}, u32[]{:S(2)}, u32[]{:S(2)}) collective-permute-start(bf16[4,16,1024]{2,1,0:T(8,128)(2,1)S(1)} %get-tuple-element.12), channel_id=1, source_target_pairs={{0,1},{1,0},{2,3},{3,2},{4,5},{5,4},{6,7},{7,6},{8,9},{9,8},{10,11... | collective-permute-start | bytes 393224 | tf_op jit(solution)/shard_map/ppermute | solution.py:209
  66.4 5.7 %collective-permute-start.5 = (bf16[16,1024]{1,0:T(8,128)(2,1)S(1)}, bf16[16,1024]{1,0:T(8,128)(2,1)S(1)}, u32[]{:S(2)}, u32[]{:S(2)}) collective-permute-start(bf16[16,1024]{1,0:T(8,128)(2,1)S(1)} %get-tuple-element.14), channel_id=1, source_target_pairs={{0,2},{2,4},{4,6},{6,0},{1,3},{3,5},{5,7},{7,1},{8,10},{10,12},{12... | collective-permute-start | bytes 98312 | tf_op jit(solution)/shard_map/ppermute | solution.py:287
  66.5 5.6 %collective-permute-start.6 = (bf16[16,1024]{1,0:T(8,128)(2,1)S(1)}, bf16[16,1024]{1,0:T(8,128)(2,1)S(1)}, u32[]{:S(2)}, u32[]{:S(2)}) collective-permute-start(bf16[16,1024]{1,0:T(8,128)(2,1)S(1)} %get-tuple-element.15), channel_id=1, source_target_pairs={{0,4},{2,6},{4,0},{6,2},{1,5},{3,7},{5,1},{7,3},{8,12},{10,14},{12... | collective-permute-start | bytes 98312 | tf_op jit(solution)/shard_map/ppermute | solution.py:287
  69.2 3.9 %collective-permute-start.7 = (bf16[16,1024]{1,0:T(8,128)(2,1)S(1)}, bf16[16,1024]{1,0:T(8,128)(2,1)S(1)}, u32[]{:S(2)}, u32[]{:S(2)}) collective-permute-start(bf16[16,1024]{1,0:T(8,128)(2,1)S(1)} %get-tuple-element.16), channel_id=1, source_target_pairs={{0,6},{2,0},{4,2},{6,4},{1,7},{3,1},{5,3},{7,5},{8,14},{10,8},{12,... | collective-permute-start | bytes 98312 | tf_op jit(solution)/shard_map/ppermute | solution.py:287

commit v3 on v2

--- a/solution.py
+++ b/solution.py
@@ -77,18 +77,18 @@
             out_ref[targets[j], :, i * width : (i + 1) * width] = product[8 * j : 8 * j + 8].astype(BF16)
 
 
-CHUNK = 1024
 COVER = (10, 10, 10)
+TILE = 512
 
 
 def attend_kernel(
     lengths_ref, arrived_ref, cos_ref, sin_ref, sign_ref, keys, values, out_ref, queries, scores, attended
 ):
-    lists = lengths_ref.shape[0]
-    longest = [jnp.maximum(lengths_ref[2 * p], lengths_ref[2 * p + 1]) for p in range(lists // 2)]
+    lists, slots = keys.shape[0], keys.shape[2]
+    pairs = lists // 2
 
     def wide(ref, pair, start):
-        span = pl.ds(start, CHUNK)
+        span = slice(start, start + TILE)
         return jnp.concatenate([ref[2 * pair, 0, span, :], ref[2 * pair + 1, 0, span, :]], axis=1)
 
     total = arrived_ref[0].astype(F32)
@@ -104,59 +104,52 @@
             vector = vector * cosine + pltpu.roll(vector, HD // 2, 1) * sine
         queries[:, h, :] = vector.astype(BF16).astype(F32)
 
-    scale = 1.0 / math.sqrt(HD)
+    scale = math.log2(math.e) / math.sqrt(HD)
     row = lax.broadcasted_iota(jnp.int32, (2 * QG, 1), 0)
-    for pair in range(lists // 2):
+
+    def score(pair):
         first, second = queries[2 * pair], queries[2 * pair + 1]
         q_both = jnp.concatenate([first[:QG], second[:QG]], axis=0)
         blank = jnp.zeros((QG, HD), F32)
         q_wide = jnp.concatenate(
             [jnp.concatenate([first[:QG], blank], axis=1), jnp.concatenate([blank, second[:QG]], axis=1)], axis=0
         ).astype(BF16)
-        k_new = jnp.concatenate(
-            [jnp.broadcast_to(v[QG : QG + 1], (QG, HD)) for v in (first, second)], axis=0
-        )
-        v_new = jnp.concatenate(
-            [jnp.broadcast_to(v[QG + 1 : QG + 2], (QG, HD)) for v in (first, second)], axis=0
-        )
+        k_new = jnp.concatenate([jnp.broadcast_to(v[QG : QG + 1], (QG, HD)) for v in (first, second)], axis=0)
         fresh = jnp.sum(q_both * k_new, axis=1, keepdims=True) * scale
         length = jnp.where(row < QG, lengths_ref[2 * pair], lengths_ref[2 * pair + 1])
-        live_chunks = (longest[pair] + CHUNK - 1) // CHUNK
-
-        def score(chunk, peak):
-            start = pl.multiple_of(chunk * CHUNK, CHUNK)
+        peak = jnp.full((2 * QG, HD), -1e30, F32)
+        for start in range(0, slots, TILE):
             block = lax.dot_general(
                 q_wide, wide(keys, pair, start), (((1,), (1,)), ((), ())), preferred_element_type=F32
             )
-            slot = lax.broadcasted_iota(jnp.int32, (2 * QG, CHUNK), 1) + start
+            slot = lax.broadcasted_iota(jnp.int32, (2 * QG, TILE), 1) + start
             block = jnp.where(slot < length, block * scale, -1e30)
-            scores[:, pl.ds(start, CHUNK)] = block
-            for t in range(CHUNK // HD):
+            scores[pair, :, start : start + TILE] = block
+            for t in range(TILE // HD):
                 peak = jnp.maximum(peak, block[:, t * HD : (t + 1) * HD])
-            return peak
-
-        peak = lax.fori_loop(0, live_chunks, score, jnp.full((2 * QG, HD), -1e30, F32))
-        peak = jnp.maximum(jnp.max(peak, axis=1, keepdims=True), fresh)
-
-        def mix(chunk, carry):
-            mass, mixed = carry
-            start = pl.multiple_of(chunk * CHUNK, CHUNK)
-            weight = jnp.exp(scores[:, pl.ds(start, CHUNK)] - peak)
-            for t in range(CHUNK // HD):
+        return fresh, jnp.maximum(jnp.max(peak, axis=1, keepdims=True), fresh)
+
+    def mix(pair, fresh, peak):
+        mass = jnp.zeros((2 * QG, HD), F32)
+        mixed = jnp.zeros((2 * QG, 2 * HD), F32)
+        for start in range(0, slots, TILE):
+            weight = jnp.exp2(scores[pair, :, start : start + TILE] - peak)
+            for t in range(TILE // HD):
                 mass = mass + weight[:, t * HD : (t + 1) * HD]
-            mixed = mixed + jnp.dot(
-                weight.astype(BF16), wide(values, pair, start), preferred_element_type=F32
-            )
-            return mass, mixed
-
-        mass, mixed = lax.fori_loop(
-            0, live_chunks, mix, (jnp.zeros((2 * QG, HD), F32), jnp.zeros((2 * QG, 2 * HD), F32))
+            mixed = mixed + jnp.dot(weight.astype(BF16), wide(values, pair, start), preferred_element_type=F32)
+        weight_new = jnp.exp2(fresh - peak)
+        denominator = jnp.sum(mass, axis=1, keepdims=True) + weight_new
+        v_new = jnp.concatenate(
+            [jnp.broadcast_to(queries[2 * pair + j, QG + 1 : QG + 2, :], (QG, HD)) for j in range(2)], axis=0
         )
-        weight_new = jnp.exp(fresh - peak)
-        denominator = jnp.sum(mass, axis=1, keepdims=True) + weight_new
         own = jnp.concatenate([mixed[:QG, :HD], mixed[QG:, HD:]], axis=0)
         own = (own + weight_new.astype(BF16).astype(F32) * v_new) / denominator
         attended[2 * QG * pair : 2 * QG * (pair + 1), :] = own
+
+    ahead = score(0)
+    for pair in range(pairs):
+        this, ahead = ahead, score(pair + 1) if pair + 1 < pairs else None
+        mix(pair, *this)
 
     matrix = hadamard_signs()
     steered = []
@@ -222,24 +215,30 @@
         out_shape=jax.ShapeDtypeStruct((2 * rows, features + EXTRA), BF16),
         in_specs=[VMEM] * 3,
         out_specs=VMEM,
-        compiler_params=params(4),
+        compiler_params=params(2),
         cost_estimate=cost(COVER[0]),
         name="rotate_in",
-    )(hidden, across_cores(hidden), steer.reshape(1, -1))
+    )(hidden.astype(F32), across_cores(hidden), steer.reshape(1, -1))
+    rotated, lengths, sign_attn = lax.optimization_barrier((rotated, lengths, sign_attn))
+    frequency = jnp.exp(jnp.arange(HD // 2, dtype=F32) * (-2.0 * math.log(ROPE_BASE) / HD))
+    angles = lengths.astype(F32)[:, None] * frequency[None, :]
+    cosine, sine = jnp.cos(angles), jnp.sin(angles)
+    cosine = jnp.concatenate([cosine, cosine], axis=1)
+    sine = jnp.concatenate([-sine, sine], axis=1)
+    sign_out = (2 * sign_attn - 1).astype(F32).reshape(1, -1)
+    received = along_x(rotated)
+    received, cosine, sine, sign_out, lengths = lax.optimization_barrier((received, cosine, sine, sign_out, jnp.minimum(lengths, slots)))
     partial = pl.pallas_call(
         project_kernel,
         out_shape=jax.ShapeDtypeStruct((peers, own_lists, columns + EXTRA), BF16),
         in_specs=[SMEM] + [VMEM] * 5,
         out_specs=VMEM,
-        compiler_params=params(8),
+        compiler_params=params(2),
         cost_estimate=cost(COVER[1]),
         name="project",
-    )(place, rotated, *along_x(rotated), qkv_weight)
+    )(place, rotated, *received, qkv_weight)
     arrived = lax.all_to_all(partial, WIDE, split_axis=0, concat_axis=0, tiled=True)
 
-    frequency = jnp.exp(jnp.arange(HD // 2, dtype=F32) * (-2.0 * math.log(ROPE_BASE) / HD))
-    angles = lengths.astype(F32)[:, None] * frequency[None, :]
-    cosine, sine = jnp.cos(angles), jnp.sin(angles)
     sent = pl.pallas_call(
         attend_kernel,
         out_shape=jax.ShapeDtypeStruct((peers, own_lists, QG * HD), BF16),
@@ -247,18 +246,18 @@
         out_specs=VMEM,
         scratch_shapes=[
             pltpu.VMEM((own_lists, 24, HD), F32),
-            pltpu.VMEM((2 * QG, slots), F32),
+            pltpu.VMEM((own_lists // 2, 2 * QG, slots), F32),
             pltpu.VMEM((own_lists * QG, HD), F32),
         ],
-        compiler_params=params(20),
+        compiler_params=params(6),
         cost_estimate=cost(COVER[2]),
         name="attend",
     )(
-        jnp.minimum(lengths, slots),
+        lengths,
         arrived,
-        jnp.concatenate([cosine, cosine], axis=1),
-        jnp.concatenate([-sine, sine], axis=1),
-        (2 * sign_attn - 1).astype(F32).reshape(1, -1),
+        cosine,
+        sine,
+        sign_out,
         key_cache,
         value_cache,
     )
@@ -271,7 +270,7 @@
         ),
         in_specs=[SMEM, VMEM, VMEM],
         out_specs=(VMEM, VMEM),
-        compiler_params=params(8),
+        compiler_params=params(2),
         name="mix",
     )(place, gathered.reshape(4, 2, rows, QG * HD), out_weight)
     own, *sends = pl.pallas_call(
@@ -280,7 +279,7 @@
         + (jax.ShapeDtypeStruct((rows, features), BF16),) * 3,
         in_specs=[SMEM, VMEM, VMEM],
         out_specs=(VMEM,) * 4,
-        compiler_params=params(4),
+        compiler_params=params(2),
         name="pair_sum",
     )(place, keep, across_cores(send))
     got = [
@@ -291,7 +290,7 @@
         out_shape=jax.ShapeDtypeStruct((rows, features), BF16),
         in_specs=[VMEM] * 5,
         out_specs=VMEM,
-        compiler_params=params(4),
+        compiler_params=params(2),
         name="last",
     )(hidden, own, *got)
 

time: 74.6 us -> 64 us (0.86)
  blocking collectives: 15 us -> 34.4 us
  starting transfers between devices: 19 us -> 7.94 us
  waiting for transfers between devices: 17.6 us -> 10 us
  local copies, waits for them, and re-layouts: 7.54 us -> 0.05 us
  Pallas kernels: 12.9 us -> 9.3 us
    all_to_all x0 -> x1, blocking collectives: none -> 20.7 us  [body(): lax.all_to_all(partial, WIDE, split_axis=0, concat_axis=0, tiled=True)]
    all_to_all x1 -> x0, waiting for transfers between devices: 11.8 us -> none  [body(): lax.all_to_all(partial, WIDE, split_axis=0, concat_axis=0, tiled=True)]
    all_to_all x1 -> x0, starting transfers between devices: 8.05 us -> none  [body(): lax.all_to_all(partial, WIDE, split_axis=0, concat_axis=0, tiled=True)]
    unnamed x14 -> x18, local copies, waits for them, and re-layouts: 7.54 us -> 0.05 us
    ppermute x3, waiting for transfers between devices: 2.84 us -> 5.58 us  [along_x(): lax.ppermute(value, 'x', [(i, (i + s) % 4) for i in range(4)])]
    pallas_call x1, Pallas kernels: 7.8 us -> 5.08 us  [body(): pl.pallas_call(attend_kernel, out_shape=jax.ShapeDtypeStruct((peers, own_...]
    ppermute x3, starting transfers between devices: 5.11 us -> 3.3 us  [body(): lax.ppermute(v, 'x', [(i, (i + s) % 4) for i in range(4)])]
    ppermute x3, waiting for transfers between devices: 1.6 us -> 3.09 us  [body(): lax.ppermute(v, 'x', [(i, (i + s) % 4) for i in range(4)])]
  transfers between devices with their start and end apart: 9 -> 8, of which waited for: 7 -> 7; matrix products, arithmetic and copies ran while one was open for 2% -> 3% of each run, Pallas kernels for 0% -> 0%
where the time goes in v3:
time: 64 us; the launch traced here: 63.7 us
  blocking collectives  34.4 us (54%)
  waiting for transfers between devices  10 us (16%)
  Pallas kernels  9.3 us (15%)
  starting transfers between devices  7.94 us (12%)
  other arithmetic  1.75 us (3%)
    all_to_all x1, blocking collectives, body(): lax.all_to_all(partial, WIDE, split_axis=0, concat_axis=0, tiled=True)  20.7 us
    all_to_all x1, blocking collectives, body(): lax.all_to_all(sent, WIDE, split_axis=0, concat_axis=0, tiled=True)  13.8 us
    ppermute x3, waiting for transfers between devices, along_x(): lax.ppermute(value, 'x', [(i, (i + s) % 4) for i in range(4)])  5.58 us
    pallas_call x1, Pallas kernels, body(): pl.pallas_call(attend_kernel, out_shape=jax.ShapeDtypeStruct((peers, own_...  5.08 us
    ppermute x3, starting transfers between devices, along_x(): lax.ppermute(value, 'x', [(i, (i + s) % 4) for i in range(4)])  4.55 us
    ppermute x3, starting transfers between devices, body(): lax.ppermute(v, 'x', [(i, (i + s) % 4) for i in range(4)])  3.3 us
    ppermute x3, waiting for transfers between devices, body(): lax.ppermute(v, 'x', [(i, (i + s) % 4) for i in range(4)])  3.09 us
    pallas_call x1, Pallas kernels, body(): pl.pallas_call(project_kernel, out_shape=jax.ShapeDtypeStruct((peers, own...  1.35 us
  transfers between devices with their start and end apart: 8, of which 7 were waited for; matrix products, arithmetic and copies ran while one was open for 3% of the time, Pallas kernels for 0%

profile of v3, /device:TPU:0, one launch (start us, length us, event | category | flops | bytes accessed | tf_op | source)
XLA Modules:
  0.0 63.7 jit_solution(3700076712196790254)
XLA Ops:
  0.0 0.0 collective-permute-start
  0.0 0.7 %convert_multiply_fusion = f32[1024]{0:T(1024)S(1)} fusion(s32[1024]{0:T(1024)} %param.11, bf16[1024]{0:T(1024)(128)(2,1)} %param.10), kind=kLoop, calls=%fused_computation.5 | loop fusion | flops 5120 | bytes 10240 | tf_op jit(solution)/shard_map/mul | solution.py:212
  0.7 0.1 pad_add_fusion.place_ref
  0.8 0.8 %convert_element_type.15.own_ref = f32[16,1024]{1,0:T(8,128)S(1)} convert(bf16[16,1024]{1,0:T(8,128)(2,1)} %hidden_ref.1) | non-fusion elementwise | flops 16384 | bytes 98304 | tf_op jit(solution)/shard_map/convert_element_type | solution.py:221
  1.6 0.0 collective-permute-done.other_ref
  1.6 0.0 copy-start.4
  1.6 0.0 copy-start.3
  1.6 0.0 copy-start.2
  1.6 0.0 slice-start
  1.6 0.0 slice-start.2
  1.6 0.4 rotate_in.1.x0
  2.0 2.9 %collective-permute-start.3 = (bf16[32,1152]{1,0:T(8,128)(2,1)S(1)}, bf16[32,1152]{1,0:T(8,128)(2,1)S(1)}, u32[]{:S(2)}, u32[]{:S(2)}) collective-permute-start(bf16[32,1152]{1,0:T(8,128)(2,1)S(1)} %rotate_in.1.x0), channel_id=1, source_target_pairs={{0,6},{2,0},{4,2},{6,4},{1,7},{3,1},{5,3},{7,5},{8,14},{10,8},{12,... | collective-permute-start | bytes 221192 | tf_op jit(solution)/shard_map/ppermute | solution.py:198
  4.9 0.8 %collective-permute-start.2 = (bf16[32,1152]{1,0:T(8,128)(2,1)S(1)}, bf16[32,1152]{1,0:T(8,128)(2,1)S(1)}, u32[]{:S(2)}, u32[]{:S(2)}) collective-permute-start(bf16[32,1152]{1,0:T(8,128)(2,1)S(1)} %rotate_in.1.x0), channel_id=1, source_target_pairs={{0,4},{2,6},{4,0},{6,2},{1,5},{3,7},{5,1},{7,3},{8,12},{10,14},{12... | collective-permute-start | bytes 221192 | tf_op jit(solution)/shard_map/ppermute | solution.py:198
  5.7 0.9 %collective-permute-start.1 = (bf16[32,1152]{1,0:T(8,128)(2,1)S(1)}, bf16[32,1152]{1,0:T(8,128)(2,1)S(1)}, u32[]{:S(2)}, u32[]{:S(2)}) collective-permute-start(bf16[32,1152]{1,0:T(8,128)(2,1)S(1)} %rotate_in.1.x0), channel_id=1, source_target_pairs={{0,2},{2,4},{4,6},{6,0},{1,3},{3,5},{5,7},{7,1},{8,10},{10,12},{12... | collective-permute-start | bytes 221192 | tf_op jit(solution)/shard_map/ppermute | solution.py:198
  6.6 0.0 copy-done.4
  6.6 0.0 copy-done.3
  6.6 0.1 fusion
  6.7 0.1 pad_maximum_fusion
  6.8 1.9 %collective-permute-done.3.x3 = bf16[32,1152]{1,0:T(8,128)(2,1)S(1)} collective-permute-done((bf16[32,1152]{1,0:T(8,128)(2,1)S(1)}, bf16[32,1152]{1,0:T(8,128)(2,1)S(1)}, u32[]{:S(2)}, u32[]{:S(2)}) %collective-permute-start.3) | collective-permute-done | bytes 73760 | tf_op jit(solution)/shard_map/ppermute | solution.py:198
  8.7 2.8 %collective-permute-done.2.x2 = bf16[32,1152]{1,0:T(8,128)(2,1)S(1)} collective-permute-done((bf16[32,1152]{1,0:T(8,128)(2,1)S(1)}, bf16[32,1152]{1,0:T(8,128)(2,1)S(1)}, u32[]{:S(2)}, u32[]{:S(2)}) %collective-permute-start.2) | collective-permute-done | bytes 73760 | tf_op jit(solution)/shard_map/ppermute | solution.py:198
  11.5 0.9 %collective-permute-done.1.x1 = bf16[32,1152]{1,0:T(8,128)(2,1)S(1)} collective-permute-done((bf16[32,1152]{1,0:T(8,128)(2,1)S(1)}, bf16[32,1152]{1,0:T(8,128)(2,1)S(1)}, u32[]{:S(2)}, u32[]{:S(2)}) %collective-permute-start.1) | collective-permute-done | bytes 73760 | tf_op jit(solution)/shard_map/ppermute | solution.py:198
  12.4 0.0 copy-done.2
  12.4 0.0 slice-start.1
  12.4 0.0 slice-start.3
  12.4 1.4 %project.1 = bf16[16,8,2432]{2,1,0:T(8,128)(2,1)S(1)} custom-call(s32[2]{0:T(128)S(1)} %pad_add_fusion.place_ref, bf16[32,1152]{1,0:T(8,128)(2,1)S(1)} %rotate_in.1.x0, bf16[32,1152]{1,0:T(8,128)(2,1)S(1)} %collective-permute-done.1.x1, bf16[32,1152]{1,0:T(8,128)(2,1)S(1)} %collective-permute-done.2.x2, bf16[32,1152]{1,0:T(8,128)(2,1)S(1)} %collective-permute-done.3.x3, ...), custom_call_target="tpu_custom_call" | custom-call | flops 11000000512 | bytes 30000000 | tf_op jit(solution)/shard_map/project/pallas_call | solution.py:231
  13.7 20.7 %all_to_all.10.arrived_ref = bf16[16,8,2432]{2,1,0:T(8,128)(2,1)S(1)} all-to-all(bf16[16,8,2432]{2,1,0:T(8,128)(2,1)S(1)} %project.1), channel_id=1, replica_groups=mesh['y'=4,'z'=4,'x'=4,'core'=2] {'y','z'}, dimensions={0} | all-to-all | bytes 1245184 | tf_op jit(solution)/shard_map/all_to_all | solution.py:240
  34.4 0.0 slice-done
  34.4 0.0 slice-done.2
  34.4 0.0 slice-done.1
  34.4 0.0 slice-done.3
  34.5 0.0 copy-start
  34.5 0.0 copy-start.1
  34.5 5.1 %attend.1 = bf16[16,8,2048]{2,1,0:T(8,128)(2,1)S(1)} custom-call(s32[8]{0:T(128)S(1)} %get-tuple-element.24.lengths_ref, bf16[16,8,2432]{2,1,0:T(8,128)(2,1)S(1)} %all_to_all.10.arrived_ref, f32[8,128]{1,0:T(8,128)S(1)} %get-tuple-element.28.cos_ref, f32[8,128]{1,0:T(8,128)S(1)} %get-tuple-element.29.sin_ref, f32[1,2048]{1,0:T(1,128)S(1)} %bitcast.6, ...), custom_call_target="tpu_custom_call" | custom-call | flops 11000000512 | bytes 30000000 | tf_op jit(solution)/shard_map/attend/pallas_call | solution.py:242
  39.6 13.8 %all_to_all.11 = bf16[16,8,2048]{2,1,0:T(8,128)(2,1)S(1)} all-to-all(bf16[16,8,2048]{2,1,0:T(8,128)(2,1)S(1)} %attend.1), channel_id=1, replica_groups=mesh['y'=4,'z'=4,'x'=4,'core'=2] {'y','z'}, dimensions={0} | all-to-all | bytes 1048576 | tf_op jit(solution)/shard_map/all_to_all | solution.py:264
  53.3 0.0 copy-done
  53.3 1.3 %mix.1 = (f32[4,16,1024]{2,1,0:T(8,128)S(1)}, bf16[4,16,1024]{2,1,0:T(8,128)(2,1)S(1)}) custom-call(s32[2]{0:T(128)S(1)} %pad_add_fusion.place_ref, bf16[4,2,16,2048]{3,2,1,0:T(8,128)(2,1)S(1)} %bitcast.5, bf16[2048,1024]{1,0:T(8,128)(2,1)S(1)} %copy-done), custom_call_target="tpu_custom_call" | custom-call | tf_op jit(solution)/shard_map/mix/pallas_call | solution.py:265
  54.6 0.1 collective-permute-start.4
  54.7 1.3 %collective-permute-done.4.got_ref = bf16[4,16,1024]{2,1,0:T(8,128)(2,1)S(1)} collective-permute-done((bf16[4,16,1024]{2,1,0:T(8,128)(2,1)S(1)}, bf16[4,16,1024]{2,1,0:T(8,128)(2,1)S(1)}, u32[]{:S(2)}, u32[]{:S(2)}) %collective-permute-start.4) | collective-permute-done | bytes 131104 | tf_op jit(solution)/shard_map/ppermute | solution.py:202
  56.0 0.6 pair_sum.1
  56.6 0.1 collective-permute-start.5
  56.7 1.1 %collective-permute-start.6 = (bf16[16,1024]{1,0:T(8,128)(2,1)S(1)}, bf16[16,1024]{1,0:T(8,128)(2,1)S(1)}, u32[]{:S(2)}, u32[]{:S(2)}) collective-permute-start(bf16[16,1024]{1,0:T(8,128)(2,1)S(1)} %get-tuple-element.35), channel_id=1, source_target_pairs={{0,4},{2,6},{4,0},{6,2},{1,5},{3,7},{5,1},{7,3},{8,12},{10,14},{12... | collective-permute-start | bytes 98312 | tf_op jit(solution)/shard_map/ppermute | solution.py:286
  57.8 2.1 %collective-permute-start.7 = (bf16[16,1024]{1,0:T(8,128)(2,1)S(1)}, bf16[16,1024]{1,0:T(8,128)(2,1)S(1)}, u32[]{:S(2)}, u32[]{:S(2)}) collective-permute-start(bf16[16,1024]{1,0:T(8,128)(2,1)S(1)} %get-tuple-element.36), channel_id=1, source_target_pairs={{0,6},{2,0},{4,2},{6,4},{1,7},{3,1},{5,3},{7,5},{8,14},{10,8},{12,... | collective-permute-start | bytes 98312 | tf_op jit(solution)/shard_map/ppermute | solution.py:286
  59.9 1.9 %collective-permute-done.5.r1 = bf16[16,1024]{1,0:T(8,128)(2,1)S(1)} collective-permute-done((bf16[16,1024]{1,0:T(8,128)(2,1)S(1)}, bf16[16,1024]{1,0:T(8,128)(2,1)S(1)}, u32[]{:S(2)}, u32[]{:S(2)}) %collective-permute-start.5) | collective-permute-done | bytes 32800 | tf_op jit(solution)/shard_map/ppermute | solution.py:286
  61.8 0.4 collective-permute-done.6.r2
  62.2 0.8 %collective-permute-done.7.r3 = bf16[16,1024]{1,0:T(8,128)(2,1)S(1)} collective-permute-done((bf16[16,1024]{1,0:T(8,128)(2,1)S(1)}, bf16[16,1024]{1,0:T(8,128)(2,1)S(1)}, u32[]{:S(2)}, u32[]{:S(2)}) %collective-permute-start.7) | collective-permute-done | bytes 32800 | tf_op jit(solution)/shard_map/ppermute | solution.py:286
  63.0 0.0 copy-done.1
  63.0 0.6 %last.1 = bf16[16,1024]{1,0:T(8,128)(2,1)} custom-call(bf16[16,1024]{1,0:T(8,128)(2,1)S(1)} %copy-done.1, f32[16,1024]{1,0:T(8,128)S(1)} %get-tuple-element.33.own_ref, bf16[16,1024]{1,0:T(8,128)(2,1)S(1)} %collective-permute-done.5.r1, bf16[16,1024]{1,0:T(8,128)(2,1)S(1)} %collective-permute-done.6.r2, bf16[16,1024]{1,0:T(8,128)(2,1)S(1)} %collective-permute-done.7.r3), custom_call_target="tpu_custom_call" | custom-call | tf_op jit(solution)/shard_map/last/pallas_call | solution.py:288
  (5 shorter events, 0.0 us)
Async XLA Ops:
  0.0 1.6 %collective-permute-start = (bf16[16,1024]{1,0:T(8,128)(2,1)}, bf16[16,1024]{1,0:T(8,128)(2,1)S(1)}, u32[]{:S(2)}, u32[]{:S(2)}) collective-permute-start(bf16[16,1024]{1,0:T(8,128)(2,1)} %hidden_ref.1), channel_id=1, source_target_pairs={{0,1},{1,0},{2,3},{3,2},{4,5},{5,4},{6,7},{7,6},{8,9},{9,8},{10,11... | collective-permute-start | bytes 98312 | tf_op jit(solution)/shard_map/ppermute | solution.py:202
  1.6 5.0 %copy-start.4 = (s32[8]{0:T(128)S(1)}, s32[8]{0:T(128)}, u32[]{:S(2)}) copy-start(s32[8]{0:T(128)} %param.17) | copy-start | bytes 100
  1.6 5.0 %copy-start.3 = (s32[2048]{0:T(1024)S(1)}, s32[2048]{0:T(1024)}, u32[]{:S(2)}) copy-start(s32[2048]{0:T(1024)} %param.14) | copy-start | bytes 24580
  1.6 10.8 %copy-start.2 = (bf16[1024,2304]{1,0:T(8,128)(2,1)S(1)}, bf16[1024,2304]{1,0:T(8,128)(2,1)}, u32[]{:S(2)}) copy-start(bf16[1024,2304]{1,0:T(8,128)(2,1)} %weight.2) | copy-start | bytes 14155780
  1.6 32.8 %slice-start = ((s8[8388608]{0:T(1024)(128)(4,1)}), s8[4194304]{0:T(1024)(128)(4,1)S(1)}, s32[]{:S(2)}) async-start(s8[8388608]{0:T(1024)(128)(4,1)} %bitcast.8), calls=%async_computation.2 | async-start | bytes 8388608
  1.6 32.8 %slice-start.2 = ((s8[8388608]{0:T(1024)(128)(4,1)}), s8[4194304]{0:T(1024)(128)(4,1)S(1)}, s32[]{:S(2)}) async-start(s8[8388608]{0:T(1024)(128)(4,1)} %bitcast.10), calls=%async_computation.4 | async-start | bytes 8388608
  2.0 6.7 %collective-permute-start.3 = (bf16[32,1152]{1,0:T(8,128)(2,1)S(1)}, bf16[32,1152]{1,0:T(8,128)(2,1)S(1)}, u32[]{:S(2)}, u32[]{:S(2)}) collective-permute-start(bf16[32,1152]{1,0:T(8,128)(2,1)S(1)} %rotate_in.1.x0), channel_id=1, source_target_pairs={{0,6},{2,0},{4,2},{6,4},{1,7},{3,1},{5,3},{7,5},{8,14},{10,8},{12,... | collective-permute-start | bytes 221192 | tf_op jit(solution)/shard_map/ppermute | solution.py:198
  4.9 6.6 %collective-permute-start.2 = (bf16[32,1152]{1,0:T(8,128)(2,1)S(1)}, bf16[32,1152]{1,0:T(8,128)(2,1)S(1)}, u32[]{:S(2)}, u32[]{:S(2)}) collective-permute-start(bf16[32,1152]{1,0:T(8,128)(2,1)S(1)} %rotate_in.1.x0), channel_id=1, source_target_pairs={{0,4},{2,6},{4,0},{6,2},{1,5},{3,7},{5,1},{7,3},{8,12},{10,14},{12... | collective-permute-start | bytes 221192 | tf_op jit(solution)/shard_map/ppermute | solution.py:198
  5.7 6.7 %collective-permute-start.1 = (bf16[32,1152]{1,0:T(8,128)(2,1)S(1)}, bf16[32,1152]{1,0:T(8,128)(2,1)S(1)}, u32[]{:S(2)}, u32[]{:S(2)}) collective-permute-start(bf16[32,1152]{1,0:T(8,128)(2,1)S(1)} %rotate_in.1.x0), channel_id=1, source_target_pairs={{0,2},{2,4},{4,6},{6,0},{1,3},{3,5},{5,7},{7,1},{8,10},{10,12},{12... | collective-permute-start | bytes 221192 | tf_op jit(solution)/shard_map/ppermute | solution.py:198
  12.4 22.1 %slice-start.1 = ((s8[8388608]{0:T(1024)(128)(4,1)}), s8[4194304]{0:T(1024)(128)(4,1)S(1)}, s32[]{:S(2)}) async-start(s8[8388608]{0:T(1024)(128)(4,1)} %bitcast.8), calls=%async_computation.3 | async-start | bytes 8388608
  12.4 22.1 %slice-start.3 = ((s8[8388608]{0:T(1024)(128)(4,1)}), s8[4194304]{0:T(1024)(128)(4,1)S(1)}, s32[]{:S(2)}) async-start(s8[8388608]{0:T(1024)(128)(4,1)} %bitcast.10), calls=%async_computation.5 | async-start | bytes 8388608
  34.5 18.9 %copy-start = (bf16[2048,1024]{1,0:T(8,128)(2,1)S(1)}, bf16[2048,1024]{1,0:T(8,128)(2,1)}, u32[]{:S(2)}) copy-start(bf16[2048,1024]{1,0:T(8,128)(2,1)} %weight.3) | copy-start | bytes 12582916
  34.5 28.6 %copy-start.1 = (bf16[16,1024]{1,0:T(8,128)(2,1)S(1)}, bf16[16,1024]{1,0:T(8,128)(2,1)}, u32[]{:S(2)}) copy-start(bf16[16,1024]{1,0:T(8,128)(2,1)} %hidden_ref.1) | copy-start | bytes 98308
  54.6 1.4 %collective-permute-start.4 = (bf16[4,16,1024]{2,1,0:T(8,128)(2,1)S(1)}, bf16[4,16,1024]{2,1,0:T(8,128)(2,1)S(1)}, u32[]{:S(2)}, u32[]{:S(2)}) collective-permute-start(bf16[4,16,1024]{2,1,0:T(8,128)(2,1)S(1)} %get-tuple-element.32), channel_id=1, source_target_pairs={{0,1},{1,0},{2,3},{3,2},{4,5},{5,4},{6,7},{7,6},{8,9},{9,8},{10,11... | collective-permute-start | bytes 393224 | tf_op jit(solution)/shard_map/ppermute | solution.py:202
  56.6 5.2 %collective-permute-start.5 = (bf16[16,1024]{1,0:T(8,128)(2,1)S(1)}, bf16[16,1024]{1,0:T(8,128)(2,1)S(1)}, u32[]{:S(2)}, u32[]{:S(2)}) collective-permute-start(bf16[16,1024]{1,0:T(8,128)(2,1)S(1)} %get-tuple-element.34), channel_id=1, source_target_pairs={{0,2},{2,4},{4,6},{6,0},{1,3},{3,5},{5,7},{7,1},{8,10},{10,12},{12... | collective-permute-start | bytes 98312 | tf_op jit(solution)/shard_map/ppermute | solution.py:286
  56.7 5.5 %collective-permute-start.6 = (bf16[16,1024]{1,0:T(8,128)(2,1)S(1)}, bf16[16,1024]{1,0:T(8,128)(2,1)S(1)}, u32[]{:S(2)}, u32[]{:S(2)}) collective-permute-start(bf16[16,1024]{1,0:T(8,128)(2,1)S(1)} %get-tuple-element.35), channel_id=1, source_target_pairs={{0,4},{2,6},{4,0},{6,2},{1,5},{3,7},{5,1},{7,3},{8,12},{10,14},{12... | collective-permute-start | bytes 98312 | tf_op jit(solution)/shard_map/ppermute | solution.py:286
  57.8 5.2 %collective-permute-start.7 = (bf16[16,1024]{1,0:T(8,128)(2,1)S(1)}, bf16[16,1024]{1,0:T(8,128)(2,1)S(1)}, u32[]{:S(2)}, u32[]{:S(2)}) collective-permute-start(bf16[16,1024]{1,0:T(8,128)(2,1)S(1)} %get-tuple-element.36), channel_id=1, source_target_pairs={{0,6},{2,0},{4,2},{6,4},{1,7},{3,1},{5,3},{7,5},{8,14},{10,8},{12,... | collective-permute-start | bytes 98312 | tf_op jit(solution)/shard_map/ppermute | solution.py:286

commit v4 on v3

--- a/solution.py
+++ b/solution.py
@@ -16,7 +16,6 @@
 EXTRA = 128
 MIB = 1 << 20
 VMEM = pl.BlockSpec(memory_space=pltpu.VMEM)
-SMEM = pl.BlockSpec(memory_space=pltpu.SMEM)
 HBM = pl.BlockSpec(memory_space=pl.ANY)
 F32 = jnp.float32
 BF16 = jnp.bfloat16
@@ -55,16 +54,16 @@
             out_ref[16 * at : 16 * at + 16, b * HD : (b + 1) * HD] = turned.astype(BF16)
 
 
-def project_kernel(place_ref, x0, x1, x2, x3, weight, out_ref):
+def project_kernel(x0, x1, x2, x3, weight, out_ref):
     parts, width = 3, weight.shape[1] // 3
     features = weight.shape[0]
-    x, c = place_ref[0], place_ref[1]
+    x, c = lax.axis_index("x"), lax.axis_index("core")
     received = (x0, x1, x2, x3)
     targets = []
     for s in range(4):
         for other in range(2):
             core = c if other == 0 else 1 - c
-            source = 2 * ((x - s) & 3) + core
+            source = 2 * (x ^ s) + core
             targets += [2 * source, 2 * source + 1]
     for s in range(4):
         extra = received[s][:, features:].astype(F32)
@@ -77,7 +76,7 @@
             out_ref[targets[j], :, i * width : (i + 1) * width] = product[8 * j : 8 * j + 8].astype(BF16)
 
 
-COVER = (10, 10, 10)
+COVER = (30, 1, 10)
 TILE = 512
 
 
@@ -105,7 +104,7 @@
         queries[:, h, :] = vector.astype(BF16).astype(F32)
 
     scale = math.log2(math.e) / math.sqrt(HD)
-    row = lax.broadcasted_iota(jnp.int32, (2 * QG, 1), 0)
+    lane = lax.broadcasted_iota(jnp.int32, (2 * QG, HD), 1)
 
     def score(pair):
         first, second = queries[2 * pair], queries[2 * pair + 1]
@@ -116,17 +115,19 @@
         ).astype(BF16)
         k_new = jnp.concatenate([jnp.broadcast_to(v[QG : QG + 1], (QG, HD)) for v in (first, second)], axis=0)
         fresh = jnp.sum(q_both * k_new, axis=1, keepdims=True) * scale
-        length = jnp.where(row < QG, lengths_ref[2 * pair], lengths_ref[2 * pair + 1])
+        length = jnp.concatenate(
+            [jnp.broadcast_to(lengths_ref[2 * pair + j : 2 * pair + j + 1, :], (QG, HD)) for j in range(2)], axis=0
+        )
         peak = jnp.full((2 * QG, HD), -1e30, F32)
         for start in range(0, slots, TILE):
             block = lax.dot_general(
                 q_wide, wide(keys, pair, start), (((1,), (1,)), ((), ())), preferred_element_type=F32
             )
-            slot = lax.broadcasted_iota(jnp.int32, (2 * QG, TILE), 1) + start
-            block = jnp.where(slot < length, block * scale, -1e30)
-            scores[pair, :, start : start + TILE] = block
             for t in range(TILE // HD):
-                peak = jnp.maximum(peak, block[:, t * HD : (t + 1) * HD])
+                at = start + t * HD
+                piece = jnp.where(lane < length - at, block[:, t * HD : (t + 1) * HD] * scale, -1e30)
+                scores[pair, :, at : at + HD] = piece
+                peak = jnp.maximum(peak, piece)
         return fresh, jnp.maximum(jnp.max(peak, axis=1, keepdims=True), fresh)
 
     def mix(pair, fresh, peak):
@@ -162,9 +163,9 @@
             out_ref[w, :, h * HD : (h + 1) * HD] = piece
 
 
-def mix_kernel(place_ref, rows_ref, weight, keep_ref, send_ref):
+def mix_kernel(rows_ref, weight, keep_ref, send_ref):
     parts, width = 4, weight.shape[1] // 4
-    c = place_ref[1]
+    c = lax.axis_index("core")
     rows = jnp.concatenate([rows_ref[x, c] for x in range(4)] + [rows_ref[x, 1 - c] for x in range(4)], axis=0)
     for i in range(parts):
         product = jnp.dot(rows, weight[:, i * width : (i + 1) * width], preferred_element_type=F32)
@@ -173,11 +174,11 @@
             send_ref[x, :, i * width : (i + 1) * width] = product[64 + 16 * x : 80 + 16 * x].astype(BF16)
 
 
-def pair_sum_kernel(place_ref, keep_ref, got_ref, own_ref, s1, s2, s3):
-    x = place_ref[0]
+def pair_sum_kernel(keep_ref, got_ref, own_ref, s1, s2, s3):
+    x = lax.axis_index("x")
     own_ref[...] = keep_ref[x] + got_ref[x].astype(F32)
     for s, ref in ((1, s1), (2, s2), (3, s3)):
-        to = (x + s) & 3
+        to = x ^ s
         ref[...] = (keep_ref[to] + got_ref[to].astype(F32)).astype(BF16)
 
 
@@ -194,8 +195,8 @@
     return pl.CostEstimate(flops=int(microseconds * 1.1e9), transcendentals=0, bytes_accessed=int(microseconds * 3e6))
 
 
-def along_x(value):
-    return [lax.ppermute(value, "x", [(i, (i + s) % 4) for i in range(4)]) for s in (1, 2, 3)]
+def along_x(values):
+    return [lax.ppermute(v, "x", [(i, i ^ s) for i in range(4)]) for s, v in zip((1, 2, 3), values)]
 
 
 def across_cores(value):
@@ -207,7 +208,6 @@
     columns = qkv_weight.shape[1]
     own_lists, _, slots, _ = key_cache.shape
     peers = lax.axis_size(WIDE)
-    place = jnp.stack([lax.axis_index("x"), lax.axis_index("core")]).astype(jnp.int32)
 
     steer = gain.astype(F32) * (2 * sign_in - 1).astype(F32)
     rotated = pl.pallas_call(
@@ -226,23 +226,23 @@
     cosine = jnp.concatenate([cosine, cosine], axis=1)
     sine = jnp.concatenate([-sine, sine], axis=1)
     sign_out = (2 * sign_attn - 1).astype(F32).reshape(1, -1)
-    received = along_x(rotated)
-    received, cosine, sine, sign_out, lengths = lax.optimization_barrier((received, cosine, sine, sign_out, jnp.minimum(lengths, slots)))
+    received = along_x([rotated] * 3)
+    received, cosine, sine, sign_out, lengths = lax.optimization_barrier((received, cosine, sine, sign_out, jnp.broadcast_to(lengths[:, None], (own_lists, HD))))
     partial = pl.pallas_call(
         project_kernel,
         out_shape=jax.ShapeDtypeStruct((peers, own_lists, columns + EXTRA), BF16),
-        in_specs=[SMEM] + [VMEM] * 5,
+        in_specs=[VMEM] * 5,
         out_specs=VMEM,
         compiler_params=params(2),
         cost_estimate=cost(COVER[1]),
         name="project",
-    )(place, rotated, *received, qkv_weight)
+    )(rotated, *received, qkv_weight)
     arrived = lax.all_to_all(partial, WIDE, split_axis=0, concat_axis=0, tiled=True)
 
     sent = pl.pallas_call(
         attend_kernel,
         out_shape=jax.ShapeDtypeStruct((peers, own_lists, QG * HD), BF16),
-        in_specs=[SMEM] + [VMEM] * 6,
+        in_specs=[VMEM] * 7,
         out_specs=VMEM,
         scratch_shapes=[
             pltpu.VMEM((own_lists, 24, HD), F32),
@@ -268,23 +268,21 @@
             jax.ShapeDtypeStruct((4, rows, features), F32),
             jax.ShapeDtypeStruct((4, rows, features), BF16),
         ),
-        in_specs=[SMEM, VMEM, VMEM],
+        in_specs=[VMEM, VMEM],
         out_specs=(VMEM, VMEM),
         compiler_params=params(2),
         name="mix",
-    )(place, gathered.reshape(4, 2, rows, QG * HD), out_weight)
+    )(gathered.reshape(4, 2, rows, QG * HD), out_weight)
     own, *sends = pl.pallas_call(
         pair_sum_kernel,
         out_shape=(jax.ShapeDtypeStruct((rows, features), F32),)
         + (jax.ShapeDtypeStruct((rows, features), BF16),) * 3,
-        in_specs=[SMEM, VMEM, VMEM],
+        in_specs=[VMEM, VMEM],
         out_specs=(VMEM,) * 4,
         compiler_params=params(2),
         name="pair_sum",
-    )(place, keep, across_cores(send))
-    got = [
-        lax.ppermute(v, "x", [(i, (i + s) % 4) for i in range(4)]) for s, v in zip((1, 2, 3), sends)
-    ]
+    )(keep, across_cores(send))
+    got = along_x(sends)
     return pl.pallas_call(
         last_kernel,
         out_shape=jax.ShapeDtypeStruct((rows, features), BF16),

time: 64 us -> 61.4 us (0.959)
  Pallas kernels: 9.3 us -> 7.17 us
  blocking collectives: 34.4 us -> 32.6 us
  starting transfers between devices: 7.94 us -> 8.99 us
    all_to_all x1, blocking collectives: 20.7 us -> 19.2 us  [body(): lax.all_to_all(partial, WIDE, split_axis=0, concat_axis=0, tiled=True)]
    ppermute x6, starting transfers between devices: 7.85 us -> 8.9 us  [along_x(): lax.ppermute(v, 'x', [(i, i ^ s) for i in range(4)])]
  transfers between devices with their start and end apart: 8 -> 8, of which waited for: 7 -> 5; matrix products, arithmetic and copies ran while one was open for 3% -> 3% of each run, Pallas kernels for 0% -> 0%
where the time goes in v4:
time: 61.4 us; the launch traced here: 61.2 us
  blocking collectives  32.6 us (53%)
  waiting for transfers between devices  10.5 us (17%)
  starting transfers between devices  8.99 us (15%)
  Pallas kernels  7.17 us (12%)
  other arithmetic  1.68 us (3%)
    all_to_all x1, blocking collectives, body(): lax.all_to_all(partial, WIDE, split_axis=0, concat_axis=0, tiled=True)  19.2 us
    all_to_all x1, blocking collectives, body(): lax.all_to_all(sent, WIDE, split_axis=0, concat_axis=0, tiled=True)  13.4 us
    ppermute x6, waiting for transfers between devices, along_x(): lax.ppermute(v, 'x', [(i, i ^ s) for i in range(4)])  9.18 us
    ppermute x6, starting transfers between devices, along_x(): lax.ppermute(v, 'x', [(i, i ^ s) for i in range(4)])  8.9 us
    pallas_call x1, Pallas kernels, body(): pl.pallas_call(attend_kernel, out_shape=jax.ShapeDtypeStruct((peers, own_...  4.55 us
    ppermute x2, waiting for transfers between devices, across_cores(): return lax.ppermute(value, 'core', [(0, 1), (1, 0)])  1.34 us
  transfers between devices with their start and end apart: 8, of which 5 were waited for; matrix products, arithmetic and copies ran while one was open for 3% of the time, Pallas kernels for 0%

profile of v4, /device:TPU:0, one launch (start us, length us, event | category | flops | bytes accessed | tf_op | source)
XLA Modules:
  0.0 61.2 jit_solution(10958216867072291536)
XLA Ops:
  0.0 0.0 collective-permute-start
  0.0 0.7 %convert_multiply_fusion = f32[1024]{0:T(1024)S(1)} fusion(s32[1024]{0:T(1024)} %param.11, bf16[1024]{0:T(1024)(128)(2,1)} %param.10), kind=kLoop, calls=%fused_computation.5 | loop fusion | flops 5120 | bytes 10240 | tf_op jit(solution)/shard_map/mul | solution.py:212
  0.7 0.8 %convert_element_type.15.own_ref = f32[16,1024]{1,0:T(8,128)S(1)} convert(bf16[16,1024]{1,0:T(8,128)(2,1)} %hidden_ref.1) | non-fusion elementwise | flops 16384 | bytes 98304 | tf_op jit(solution)/shard_map/convert_element_type | solution.py:221
  1.5 0.0 collective-permute-done.other_ref
  1.5 0.0 copy-start.6
  1.5 0.0 copy-start.5
  1.5 0.0 copy-start
  1.5 0.0 copy-start.3
  1.5 0.0 copy-start.4
  1.6 0.4 rotate_in.1.x0
  1.9 2.9 %collective-permute-start.3 = (bf16[32,1152]{1,0:T(8,128)(2,1)S(1)}, bf16[32,1152]{1,0:T(8,128)(2,1)S(1)}, u32[]{:S(2)}, u32[]{:S(2)}) collective-permute-start(bf16[32,1152]{1,0:T(8,128)(2,1)S(1)} %rotate_in.1.x0), channel_id=1, source_target_pairs={{0,6},{2,4},{4,2},{6,0},{1,7},{3,5},{5,3},{7,1},{8,14},{10,12},{12... | collective-permute-start | bytes 221192 | tf_op jit(solution)/shard_map/ppermute | solution.py:199
  4.8 0.8 %collective-permute-start.2 = (bf16[32,1152]{1,0:T(8,128)(2,1)S(1)}, bf16[32,1152]{1,0:T(8,128)(2,1)S(1)}, u32[]{:S(2)}, u32[]{:S(2)}) collective-permute-start(bf16[32,1152]{1,0:T(8,128)(2,1)S(1)} %rotate_in.1.x0), channel_id=1, source_target_pairs={{0,4},{2,6},{4,0},{6,2},{1,5},{3,7},{5,1},{7,3},{8,12},{10,14},{12... | collective-permute-start | bytes 221192 | tf_op jit(solution)/shard_map/ppermute | solution.py:199
  5.6 0.5 collective-permute-start.1
  6.1 0.0 copy-done.6
  6.1 0.0 copy-done.5
  6.1 0.1 fusion
  6.2 0.1 pad_maximum_fusion
  6.3 2.4 %collective-permute-done.3.x3 = bf16[32,1152]{1,0:T(8,128)(2,1)S(1)} collective-permute-done((bf16[32,1152]{1,0:T(8,128)(2,1)S(1)}, bf16[32,1152]{1,0:T(8,128)(2,1)S(1)}, u32[]{:S(2)}, u32[]{:S(2)}) %collective-permute-start.3) | collective-permute-done | bytes 73760 | tf_op jit(solution)/shard_map/ppermute | solution.py:199
  8.6 2.8 %collective-permute-done.2.x2 = bf16[32,1152]{1,0:T(8,128)(2,1)S(1)} collective-permute-done((bf16[32,1152]{1,0:T(8,128)(2,1)S(1)}, bf16[32,1152]{1,0:T(8,128)(2,1)S(1)}, u32[]{:S(2)}, u32[]{:S(2)}) %collective-permute-start.2) | collective-permute-done | bytes 73760 | tf_op jit(solution)/shard_map/ppermute | solution.py:199
  11.4 0.0 collective-permute-done.1.x1
  11.4 0.1 broadcast_in_dim.2.lengths_ref
  11.5 0.0 copy-done
  11.5 0.8 %project.1 = bf16[16,8,2432]{2,1,0:T(8,128)(2,1)S(1)} custom-call(bf16[32,1152]{1,0:T(8,128)(2,1)S(1)} %rotate_in.1.x0, bf16[32,1152]{1,0:T(8,128)(2,1)S(1)} %collective-permute-done.1.x1, bf16[32,1152]{1,0:T(8,128)(2,1)S(1)} %collective-permute-done.2.x2, bf16[32,1152]{1,0:T(8,128)(2,1)S(1)} %collective-permute-done.3.x3, bf16[1024,2304]{1,0:T(8,128)(2,1)S(1)} %copy-done), custom_call_target="tpu_custom_call" | custom-call | flops 1100000000 | bytes 3000000 | tf_op jit(solution)/shard_map/project/pallas_call | solution.py:231
  12.3 19.2 %all_to_all.10.arrived_ref = bf16[16,8,2432]{2,1,0:T(8,128)(2,1)S(1)} all-to-all(bf16[16,8,2432]{2,1,0:T(8,128)(2,1)S(1)} %project.1), channel_id=1, replica_groups=mesh['y'=4,'z'=4,'x'=4,'core'=2] {'y','z'}, dimensions={0} | all-to-all | bytes 1245184 | tf_op jit(solution)/shard_map/all_to_all | solution.py:240
  31.5 0.0 copy-done.3
  31.5 0.0 copy-done.4
  31.5 0.0 copy-start.1
  31.5 0.0 copy-start.2
  31.5 4.5 %attend.1 = bf16[16,8,2048]{2,1,0:T(8,128)(2,1)S(1)} custom-call(s32[8,128]{1,0:T(8,128)S(1)} %broadcast_in_dim.2.lengths_ref, bf16[16,8,2432]{2,1,0:T(8,128)(2,1)S(1)} %all_to_all.10.arrived_ref, f32[8,128]{1,0:T(8,128)S(1)} %get-tuple-element.28.cos_ref, f32[8,128]{1,0:T(8,128)S(1)} %get-tuple-element.29.sin_ref, f32[1,2048]{1,0:T(1,128)S(1)} %bitcast.4, ...), custom_call_target="tpu_custom_call" | custom-call | flops 11000000512 | bytes 30000000 | tf_op jit(solution)/shard_map/attend/pallas_call | solution.py:242
  36.1 13.4 %all_to_all.11 = bf16[16,8,2048]{2,1,0:T(8,128)(2,1)S(1)} all-to-all(bf16[16,8,2048]{2,1,0:T(8,128)(2,1)S(1)} %attend.1), channel_id=1, replica_groups=mesh['y'=4,'z'=4,'x'=4,'core'=2] {'y','z'}, dimensions={0} | all-to-all | bytes 1048576 | tf_op jit(solution)/shard_map/all_to_all | solution.py:264
  49.5 0.0 copy-done.1
  49.5 0.8 %mix.1 = (f32[4,16,1024]{2,1,0:T(8,128)S(1)}, bf16[4,16,1024]{2,1,0:T(8,128)(2,1)S(1)}) custom-call(bf16[4,2,16,2048]{3,2,1,0:T(8,128)(2,1)S(1)} %bitcast.3, bf16[2048,1024]{1,0:T(8,128)(2,1)S(1)} %copy-done.1), custom_call_target="tpu_custom_call" | custom-call | tf_op jit(solution)/shard_map/mix/pallas_call | solution.py:265
  50.3 0.1 collective-permute-start.4
  50.4 1.3 %collective-permute-done.4.got_ref = bf16[4,16,1024]{2,1,0:T(8,128)(2,1)S(1)} collective-permute-done((bf16[4,16,1024]{2,1,0:T(8,128)(2,1)S(1)}, bf16[4,16,1024]{2,1,0:T(8,128)(2,1)S(1)}, u32[]{:S(2)}, u32[]{:S(2)}) %collective-permute-start.4) | collective-permute-done | bytes 131104 | tf_op jit(solution)/shard_map/ppermute | solution.py:203
  51.7 0.9 %collective-permute-start.5 = (bf16[16,1024]{1,0:T(8,128)(2,1)S(1)}, bf16[16,1024]{1,0:T(8,128)(2,1)S(1)}, u32[]{:S(2)}, u32[]{:S(2)}) collective-permute-start(bf16[16,1024]{1,0:T(8,128)(2,1)S(1)} %get-tuple-element.34), channel_id=1, source_target_pairs={{0,2},{2,0},{4,6},{6,4},{1,3},{3,1},{5,7},{7,5},{8,10},{10,8},{12,... | collective-permute-start | bytes 98312 | tf_op jit(solution)/shard_map/ppermute | solution.py:199
  52.7 2.7 %collective-permute-start.6 = (bf16[16,1024]{1,0:T(8,128)(2,1)S(1)}, bf16[16,1024]{1,0:T(8,128)(2,1)S(1)}, u32[]{:S(2)}, u32[]{:S(2)}) collective-permute-start(bf16[16,1024]{1,0:T(8,128)(2,1)S(1)} %get-tuple-element.35), channel_id=1, source_target_pairs={{0,4},{2,6},{4,0},{6,2},{1,5},{3,7},{5,1},{7,3},{8,12},{10,14},{12... | collective-permute-start | bytes 98312 | tf_op jit(solution)/shard_map/ppermute | solution.py:199
  55.4 1.1 %collective-permute-start.7 = (bf16[16,1024]{1,0:T(8,128)(2,1)S(1)}, bf16[16,1024]{1,0:T(8,128)(2,1)S(1)}, u32[]{:S(2)}, u32[]{:S(2)}) collective-permute-start(bf16[16,1024]{1,0:T(8,128)(2,1)S(1)} %get-tuple-element.36), channel_id=1, source_target_pairs={{0,6},{2,4},{4,2},{6,0},{1,7},{3,5},{5,3},{7,1},{8,14},{10,12},{12... | collective-permute-start | bytes 98312 | tf_op jit(solution)/shard_map/ppermute | solution.py:199
  56.5 0.0 collective-permute-done.5.r1
  56.5 1.6 %collective-permute-done.6.r2 = bf16[16,1024]{1,0:T(8,128)(2,1)S(1)} collective-permute-done((bf16[16,1024]{1,0:T(8,128)(2,1)S(1)}, bf16[16,1024]{1,0:T(8,128)(2,1)S(1)}, u32[]{:S(2)}, u32[]{:S(2)}) %collective-permute-start.6) | collective-permute-done | bytes 32800 | tf_op jit(solution)/shard_map/ppermute | solution.py:199
  58.1 2.4 %collective-permute-done.7.r3 = bf16[16,1024]{1,0:T(8,128)(2,1)S(1)} collective-permute-done((bf16[16,1024]{1,0:T(8,128)(2,1)S(1)}, bf16[16,1024]{1,0:T(8,128)(2,1)S(1)}, u32[]{:S(2)}, u32[]{:S(2)}) %collective-permute-start.7) | collective-permute-done | bytes 32800 | tf_op jit(solution)/shard_map/ppermute | solution.py:199
  60.5 0.0 copy-done.2
  60.5 0.6 %last.1 = bf16[16,1024]{1,0:T(8,128)(2,1)} custom-call(bf16[16,1024]{1,0:T(8,128)(2,1)S(1)} %copy-done.2, f32[16,1024]{1,0:T(8,128)S(1)} %get-tuple-element.33.own_ref, bf16[16,1024]{1,0:T(8,128)(2,1)S(1)} %collective-permute-done.5.r1, bf16[16,1024]{1,0:T(8,128)(2,1)S(1)} %collective-permute-done.6.r2, bf16[16,1024]{1,0:T(8,128)(2,1)S(1)} %collective-permute-done.7.r3), custom_call_target="tpu_custom_call" | custom-call | tf_op jit(solution)/shard_map/last/pallas_call | solution.py:286
  (4 shorter events, 0.0 us)
Async XLA Ops:
  0.0 1.5 %collective-permute-start = (bf16[16,1024]{1,0:T(8,128)(2,1)}, bf16[16,1024]{1,0:T(8,128)(2,1)S(1)}, u32[]{:S(2)}, u32[]{:S(2)}) collective-permute-start(bf16[16,1024]{1,0:T(8,128)(2,1)} %hidden_ref.1), channel_id=1, source_target_pairs={{0,1},{1,0},{2,3},{3,2},{4,5},{5,4},{6,7},{7,6},{8,9},{9,8},{10,11... | collective-permute-start | bytes 98312 | tf_op jit(solution)/shard_map/ppermute | solution.py:203
  1.5 4.6 %copy-start.6 = (s32[8]{0:T(128)S(1)}, s32[8]{0:T(128)}, u32[]{:S(2)}) copy-start(s32[8]{0:T(128)} %param.17) | copy-start | bytes 100
  1.5 4.6 %copy-start.5 = (s32[2048]{0:T(1024)S(1)}, s32[2048]{0:T(1024)}, u32[]{:S(2)}) copy-start(s32[2048]{0:T(1024)} %param.14) | copy-start | bytes 24580
  1.5 10.0 %copy-start = (bf16[1024,2304]{1,0:T(8,128)(2,1)S(1)}, bf16[1024,2304]{1,0:T(8,128)(2,1)}, u32[]{:S(2)}) copy-start(bf16[1024,2304]{1,0:T(8,128)(2,1)} %weight.2) | copy-start | bytes 14155780
  1.5 30.0 %copy-start.3 = (bf16[8,1,4096,128]{3,2,1,0:T(8,128)(2,1)S(1)}, bf16[8,1,4096,128]{3,2,1,0:T(8,128)(2,1)}, u32[]{:S(2)}) copy-start(bf16[8,1,4096,128]{3,2,1,0:T(8,128)(2,1)} %keys.1) | copy-start | bytes 25165828
  1.5 30.0 %copy-start.4 = (bf16[8,1,4096,128]{3,2,1,0:T(8,128)(2,1)S(1)}, bf16[8,1,4096,128]{3,2,1,0:T(8,128)(2,1)}, u32[]{:S(2)}) copy-start(bf16[8,1,4096,128]{3,2,1,0:T(8,128)(2,1)} %values.1) | copy-start | bytes 25165828
  1.9 6.7 %collective-permute-start.3 = (bf16[32,1152]{1,0:T(8,128)(2,1)S(1)}, bf16[32,1152]{1,0:T(8,128)(2,1)S(1)}, u32[]{:S(2)}, u32[]{:S(2)}) collective-permute-start(bf16[32,1152]{1,0:T(8,128)(2,1)S(1)} %rotate_in.1.x0), channel_id=1, source_target_pairs={{0,6},{2,4},{4,2},{6,0},{1,7},{3,5},{5,3},{7,1},{8,14},{10,12},{12... | collective-permute-start | bytes 221192 | tf_op jit(solution)/shard_map/ppermute | solution.py:199
  4.8 6.6 %collective-permute-start.2 = (bf16[32,1152]{1,0:T(8,128)(2,1)S(1)}, bf16[32,1152]{1,0:T(8,128)(2,1)S(1)}, u32[]{:S(2)}, u32[]{:S(2)}) collective-permute-start(bf16[32,1152]{1,0:T(8,128)(2,1)S(1)} %rotate_in.1.x0), channel_id=1, source_target_pairs={{0,4},{2,6},{4,0},{6,2},{1,5},{3,7},{5,1},{7,3},{8,12},{10,14},{12... | collective-permute-start | bytes 221192 | tf_op jit(solution)/shard_map/ppermute | solution.py:199
  5.6 5.8 %collective-permute-start.1 = (bf16[32,1152]{1,0:T(8,128)(2,1)S(1)}, bf16[32,1152]{1,0:T(8,128)(2,1)S(1)}, u32[]{:S(2)}, u32[]{:S(2)}) collective-permute-start(bf16[32,1152]{1,0:T(8,128)(2,1)S(1)} %rotate_in.1.x0), channel_id=1, source_target_pairs={{0,2},{2,0},{4,6},{6,4},{1,3},{3,1},{5,7},{7,5},{8,10},{10,8},{12,... | collective-permute-start | bytes 221192 | tf_op jit(solution)/shard_map/ppermute | solution.py:199
  31.5 18.0 %copy-start.1 = (bf16[2048,1024]{1,0:T(8,128)(2,1)S(1)}, bf16[2048,1024]{1,0:T(8,128)(2,1)}, u32[]{:S(2)}) copy-start(bf16[2048,1024]{1,0:T(8,128)(2,1)} %weight.3) | copy-start | bytes 12582916
  31.5 29.0 %copy-start.2 = (bf16[16,1024]{1,0:T(8,128)(2,1)S(1)}, bf16[16,1024]{1,0:T(8,128)(2,1)}, u32[]{:S(2)}) copy-start(bf16[16,1024]{1,0:T(8,128)(2,1)} %hidden_ref.1) | copy-start | bytes 98308
  50.3 1.4 %collective-permute-start.4 = (bf16[4,16,1024]{2,1,0:T(8,128)(2,1)S(1)}, bf16[4,16,1024]{2,1,0:T(8,128)(2,1)S(1)}, u32[]{:S(2)}, u32[]{:S(2)}) collective-permute-start(bf16[4,16,1024]{2,1,0:T(8,128)(2,1)S(1)} %get-tuple-element.32), channel_id=1, source_target_pairs={{0,1},{1,0},{2,3},{3,2},{4,5},{5,4},{6,7},{7,6},{8,9},{9,8},{10,11... | collective-permute-start | bytes 393224 | tf_op jit(solution)/shard_map/ppermute | solution.py:203
  51.7 4.8 %collective-permute-start.5 = (bf16[16,1024]{1,0:T(8,128)(2,1)S(1)}, bf16[16,1024]{1,0:T(8,128)(2,1)S(1)}, u32[]{:S(2)}, u32[]{:S(2)}) collective-permute-start(bf16[16,1024]{1,0:T(8,128)(2,1)S(1)} %get-tuple-element.34), channel_id=1, source_target_pairs={{0,2},{2,0},{4,6},{6,4},{1,3},{3,1},{5,7},{7,5},{8,10},{10,8},{12,... | collective-permute-start | bytes 98312 | tf_op jit(solution)/shard_map/ppermute | solution.py:199
  52.7 5.4 %collective-permute-start.6 = (bf16[16,1024]{1,0:T(8,128)(2,1)S(1)}, bf16[16,1024]{1,0:T(8,128)(2,1)S(1)}, u32[]{:S(2)}, u32[]{:S(2)}) collective-permute-start(bf16[16,1024]{1,0:T(8,128)(2,1)S(1)} %get-tuple-element.35), channel_id=1, source_target_pairs={{0,4},{2,6},{4,0},{6,2},{1,5},{3,7},{5,1},{7,3},{8,12},{10,14},{12... | collective-permute-start | bytes 98312 | tf_op jit(solution)/shard_map/ppermute | solution.py:199
  55.4 5.1 %collective-permute-start.7 = (bf16[16,1024]{1,0:T(8,128)(2,1)S(1)}, bf16[16,1024]{1,0:T(8,128)(2,1)S(1)}, u32[]{:S(2)}, u32[]{:S(2)}) collective-permute-start(bf16[16,1024]{1,0:T(8,128)(2,1)S(1)} %get-tuple-element.36), channel_id=1, source_target_pairs={{0,6},{2,4},{4,2},{6,0},{1,7},{3,5},{5,3},{7,1},{8,14},{10,12},{12... | collective-permute-start | bytes 98312 | tf_op jit(solution)/shard_map/ppermute | solution.py:199

commit v5 on v4

--- a/solution.py
+++ b/solution.py
@@ -77,19 +77,13 @@
 
 
 COVER = (30, 1, 10)
-TILE = 512
+TILE = 1024
 
 
 def attend_kernel(
     lengths_ref, arrived_ref, cos_ref, sin_ref, sign_ref, keys, values, out_ref, queries, scores, attended
 ):
     lists, slots = keys.shape[0], keys.shape[2]
-    pairs = lists // 2
-
-    def wide(ref, pair, start):
-        span = slice(start, start + TILE)
-        return jnp.concatenate([ref[2 * pair, 0, span, :], ref[2 * pair + 1, 0, span, :]], axis=1)
-
     total = arrived_ref[0].astype(F32)
     for w in range(1, arrived_ref.shape[0]):
         total = total + arrived_ref[w].astype(F32)
@@ -104,53 +98,39 @@
         queries[:, h, :] = vector.astype(BF16).astype(F32)
 
     scale = math.log2(math.e) / math.sqrt(HD)
-    lane = lax.broadcasted_iota(jnp.int32, (2 * QG, HD), 1)
-
-    def score(pair):
-        first, second = queries[2 * pair], queries[2 * pair + 1]
-        q_both = jnp.concatenate([first[:QG], second[:QG]], axis=0)
-        blank = jnp.zeros((QG, HD), F32)
-        q_wide = jnp.concatenate(
-            [jnp.concatenate([first[:QG], blank], axis=1), jnp.concatenate([blank, second[:QG]], axis=1)], axis=0
-        ).astype(BF16)
-        k_new = jnp.concatenate([jnp.broadcast_to(v[QG : QG + 1], (QG, HD)) for v in (first, second)], axis=0)
-        fresh = jnp.sum(q_both * k_new, axis=1, keepdims=True) * scale
-        length = jnp.concatenate(
-            [jnp.broadcast_to(lengths_ref[2 * pair + j : 2 * pair + j + 1, :], (QG, HD)) for j in range(2)], axis=0
-        )
-        peak = jnp.full((2 * QG, HD), -1e30, F32)
-        for start in range(0, slots, TILE):
+    lane = lax.broadcasted_iota(jnp.int32, (QG, HD), 1)
+    spans = [slice(start, start + TILE) for start in range(0, slots, TILE)]
+    query, fresh, peak = [], [], []
+    for i in range(lists):
+        heads = queries[i]
+        query.append(heads[:QG].astype(BF16))
+        fresh.append(jnp.sum(heads[:QG] * heads[QG : QG + 1], axis=1, keepdims=True) * scale)
+        peak.append(jnp.full((QG, HD), -1e30, F32))
+    for span in spans:
+        for i in range(lists):
             block = lax.dot_general(
-                q_wide, wide(keys, pair, start), (((1,), (1,)), ((), ())), preferred_element_type=F32
+                query[i], keys[i, 0, span, :], (((1,), (1,)), ((), ())), preferred_element_type=F32
             )
+            length = jnp.broadcast_to(lengths_ref[i : i + 1, :], (QG, HD))
             for t in range(TILE // HD):
-                at = start + t * HD
+                at = span.start + t * HD
                 piece = jnp.where(lane < length - at, block[:, t * HD : (t + 1) * HD] * scale, -1e30)
-                scores[pair, :, at : at + HD] = piece
-                peak = jnp.maximum(peak, piece)
-        return fresh, jnp.maximum(jnp.max(peak, axis=1, keepdims=True), fresh)
-
-    def mix(pair, fresh, peak):
-        mass = jnp.zeros((2 * QG, HD), F32)
-        mixed = jnp.zeros((2 * QG, 2 * HD), F32)
-        for start in range(0, slots, TILE):
-            weight = jnp.exp2(scores[pair, :, start : start + TILE] - peak)
+                scores[i, :, at : at + HD] = piece
+                peak[i] = jnp.maximum(peak[i], piece)
+    peak = [jnp.maximum(jnp.max(peak[i], axis=1, keepdims=True), fresh[i]) for i in range(lists)]
+    mass = [jnp.zeros((QG, HD), F32)] * lists
+    mixed = [jnp.zeros((QG, HD), F32)] * lists
+    for span in spans:
+        for i in range(lists):
+            weight = jnp.exp2(scores[i, :, span] - peak[i])
             for t in range(TILE // HD):
-                mass = mass + weight[:, t * HD : (t + 1) * HD]
-            mixed = mixed + jnp.dot(weight.astype(BF16), wide(values, pair, start), preferred_element_type=F32)
-        weight_new = jnp.exp2(fresh - peak)
-        denominator = jnp.sum(mass, axis=1, keepdims=True) + weight_new
-        v_new = jnp.concatenate(
-            [jnp.broadcast_to(queries[2 * pair + j, QG + 1 : QG + 2, :], (QG, HD)) for j in range(2)], axis=0
-        )
-        own = jnp.concatenate([mixed[:QG, :HD], mixed[QG:, HD:]], axis=0)
-        own = (own + weight_new.astype(BF16).astype(F32) * v_new) / denominator
-        attended[2 * QG * pair : 2 * QG * (pair + 1), :] = own
-
-    ahead = score(0)
-    for pair in range(pairs):
-        this, ahead = ahead, score(pair + 1) if pair + 1 < pairs else None
-        mix(pair, *this)
+                mass[i] = mass[i] + weight[:, t * HD : (t + 1) * HD]
+            mixed[i] = mixed[i] + jnp.dot(weight.astype(BF16), values[i, 0, span, :], preferred_element_type=F32)
+    for i in range(lists):
+        weight_new = jnp.exp2(fresh[i] - peak[i])
+        denominator = jnp.sum(mass[i], axis=1, keepdims=True) + weight_new
+        added = weight_new.astype(BF16).astype(F32) * queries[i, QG + 1 : QG + 2, :]
+        attended[QG * i : QG * (i + 1), :] = (mixed[i] + added) / denominator
 
     matrix = hadamard_signs()
     steered = []
@@ -246,7 +226,7 @@
         out_specs=VMEM,
         scratch_shapes=[
             pltpu.VMEM((own_lists, 24, HD), F32),
-            pltpu.VMEM((own_lists // 2, 2 * QG, slots), F32),
+            pltpu.VMEM((own_lists, QG, slots), F32),
             pltpu.VMEM((own_lists * QG, HD), F32),
         ],
         compiler_params=params(6),

time: 61.4 us -> 60.9 us (level)
  no operation moved by 1% of the time
where the time goes in v5:
time: 60.9 us; the launch traced here: 60.7 us
  blocking collectives  32.6 us (54%)
  waiting for transfers between devices  10.5 us (17%)
  starting transfers between devices  8.99 us (15%)
  Pallas kernels  6.65 us (11%)
  other arithmetic  1.68 us (3%)
    all_to_all x1, blocking collectives, body(): lax.all_to_all(partial, WIDE, split_axis=0, concat_axis=0, tiled=True)  19.2 us
    all_to_all x1, blocking collectives, body(): lax.all_to_all(sent, WIDE, split_axis=0, concat_axis=0, tiled=True)  13.4 us
    ppermute x6, waiting for transfers between devices, along_x(): lax.ppermute(v, 'x', [(i, i ^ s) for i in range(4)])  9.18 us
    ppermute x6, starting transfers between devices, along_x(): lax.ppermute(v, 'x', [(i, i ^ s) for i in range(4)])  8.9 us
    pallas_call x1, Pallas kernels, body(): pl.pallas_call(attend_kernel, out_shape=jax.ShapeDtypeStruct((peers, own_...  4.03 us
    ppermute x2, waiting for transfers between devices, across_cores(): return lax.ppermute(value, 'core', [(0, 1), (1, 0)])  1.34 us
  transfers between devices with their start and end apart: 8, of which 5 were waited for; matrix products, arithmetic and copies ran while one was open for 3% of the time, Pallas kernels for 0%

profile of v5, /device:TPU:0, one launch (start us, length us, event | category | flops | bytes accessed | tf_op | source)
XLA Modules:
  0.0 60.7 jit_solution(13985415710122849693)
XLA Ops:
  0.0 0.0 collective-permute-start
  0.0 0.7 %convert_multiply_fusion = f32[1024]{0:T(1024)S(1)} fusion(s32[1024]{0:T(1024)} %param.11, bf16[1024]{0:T(1024)(128)(2,1)} %param.10), kind=kLoop, calls=%fused_computation.5 | loop fusion | flops 5120 | bytes 10240 | tf_op jit(solution)/shard_map/mul | solution.py:192
  0.7 0.8 %convert_element_type.15.own_ref = f32[16,1024]{1,0:T(8,128)S(1)} convert(bf16[16,1024]{1,0:T(8,128)(2,1)} %hidden_ref.1) | non-fusion elementwise | flops 16384 | bytes 98304 | tf_op jit(solution)/shard_map/convert_element_type | solution.py:201
  1.5 0.0 collective-permute-done.other_ref
  1.5 0.0 copy-start.6
  1.5 0.0 copy-start.5
  1.5 0.0 copy-start
  1.5 0.0 copy-start.3
  1.5 0.0 copy-start.4
  1.6 0.4 rotate_in.1.x0
  1.9 2.9 %collective-permute-start.3 = (bf16[32,1152]{1,0:T(8,128)(2,1)S(1)}, bf16[32,1152]{1,0:T(8,128)(2,1)S(1)}, u32[]{:S(2)}, u32[]{:S(2)}) collective-permute-start(bf16[32,1152]{1,0:T(8,128)(2,1)S(1)} %rotate_in.1.x0), channel_id=1, source_target_pairs={{0,6},{2,4},{4,2},{6,0},{1,7},{3,5},{5,3},{7,1},{8,14},{10,12},{12... | collective-permute-start | bytes 221192 | tf_op jit(solution)/shard_map/ppermute | solution.py:179
  4.8 0.8 %collective-permute-start.2 = (bf16[32,1152]{1,0:T(8,128)(2,1)S(1)}, bf16[32,1152]{1,0:T(8,128)(2,1)S(1)}, u32[]{:S(2)}, u32[]{:S(2)}) collective-permute-start(bf16[32,1152]{1,0:T(8,128)(2,1)S(1)} %rotate_in.1.x0), channel_id=1, source_target_pairs={{0,4},{2,6},{4,0},{6,2},{1,5},{3,7},{5,1},{7,3},{8,12},{10,14},{12... | collective-permute-start | bytes 221192 | tf_op jit(solution)/shard_map/ppermute | solution.py:179
  5.6 0.5 collective-permute-start.1
  6.1 0.0 copy-done.6
  6.1 0.0 copy-done.5
  6.1 0.1 fusion
  6.2 0.1 pad_maximum_fusion
  6.3 2.4 %collective-permute-done.3.x3 = bf16[32,1152]{1,0:T(8,128)(2,1)S(1)} collective-permute-done((bf16[32,1152]{1,0:T(8,128)(2,1)S(1)}, bf16[32,1152]{1,0:T(8,128)(2,1)S(1)}, u32[]{:S(2)}, u32[]{:S(2)}) %collective-permute-start.3) | collective-permute-done | bytes 73760 | tf_op jit(solution)/shard_map/ppermute | solution.py:179
  8.6 2.8 %collective-permute-done.2.x2 = bf16[32,1152]{1,0:T(8,128)(2,1)S(1)} collective-permute-done((bf16[32,1152]{1,0:T(8,128)(2,1)S(1)}, bf16[32,1152]{1,0:T(8,128)(2,1)S(1)}, u32[]{:S(2)}, u32[]{:S(2)}) %collective-permute-start.2) | collective-permute-done | bytes 73760 | tf_op jit(solution)/shard_map/ppermute | solution.py:179
  11.4 0.0 collective-permute-done.1.x1
  11.4 0.1 broadcast_in_dim.2.lengths_ref
  11.5 0.0 copy-done
  11.5 0.8 %project.1 = bf16[16,8,2432]{2,1,0:T(8,128)(2,1)S(1)} custom-call(bf16[32,1152]{1,0:T(8,128)(2,1)S(1)} %rotate_in.1.x0, bf16[32,1152]{1,0:T(8,128)(2,1)S(1)} %collective-permute-done.1.x1, bf16[32,1152]{1,0:T(8,128)(2,1)S(1)} %collective-permute-done.2.x2, bf16[32,1152]{1,0:T(8,128)(2,1)S(1)} %collective-permute-done.3.x3, bf16[1024,2304]{1,0:T(8,128)(2,1)S(1)} %copy-done), custom_call_target="tpu_custom_call" | custom-call | flops 1100000000 | bytes 3000000 | tf_op jit(solution)/shard_map/project/pallas_call | solution.py:211
  12.3 19.2 %all_to_all.10.arrived_ref = bf16[16,8,2432]{2,1,0:T(8,128)(2,1)S(1)} all-to-all(bf16[16,8,2432]{2,1,0:T(8,128)(2,1)S(1)} %project.1), channel_id=1, replica_groups=mesh['y'=4,'z'=4,'x'=4,'core'=2] {'y','z'}, dimensions={0} | all-to-all | bytes 1245184 | tf_op jit(solution)/shard_map/all_to_all | solution.py:220
  31.5 0.0 copy-done.3
  31.5 0.0 copy-done.4
  31.5 0.0 copy-start.1
  31.5 0.0 copy-start.2
  31.5 4.0 %attend.1 = bf16[16,8,2048]{2,1,0:T(8,128)(2,1)S(1)} custom-call(s32[8,128]{1,0:T(8,128)S(1)} %broadcast_in_dim.2.lengths_ref, bf16[16,8,2432]{2,1,0:T(8,128)(2,1)S(1)} %all_to_all.10.arrived_ref, f32[8,128]{1,0:T(8,128)S(1)} %get-tuple-element.28.cos_ref, f32[8,128]{1,0:T(8,128)S(1)} %get-tuple-element.29.sin_ref, f32[1,2048]{1,0:T(1,128)S(1)} %bitcast.4, ...), custom_call_target="tpu_custom_call" | custom-call | flops 11000000512 | bytes 30000000 | tf_op jit(solution)/shard_map/attend/pallas_call | solution.py:222
  35.6 13.4 %all_to_all.11 = bf16[16,8,2048]{2,1,0:T(8,128)(2,1)S(1)} all-to-all(bf16[16,8,2048]{2,1,0:T(8,128)(2,1)S(1)} %attend.1), channel_id=1, replica_groups=mesh['y'=4,'z'=4,'x'=4,'core'=2] {'y','z'}, dimensions={0} | all-to-all | bytes 1048576 | tf_op jit(solution)/shard_map/all_to_all | solution.py:244
  49.0 0.0 copy-done.1
  49.0 0.7 %mix.1 = (f32[4,16,1024]{2,1,0:T(8,128)S(1)}, bf16[4,16,1024]{2,1,0:T(8,128)(2,1)S(1)}) custom-call(bf16[4,2,16,2048]{3,2,1,0:T(8,128)(2,1)S(1)} %bitcast.3, bf16[2048,1024]{1,0:T(8,128)(2,1)S(1)} %copy-done.1), custom_call_target="tpu_custom_call" | custom-call | tf_op jit(solution)/shard_map/mix/pallas_call | solution.py:245
  49.7 0.1 collective-permute-start.4
  49.8 1.3 %collective-permute-done.4.got_ref = bf16[4,16,1024]{2,1,0:T(8,128)(2,1)S(1)} collective-permute-done((bf16[4,16,1024]{2,1,0:T(8,128)(2,1)S(1)}, bf16[4,16,1024]{2,1,0:T(8,128)(2,1)S(1)}, u32[]{:S(2)}, u32[]{:S(2)}) %collective-permute-start.4) | collective-permute-done | bytes 131104 | tf_op jit(solution)/shard_map/ppermute | solution.py:183
  51.2 1.0 %collective-permute-start.5 = (bf16[16,1024]{1,0:T(8,128)(2,1)S(1)}, bf16[16,1024]{1,0:T(8,128)(2,1)S(1)}, u32[]{:S(2)}, u32[]{:S(2)}) collective-permute-start(bf16[16,1024]{1,0:T(8,128)(2,1)S(1)} %get-tuple-element.34), channel_id=1, source_target_pairs={{0,2},{2,0},{4,6},{6,4},{1,3},{3,1},{5,7},{7,5},{8,10},{10,8},{12,... | collective-permute-start | bytes 98312 | tf_op jit(solution)/shard_map/ppermute | solution.py:179
  52.2 2.7 %collective-permute-start.6 = (bf16[16,1024]{1,0:T(8,128)(2,1)S(1)}, bf16[16,1024]{1,0:T(8,128)(2,1)S(1)}, u32[]{:S(2)}, u32[]{:S(2)}) collective-permute-start(bf16[16,1024]{1,0:T(8,128)(2,1)S(1)} %get-tuple-element.35), channel_id=1, source_target_pairs={{0,4},{2,6},{4,0},{6,2},{1,5},{3,7},{5,1},{7,3},{8,12},{10,14},{12... | collective-permute-start | bytes 98312 | tf_op jit(solution)/shard_map/ppermute | solution.py:179
  54.9 1.1 %collective-permute-start.7 = (bf16[16,1024]{1,0:T(8,128)(2,1)S(1)}, bf16[16,1024]{1,0:T(8,128)(2,1)S(1)}, u32[]{:S(2)}, u32[]{:S(2)}) collective-permute-start(bf16[16,1024]{1,0:T(8,128)(2,1)S(1)} %get-tuple-element.36), channel_id=1, source_target_pairs={{0,6},{2,4},{4,2},{6,0},{1,7},{3,5},{5,3},{7,1},{8,14},{10,12},{12... | collective-permute-start | bytes 98312 | tf_op jit(solution)/shard_map/ppermute | solution.py:179
  56.0 0.0 collective-permute-done.5.r1
  56.0 1.6 %collective-permute-done.6.r2 = bf16[16,1024]{1,0:T(8,128)(2,1)S(1)} collective-permute-done((bf16[16,1024]{1,0:T(8,128)(2,1)S(1)}, bf16[16,1024]{1,0:T(8,128)(2,1)S(1)}, u32[]{:S(2)}, u32[]{:S(2)}) %collective-permute-start.6) | collective-permute-done | bytes 32800 | tf_op jit(solution)/shard_map/ppermute | solution.py:179
  57.6 2.4 %collective-permute-done.7.r3 = bf16[16,1024]{1,0:T(8,128)(2,1)S(1)} collective-permute-done((bf16[16,1024]{1,0:T(8,128)(2,1)S(1)}, bf16[16,1024]{1,0:T(8,128)(2,1)S(1)}, u32[]{:S(2)}, u32[]{:S(2)}) %collective-permute-start.7) | collective-permute-done | bytes 32800 | tf_op jit(solution)/shard_map/ppermute | solution.py:179
  60.0 0.0 copy-done.2
  60.0 0.6 %last.1 = bf16[16,1024]{1,0:T(8,128)(2,1)} custom-call(bf16[16,1024]{1,0:T(8,128)(2,1)S(1)} %copy-done.2, f32[16,1024]{1,0:T(8,128)S(1)} %get-tuple-element.33.own_ref, bf16[16,1024]{1,0:T(8,128)(2,1)S(1)} %collective-permute-done.5.r1, bf16[16,1024]{1,0:T(8,128)(2,1)S(1)} %collective-permute-done.6.r2, bf16[16,1024]{1,0:T(8,128)(2,1)S(1)} %collective-permute-done.7.r3), custom_call_target="tpu_custom_call" | custom-call | tf_op jit(solution)/shard_map/last/pallas_call | solution.py:266
  (4 shorter events, 0.0 us)
Async XLA Ops:
  0.0 1.5 %collective-permute-start = (bf16[16,1024]{1,0:T(8,128)(2,1)}, bf16[16,1024]{1,0:T(8,128)(2,1)S(1)}, u32[]{:S(2)}, u32[]{:S(2)}) collective-permute-start(bf16[16,1024]{1,0:T(8,128)(2,1)} %hidden_ref.1), channel_id=1, source_target_pairs={{0,1},{1,0},{2,3},{3,2},{4,5},{5,4},{6,7},{7,6},{8,9},{9,8},{10,11... | collective-permute-start | bytes 98312 | tf_op jit(solution)/shard_map/ppermute | solution.py:183
  1.5 4.6 %copy-start.6 = (s32[8]{0:T(128)S(1)}, s32[8]{0:T(128)}, u32[]{:S(2)}) copy-start(s32[8]{0:T(128)} %param.17) | copy-start | bytes 100
  1.5 4.6 %copy-start.5 = (s32[2048]{0:T(1024)S(1)}, s32[2048]{0:T(1024)}, u32[]{:S(2)}) copy-start(s32[2048]{0:T(1024)} %param.14) | copy-start | bytes 24580
  1.5 10.0 %copy-start = (bf16[1024,2304]{1,0:T(8,128)(2,1)S(1)}, bf16[1024,2304]{1,0:T(8,128)(2,1)}, u32[]{:S(2)}) copy-start(bf16[1024,2304]{1,0:T(8,128)(2,1)} %weight.2) | copy-start | bytes 14155780
  1.5 30.0 %copy-start.3 = (bf16[8,1,4096,128]{3,2,1,0:T(8,128)(2,1)S(1)}, bf16[8,1,4096,128]{3,2,1,0:T(8,128)(2,1)}, u32[]{:S(2)}) copy-start(bf16[8,1,4096,128]{3,2,1,0:T(8,128)(2,1)} %keys.1) | copy-start | bytes 25165828
  1.5 30.0 %copy-start.4 = (bf16[8,1,4096,128]{3,2,1,0:T(8,128)(2,1)S(1)}, bf16[8,1,4096,128]{3,2,1,0:T(8,128)(2,1)}, u32[]{:S(2)}) copy-start(bf16[8,1,4096,128]{3,2,1,0:T(8,128)(2,1)} %values.1) | copy-start | bytes 25165828
  1.9 6.7 %collective-permute-start.3 = (bf16[32,1152]{1,0:T(8,128)(2,1)S(1)}, bf16[32,1152]{1,0:T(8,128)(2,1)S(1)}, u32[]{:S(2)}, u32[]{:S(2)}) collective-permute-start(bf16[32,1152]{1,0:T(8,128)(2,1)S(1)} %rotate_in.1.x0), channel_id=1, source_target_pairs={{0,6},{2,4},{4,2},{6,0},{1,7},{3,5},{5,3},{7,1},{8,14},{10,12},{12... | collective-permute-start | bytes 221192 | tf_op jit(solution)/shard_map/ppermute | solution.py:179
  4.8 6.6 %collective-permute-start.2 = (bf16[32,1152]{1,0:T(8,128)(2,1)S(1)}, bf16[32,1152]{1,0:T(8,128)(2,1)S(1)}, u32[]{:S(2)}, u32[]{:S(2)}) collective-permute-start(bf16[32,1152]{1,0:T(8,128)(2,1)S(1)} %rotate_in.1.x0), channel_id=1, source_target_pairs={{0,4},{2,6},{4,0},{6,2},{1,5},{3,7},{5,1},{7,3},{8,12},{10,14},{12... | collective-permute-start | bytes 221192 | tf_op jit(solution)/shard_map/ppermute | solution.py:179
  5.6 5.8 %collective-permute-start.1 = (bf16[32,1152]{1,0:T(8,128)(2,1)S(1)}, bf16[32,1152]{1,0:T(8,128)(2,1)S(1)}, u32[]{:S(2)}, u32[]{:S(2)}) collective-permute-start(bf16[32,1152]{1,0:T(8,128)(2,1)S(1)} %rotate_in.1.x0), channel_id=1, source_target_pairs={{0,2},{2,0},{4,6},{6,4},{1,3},{3,1},{5,7},{7,5},{8,10},{10,8},{12,... | collective-permute-start | bytes 221192 | tf_op jit(solution)/shard_map/ppermute | solution.py:179
  31.5 17.5 %copy-start.1 = (bf16[2048,1024]{1,0:T(8,128)(2,1)S(1)}, bf16[2048,1024]{1,0:T(8,128)(2,1)}, u32[]{:S(2)}) copy-start(bf16[2048,1024]{1,0:T(8,128)(2,1)} %weight.3) | copy-start | bytes 12582916
  31.5 28.5 %copy-start.2 = (bf16[16,1024]{1,0:T(8,128)(2,1)S(1)}, bf16[16,1024]{1,0:T(8,128)(2,1)}, u32[]{:S(2)}) copy-start(bf16[16,1024]{1,0:T(8,128)(2,1)} %hidden_ref.1) | copy-start | bytes 98308
  49.7 1.4 %collective-permute-start.4 = (bf16[4,16,1024]{2,1,0:T(8,128)(2,1)S(1)}, bf16[4,16,1024]{2,1,0:T(8,128)(2,1)S(1)}, u32[]{:S(2)}, u32[]{:S(2)}) collective-permute-start(bf16[4,16,1024]{2,1,0:T(8,128)(2,1)S(1)} %get-tuple-element.32), channel_id=1, source_target_pairs={{0,1},{1,0},{2,3},{3,2},{4,5},{5,4},{6,7},{7,6},{8,9},{9,8},{10,11... | collective-permute-start | bytes 393224 | tf_op jit(solution)/shard_map/ppermute | solution.py:183
  51.2 4.8 %collective-permute-start.5 = (bf16[16,1024]{1,0:T(8,128)(2,1)S(1)}, bf16[16,1024]{1,0:T(8,128)(2,1)S(1)}, u32[]{:S(2)}, u32[]{:S(2)}) collective-permute-start(bf16[16,1024]{1,0:T(8,128)(2,1)S(1)} %get-tuple-element.34), channel_id=1, source_target_pairs={{0,2},{2,0},{4,6},{6,4},{1,3},{3,1},{5,7},{7,5},{8,10},{10,8},{12,... | collective-permute-start | bytes 98312 | tf_op jit(solution)/shard_map/ppermute | solution.py:179
  52.2 5.4 %collective-permute-start.6 = (bf16[16,1024]{1,0:T(8,128)(2,1)S(1)}, bf16[16,1024]{1,0:T(8,128)(2,1)S(1)}, u32[]{:S(2)}, u32[]{:S(2)}) collective-permute-start(bf16[16,1024]{1,0:T(8,128)(2,1)S(1)} %get-tuple-element.35), channel_id=1, source_target_pairs={{0,4},{2,6},{4,0},{6,2},{1,5},{3,7},{5,1},{7,3},{8,12},{10,14},{12... | collective-permute-start | bytes 98312 | tf_op jit(solution)/shard_map/ppermute | solution.py:179
  54.9 5.1 %collective-permute-start.7 = (bf16[16,1024]{1,0:T(8,128)(2,1)S(1)}, bf16[16,1024]{1,0:T(8,128)(2,1)S(1)}, u32[]{:S(2)}, u32[]{:S(2)}) collective-permute-start(bf16[16,1024]{1,0:T(8,128)(2,1)S(1)} %get-tuple-element.36), channel_id=1, source_target_pairs={{0,6},{2,4},{4,2},{6,0},{1,7},{3,5},{5,3},{7,1},{8,14},{10,12},{12... | collective-permute-start | bytes 98312 | tf_op jit(solution)/shard_map/ppermute | solution.py:179

commit v6 on v5

--- a/solution.py
+++ b/solution.py
@@ -40,6 +40,7 @@
     matrix = hadamard_signs()
     steer = steer_ref[...]
     lane = lax.broadcasted_iota(jnp.int32, (16, EXTRA), 1)
+    blocks = []
     for at, ref in enumerate((own_ref, other_ref)):
         rows = ref[...].astype(F32)
         squares = jnp.sum(rows * rows, axis=1, keepdims=True)
@@ -49,9 +50,11 @@
         pieces = jnp.where(lane == 0, first, jnp.where(lane == 1, second, jnp.where(lane == 2, third, 0.0)))
         out_ref[16 * at : 16 * at + 16, features:] = pieces.astype(BF16)
         steered = rows * steer
-        for b in range(features // HD):
-            turned = two_piece_dot(steered[:, b * HD : (b + 1) * HD], matrix) * (1.0 / math.sqrt(HD))
-            out_ref[16 * at : 16 * at + 16, b * HD : (b + 1) * HD] = turned.astype(BF16)
+        blocks += [steered[:, b * HD : (b + 1) * HD] for b in range(features // HD)]
+    turned = two_piece_dot(jnp.concatenate(blocks, axis=0), matrix) * (1.0 / math.sqrt(HD))
+    for i in range(len(blocks)):
+        at, b = divmod(i, features // HD)
+        out_ref[16 * at : 16 * at + 16, b * HD : (b + 1) * HD] = turned[16 * i : 16 * i + 16].astype(BF16)
 
 
 def project_kernel(x0, x1, x2, x3, weight, out_ref):
@@ -90,11 +93,13 @@
     columns = (QG + 2) * HD
     squares = jnp.sum(total[:, columns:], axis=1, keepdims=True)
     factor = lax.rsqrt(squares * (1.0 / D) + 1e-05)
-    cosine, sine = cos_ref[...], sin_ref[...]
+    cosine, sine = cos_ref[...] * factor, sin_ref[...] * factor
     for h in range(QG + 2):
-        vector = total[:, h * HD : (h + 1) * HD] * factor
+        vector = total[:, h * HD : (h + 1) * HD]
         if h <= QG:
             vector = vector * cosine + pltpu.roll(vector, HD // 2, 1) * sine
+        else:
+            vector = vector * factor
         queries[:, h, :] = vector.astype(BF16).astype(F32)
 
     scale = math.log2(math.e) / math.sqrt(HD)

time: 60.9 us -> 60.7 us (level)
  no operation moved by 1% of the time
where the time goes in v6:
time: 60.7 us; the launch traced here: 60.5 us
  blocking collectives  32.6 us (54%)
  waiting for transfers between devices  10.5 us (17%)
  starting transfers between devices  9.04 us (15%)
  Pallas kernels  6.41 us (11%)
  other arithmetic  1.68 us (3%)
    all_to_all x1, blocking collectives, body(): lax.all_to_all(partial, WIDE, split_axis=0, concat_axis=0, tiled=True)  19.2 us
    all_to_all x1, blocking collectives, body(): lax.all_to_all(sent, WIDE, split_axis=0, concat_axis=0, tiled=True)  13.4 us
    ppermute x6, waiting for transfers between devices, along_x(): lax.ppermute(v, 'x', [(i, i ^ s) for i in range(4)])  9.18 us
    ppermute x6, starting transfers between devices, along_x(): lax.ppermute(v, 'x', [(i, i ^ s) for i in range(4)])  8.95 us
    pallas_call x1, Pallas kernels, body(): pl.pallas_call(attend_kernel, out_shape=jax.ShapeDtypeStruct((peers, own_...  3.99 us
    ppermute x2, waiting for transfers between devices, across_cores(): return lax.ppermute(value, 'core', [(0, 1), (1, 0)])  1.34 us
  transfers between devices with their start and end apart: 8, of which 5 were waited for; matrix products, arithmetic and copies ran while one was open for 3% of the time, Pallas kernels for 0%

profile of v6, /device:TPU:0, one launch (start us, length us, event | category | flops | bytes accessed | tf_op | source)
XLA Modules:
  0.0 60.5 jit_solution(9642154385926699095)
XLA Ops:
  0.0 0.0 collective-permute-start
  0.0 0.7 %convert_multiply_fusion = f32[1024]{0:T(1024)S(1)} fusion(s32[1024]{0:T(1024)} %param.11, bf16[1024]{0:T(1024)(128)(2,1)} %param.10), kind=kLoop, calls=%fused_computation.5 | loop fusion | flops 5120 | bytes 10240 | tf_op jit(solution)/shard_map/mul | solution.py:197
  0.7 0.8 %convert_element_type.15.own_ref = f32[16,1024]{1,0:T(8,128)S(1)} convert(bf16[16,1024]{1,0:T(8,128)(2,1)} %hidden_ref.1) | non-fusion elementwise | flops 16384 | bytes 98304 | tf_op jit(solution)/shard_map/convert_element_type | solution.py:206
  1.5 0.0 collective-permute-done.other_ref
  1.5 0.0 copy-start.6
  1.5 0.0 copy-start.5
  1.5 0.0 copy-start
  1.5 0.0 copy-start.3
  1.5 0.0 copy-start.4
  1.6 0.2 rotate_in.1.x0
  1.8 2.9 %collective-permute-start.3 = (bf16[32,1152]{1,0:T(8,128)(2,1)S(1)}, bf16[32,1152]{1,0:T(8,128)(2,1)S(1)}, u32[]{:S(2)}, u32[]{:S(2)}) collective-permute-start(bf16[32,1152]{1,0:T(8,128)(2,1)S(1)} %rotate_in.1.x0), channel_id=1, source_target_pairs={{0,6},{2,4},{4,2},{6,0},{1,7},{3,5},{5,3},{7,1},{8,14},{10,12},{12... | collective-permute-start | bytes 221192 | tf_op jit(solution)/shard_map/ppermute | solution.py:184
  4.7 0.8 %collective-permute-start.2 = (bf16[32,1152]{1,0:T(8,128)(2,1)S(1)}, bf16[32,1152]{1,0:T(8,128)(2,1)S(1)}, u32[]{:S(2)}, u32[]{:S(2)}) collective-permute-start(bf16[32,1152]{1,0:T(8,128)(2,1)S(1)} %rotate_in.1.x0), channel_id=1, source_target_pairs={{0,4},{2,6},{4,0},{6,2},{1,5},{3,7},{5,1},{7,3},{8,12},{10,14},{12... | collective-permute-start | bytes 221192 | tf_op jit(solution)/shard_map/ppermute | solution.py:184
  5.5 0.5 collective-permute-start.1
  5.9 0.0 copy-done.6
  5.9 0.0 copy-done.5
  5.9 0.1 fusion
  6.1 0.1 pad_maximum_fusion
  6.1 2.4 %collective-permute-done.3.x3 = bf16[32,1152]{1,0:T(8,128)(2,1)S(1)} collective-permute-done((bf16[32,1152]{1,0:T(8,128)(2,1)S(1)}, bf16[32,1152]{1,0:T(8,128)(2,1)S(1)}, u32[]{:S(2)}, u32[]{:S(2)}) %collective-permute-start.3) | collective-permute-done | bytes 73760 | tf_op jit(solution)/shard_map/ppermute | solution.py:184
  8.5 2.8 %collective-permute-done.2.x2 = bf16[32,1152]{1,0:T(8,128)(2,1)S(1)} collective-permute-done((bf16[32,1152]{1,0:T(8,128)(2,1)S(1)}, bf16[32,1152]{1,0:T(8,128)(2,1)S(1)}, u32[]{:S(2)}, u32[]{:S(2)}) %collective-permute-start.2) | collective-permute-done | bytes 73760 | tf_op jit(solution)/shard_map/ppermute | solution.py:184
  11.3 0.0 collective-permute-done.1.x1
  11.3 0.1 broadcast_in_dim.2.lengths_ref
  11.4 0.0 copy-done
  11.4 0.8 %project.1 = bf16[16,8,2432]{2,1,0:T(8,128)(2,1)S(1)} custom-call(bf16[32,1152]{1,0:T(8,128)(2,1)S(1)} %rotate_in.1.x0, bf16[32,1152]{1,0:T(8,128)(2,1)S(1)} %collective-permute-done.1.x1, bf16[32,1152]{1,0:T(8,128)(2,1)S(1)} %collective-permute-done.2.x2, bf16[32,1152]{1,0:T(8,128)(2,1)S(1)} %collective-permute-done.3.x3, bf16[1024,2304]{1,0:T(8,128)(2,1)S(1)} %copy-done), custom_call_target="tpu_custom_call" | custom-call | flops 1100000000 | bytes 3000000 | tf_op jit(solution)/shard_map/project/pallas_call | solution.py:216
  12.2 19.2 %all_to_all.10.arrived_ref = bf16[16,8,2432]{2,1,0:T(8,128)(2,1)S(1)} all-to-all(bf16[16,8,2432]{2,1,0:T(8,128)(2,1)S(1)} %project.1), channel_id=1, replica_groups=mesh['y'=4,'z'=4,'x'=4,'core'=2] {'y','z'}, dimensions={0} | all-to-all | bytes 1245184 | tf_op jit(solution)/shard_map/all_to_all | solution.py:225
  31.4 0.0 copy-done.3
  31.4 0.0 copy-done.4
  31.4 0.0 copy-start.1
  31.4 0.0 copy-start.2
  31.4 4.0 %attend.1 = bf16[16,8,2048]{2,1,0:T(8,128)(2,1)S(1)} custom-call(s32[8,128]{1,0:T(8,128)S(1)} %broadcast_in_dim.2.lengths_ref, bf16[16,8,2432]{2,1,0:T(8,128)(2,1)S(1)} %all_to_all.10.arrived_ref, f32[8,128]{1,0:T(8,128)S(1)} %get-tuple-element.28.cos_ref, f32[8,128]{1,0:T(8,128)S(1)} %get-tuple-element.29.sin_ref, f32[1,2048]{1,0:T(1,128)S(1)} %bitcast.4, ...), custom_call_target="tpu_custom_call" | custom-call | flops 11000000512 | bytes 30000000 | tf_op jit(solution)/shard_map/attend/pallas_call | solution.py:227
  35.4 13.4 %all_to_all.11 = bf16[16,8,2048]{2,1,0:T(8,128)(2,1)S(1)} all-to-all(bf16[16,8,2048]{2,1,0:T(8,128)(2,1)S(1)} %attend.1), channel_id=1, replica_groups=mesh['y'=4,'z'=4,'x'=4,'core'=2] {'y','z'}, dimensions={0} | all-to-all | bytes 1048576 | tf_op jit(solution)/shard_map/all_to_all | solution.py:249
  48.8 0.0 copy-done.1
  48.8 0.8 %mix.1 = (f32[4,16,1024]{2,1,0:T(8,128)S(1)}, bf16[4,16,1024]{2,1,0:T(8,128)(2,1)S(1)}) custom-call(bf16[4,2,16,2048]{3,2,1,0:T(8,128)(2,1)S(1)} %bitcast.3, bf16[2048,1024]{1,0:T(8,128)(2,1)S(1)} %copy-done.1), custom_call_target="tpu_custom_call" | custom-call | tf_op jit(solution)/shard_map/mix/pallas_call | solution.py:250
  49.6 0.1 collective-permute-start.4
  49.7 1.3 %collective-permute-done.4.got_ref = bf16[4,16,1024]{2,1,0:T(8,128)(2,1)S(1)} collective-permute-done((bf16[4,16,1024]{2,1,0:T(8,128)(2,1)S(1)}, bf16[4,16,1024]{2,1,0:T(8,128)(2,1)S(1)}, u32[]{:S(2)}, u32[]{:S(2)}) %collective-permute-start.4) | collective-permute-done | bytes 131104 | tf_op jit(solution)/shard_map/ppermute | solution.py:188
  51.0 1.0 %collective-permute-start.5 = (bf16[16,1024]{1,0:T(8,128)(2,1)S(1)}, bf16[16,1024]{1,0:T(8,128)(2,1)S(1)}, u32[]{:S(2)}, u32[]{:S(2)}) collective-permute-start(bf16[16,1024]{1,0:T(8,128)(2,1)S(1)} %get-tuple-element.34), channel_id=1, source_target_pairs={{0,2},{2,0},{4,6},{6,4},{1,3},{3,1},{5,7},{7,5},{8,10},{10,8},{12,... | collective-permute-start | bytes 98312 | tf_op jit(solution)/shard_map/ppermute | solution.py:184
  52.0 2.7 %collective-permute-start.6 = (bf16[16,1024]{1,0:T(8,128)(2,1)S(1)}, bf16[16,1024]{1,0:T(8,128)(2,1)S(1)}, u32[]{:S(2)}, u32[]{:S(2)}) collective-permute-start(bf16[16,1024]{1,0:T(8,128)(2,1)S(1)} %get-tuple-element.35), channel_id=1, source_target_pairs={{0,4},{2,6},{4,0},{6,2},{1,5},{3,7},{5,1},{7,3},{8,12},{10,14},{12... | collective-permute-start | bytes 98312 | tf_op jit(solution)/shard_map/ppermute | solution.py:184
  54.7 1.1 %collective-permute-start.7 = (bf16[16,1024]{1,0:T(8,128)(2,1)S(1)}, bf16[16,1024]{1,0:T(8,128)(2,1)S(1)}, u32[]{:S(2)}, u32[]{:S(2)}) collective-permute-start(bf16[16,1024]{1,0:T(8,128)(2,1)S(1)} %get-tuple-element.36), channel_id=1, source_target_pairs={{0,6},{2,4},{4,2},{6,0},{1,7},{3,5},{5,3},{7,1},{8,14},{10,12},{12... | collective-permute-start | bytes 98312 | tf_op jit(solution)/shard_map/ppermute | solution.py:184
  55.8 0.0 collective-permute-done.5.r1
  55.8 1.6 %collective-permute-done.6.r2 = bf16[16,1024]{1,0:T(8,128)(2,1)S(1)} collective-permute-done((bf16[16,1024]{1,0:T(8,128)(2,1)S(1)}, bf16[16,1024]{1,0:T(8,128)(2,1)S(1)}, u32[]{:S(2)}, u32[]{:S(2)}) %collective-permute-start.6) | collective-permute-done | bytes 32800 | tf_op jit(solution)/shard_map/ppermute | solution.py:184
  57.4 2.4 %collective-permute-done.7.r3 = bf16[16,1024]{1,0:T(8,128)(2,1)S(1)} collective-permute-done((bf16[16,1024]{1,0:T(8,128)(2,1)S(1)}, bf16[16,1024]{1,0:T(8,128)(2,1)S(1)}, u32[]{:S(2)}, u32[]{:S(2)}) %collective-permute-start.7) | collective-permute-done | bytes 32800 | tf_op jit(solution)/shard_map/ppermute | solution.py:184
  59.8 0.0 copy-done.2
  59.8 0.6 %last.1 = bf16[16,1024]{1,0:T(8,128)(2,1)} custom-call(bf16[16,1024]{1,0:T(8,128)(2,1)S(1)} %copy-done.2, f32[16,1024]{1,0:T(8,128)S(1)} %get-tuple-element.33.own_ref, bf16[16,1024]{1,0:T(8,128)(2,1)S(1)} %collective-permute-done.5.r1, bf16[16,1024]{1,0:T(8,128)(2,1)S(1)} %collective-permute-done.6.r2, bf16[16,1024]{1,0:T(8,128)(2,1)S(1)} %collective-permute-done.7.r3), custom_call_target="tpu_custom_call" | custom-call | tf_op jit(solution)/shard_map/last/pallas_call | solution.py:271
  (4 shorter events, 0.0 us)
Async XLA Ops:
  0.0 1.5 %collective-permute-start = (bf16[16,1024]{1,0:T(8,128)(2,1)}, bf16[16,1024]{1,0:T(8,128)(2,1)S(1)}, u32[]{:S(2)}, u32[]{:S(2)}) collective-permute-start(bf16[16,1024]{1,0:T(8,128)(2,1)} %hidden_ref.1), channel_id=1, source_target_pairs={{0,1},{1,0},{2,3},{3,2},{4,5},{5,4},{6,7},{7,6},{8,9},{9,8},{10,11... | collective-permute-start | bytes 98312 | tf_op jit(solution)/shard_map/ppermute | solution.py:188
  1.5 4.4 %copy-start.6 = (s32[8]{0:T(128)S(1)}, s32[8]{0:T(128)}, u32[]{:S(2)}) copy-start(s32[8]{0:T(128)} %param.17) | copy-start | bytes 100
  1.5 4.4 %copy-start.5 = (s32[2048]{0:T(1024)S(1)}, s32[2048]{0:T(1024)}, u32[]{:S(2)}) copy-start(s32[2048]{0:T(1024)} %param.14) | copy-start | bytes 24580
  1.5 9.8 %copy-start = (bf16[1024,2304]{1,0:T(8,128)(2,1)S(1)}, bf16[1024,2304]{1,0:T(8,128)(2,1)}, u32[]{:S(2)}) copy-start(bf16[1024,2304]{1,0:T(8,128)(2,1)} %weight.2) | copy-start | bytes 14155780
  1.5 29.8 %copy-start.3 = (bf16[8,1,4096,128]{3,2,1,0:T(8,128)(2,1)S(1)}, bf16[8,1,4096,128]{3,2,1,0:T(8,128)(2,1)}, u32[]{:S(2)}) copy-start(bf16[8,1,4096,128]{3,2,1,0:T(8,128)(2,1)} %keys.1) | copy-start | bytes 25165828
  1.5 29.8 %copy-start.4 = (bf16[8,1,4096,128]{3,2,1,0:T(8,128)(2,1)S(1)}, bf16[8,1,4096,128]{3,2,1,0:T(8,128)(2,1)}, u32[]{:S(2)}) copy-start(bf16[8,1,4096,128]{3,2,1,0:T(8,128)(2,1)} %values.1) | copy-start | bytes 25165828
  1.8 6.7 %collective-permute-start.3 = (bf16[32,1152]{1,0:T(8,128)(2,1)S(1)}, bf16[32,1152]{1,0:T(8,128)(2,1)S(1)}, u32[]{:S(2)}, u32[]{:S(2)}) collective-permute-start(bf16[32,1152]{1,0:T(8,128)(2,1)S(1)} %rotate_in.1.x0), channel_id=1, source_target_pairs={{0,6},{2,4},{4,2},{6,0},{1,7},{3,5},{5,3},{7,1},{8,14},{10,12},{12... | collective-permute-start | bytes 221192 | tf_op jit(solution)/shard_map/ppermute | solution.py:184
  4.7 6.6 %collective-permute-start.2 = (bf16[32,1152]{1,0:T(8,128)(2,1)S(1)}, bf16[32,1152]{1,0:T(8,128)(2,1)S(1)}, u32[]{:S(2)}, u32[]{:S(2)}) collective-permute-start(bf16[32,1152]{1,0:T(8,128)(2,1)S(1)} %rotate_in.1.x0), channel_id=1, source_target_pairs={{0,4},{2,6},{4,0},{6,2},{1,5},{3,7},{5,1},{7,3},{8,12},{10,14},{12... | collective-permute-start | bytes 221192 | tf_op jit(solution)/shard_map/ppermute | solution.py:184
  5.5 5.8 %collective-permute-start.1 = (bf16[32,1152]{1,0:T(8,128)(2,1)S(1)}, bf16[32,1152]{1,0:T(8,128)(2,1)S(1)}, u32[]{:S(2)}, u32[]{:S(2)}) collective-permute-start(bf16[32,1152]{1,0:T(8,128)(2,1)S(1)} %rotate_in.1.x0), channel_id=1, source_target_pairs={{0,2},{2,0},{4,6},{6,4},{1,3},{3,1},{5,7},{7,5},{8,10},{10,8},{12,... | collective-permute-start | bytes 221192 | tf_op jit(solution)/shard_map/ppermute | solution.py:184
  31.4 17.4 %copy-start.1 = (bf16[2048,1024]{1,0:T(8,128)(2,1)S(1)}, bf16[2048,1024]{1,0:T(8,128)(2,1)}, u32[]{:S(2)}) copy-start(bf16[2048,1024]{1,0:T(8,128)(2,1)} %weight.3) | copy-start | bytes 12582916
  31.4 28.4 %copy-start.2 = (bf16[16,1024]{1,0:T(8,128)(2,1)S(1)}, bf16[16,1024]{1,0:T(8,128)(2,1)}, u32[]{:S(2)}) copy-start(bf16[16,1024]{1,0:T(8,128)(2,1)} %hidden_ref.1) | copy-start | bytes 98308
  49.6 1.4 %collective-permute-start.4 = (bf16[4,16,1024]{2,1,0:T(8,128)(2,1)S(1)}, bf16[4,16,1024]{2,1,0:T(8,128)(2,1)S(1)}, u32[]{:S(2)}, u32[]{:S(2)}) collective-permute-start(bf16[4,16,1024]{2,1,0:T(8,128)(2,1)S(1)} %get-tuple-element.32), channel_id=1, source_target_pairs={{0,1},{1,0},{2,3},{3,2},{4,5},{5,4},{6,7},{7,6},{8,9},{9,8},{10,11... | collective-permute-start | bytes 393224 | tf_op jit(solution)/shard_map/ppermute | solution.py:188
  51.0 4.8 %collective-permute-start.5 = (bf16[16,1024]{1,0:T(8,128)(2,1)S(1)}, bf16[16,1024]{1,0:T(8,128)(2,1)S(1)}, u32[]{:S(2)}, u32[]{:S(2)}) collective-permute-start(bf16[16,1024]{1,0:T(8,128)(2,1)S(1)} %get-tuple-element.34), channel_id=1, source_target_pairs={{0,2},{2,0},{4,6},{6,4},{1,3},{3,1},{5,7},{7,5},{8,10},{10,8},{12,... | collective-permute-start | bytes 98312 | tf_op jit(solution)/shard_map/ppermute | solution.py:184
  52.0 5.4 %collective-permute-start.6 = (bf16[16,1024]{1,0:T(8,128)(2,1)S(1)}, bf16[16,1024]{1,0:T(8,128)(2,1)S(1)}, u32[]{:S(2)}, u32[]{:S(2)}) collective-permute-start(bf16[16,1024]{1,0:T(8,128)(2,1)S(1)} %get-tuple-element.35), channel_id=1, source_target_pairs={{0,4},{2,6},{4,0},{6,2},{1,5},{3,7},{5,1},{7,3},{8,12},{10,14},{12... | collective-permute-start | bytes 98312 | tf_op jit(solution)/shard_map/ppermute | solution.py:184
  54.7 5.1 %collective-permute-start.7 = (bf16[16,1024]{1,0:T(8,128)(2,1)S(1)}, bf16[16,1024]{1,0:T(8,128)(2,1)S(1)}, u32[]{:S(2)}, u32[]{:S(2)}) collective-permute-start(bf16[16,1024]{1,0:T(8,128)(2,1)S(1)} %get-tuple-element.36), channel_id=1, source_target_pairs={{0,6},{2,4},{4,2},{6,0},{1,7},{3,5},{5,3},{7,1},{8,14},{10,12},{12... | collective-permute-start | bytes 98312 | tf_op jit(solution)/shard_map/ppermute | solution.py:184
